TPU v7x, 32 devices: a whole 2x2x4 slice. The times are simulated.
32 devices in a mesh: dp: 2 (over x), pipe: 4 (over y, core), expert: 4 (over z).
Axes of the slice: x: 2, y: 2, z: 4, core: 2. Of those that a mesh axis runs over, the one named last changes fastest.
Arguments:
- tokens: bfloat16 [768, 3072], P(('dp', 'expert')), may hold values from -6 to 6
- routes: int32 [768, 2], P(('dp', 'expert')), may hold values from 0 to 3, all different within a row; in each aligned block of 96 rows (0 to 95, 96 to 191, ...) at most 50 rows name the same one
- route_weights: float32 [768, 2], P(('dp', 'expert')), may hold values from 0.2 to 1
- w_gate: bfloat16 [4, 3072, 8192], P('expert', None, 'pipe'), may hold values from -0.109375 to 0.109375
- w_up: bfloat16 [4, 3072, 8192], P('expert', None, 'pipe'), may hold values from -0.109375 to 0.109375
- w_down: bfloat16 [4, 8192, 3072], P('expert', 'pipe'), may hold values from -0.0625 to 0.0625
Outputs:
- mixed: bfloat16 [768, 3072], P(('dp', 'expert'), 'pipe')
Inputs may be any that keep to these rules, and one draw needn't show every extreme that they name: `routes`: each row names two different experts. Among the 96 rows of one block no expert is named more than 50 times, a bound that some block reaches.
All inputs are finite; a program needn't handle non-finite values.
Results may differ from a plain program's by a relative error of at most 0.019.
Values may be sent and summed in bfloat16 or wider, within the bound.
No kernel may reach another device: no remote copies, remote signals or barrier semaphores. Data moves between devices by JAX's collectives and lax.ppermute only.
A program may use at most 128 MiB of HBM per device.

v0:
```python
import jax
import jax.numpy as jnp
from jax import lax
from jax.sharding import PartitionSpec as P


def slot_table(route_rows, expert_total):
    choices = route_rows.reshape(-1)
    expert_ids = jnp.arange(expert_total, dtype=jnp.int32)
    matches = (choices[None, :] == expert_ids[:, None]).astype(jnp.int32)
    rank_of = jnp.cumsum(matches, axis=1) - 1
    return (choices, jnp.sum(rank_of * matches, axis=0))


def on_device(tokens, routes, route_weights, w_gate, w_up, w_down):
    expert_count = lax.axis_size("expert")
    pipe_count = lax.axis_size("pipe")
    replica_count = lax.axis_size("dp")
    expert_total = w_gate.shape[0] * expert_count
    hidden_width = w_gate.shape[2]
    tok_rows = tokens.shape[0]
    model_width = tokens.shape[1]
    capacity = min(
        tok_rows,
        replica_count * ((2 * tok_rows + expert_total - 1) // expert_total // replica_count + 1),
    )
    slot_share = capacity // replica_count
    col_share = model_width // pipe_count
    group_count = replica_count * expert_total
    choices, slot_of = slot_table(routes, expert_total)
    target = (
        slot_of // slot_share * (expert_total * slot_share)
        + choices * slot_share
        + slot_of % slot_share
    )
    column_ids = jnp.arange(group_count * slot_share, dtype=jnp.int32)
    picker = (column_ids[:, None] == target[None, :]).astype(jnp.bfloat16)
    gate_full = w_gate[0]
    up_full = w_up[0]
    own_columns = lax.dynamic_slice_in_dim(tokens, lax.axis_index("pipe") * col_share, col_share, 1)
    doubled = jnp.repeat(own_columns, 2, axis=0)
    outgoing = jnp.dot(picker, doubled, preferred_element_type=jnp.float32)
    outgoing = outgoing.astype(jnp.bfloat16).reshape(group_count, slot_share, col_share)
    arrived = lax.all_to_all(outgoing, ("dp", "expert"), split_axis=0, concat_axis=0, tiled=True)
    column_piece = lax.all_gather(arrived, "pipe", axis=2, tiled=True)
    gate_part = jnp.einsum(
        "gsd,df->gsf", column_piece, gate_full, preferred_element_type=jnp.float32
    )
    up_part = jnp.einsum("gsd,df->gsf", column_piece, up_full, preferred_element_type=jnp.float32)
    hidden = (jax.nn.silu(gate_part) * up_part).astype(jnp.bfloat16)
    down_blocks = w_down[0].reshape(hidden_width, pipe_count, col_share)
    block_term = jnp.einsum(
        "gsf,fke->kgse", hidden, down_blocks, preferred_element_type=jnp.float32
    )
    block_term = lax.optimization_barrier(block_term.astype(jnp.bfloat16))
    section = lax.psum_scatter(
        block_term.astype(jnp.float32).astype(jnp.bfloat16), "pipe", scatter_dimension=0, tiled=True
    )
    summed = section.reshape(group_count, slot_share, col_share)
    returned = lax.all_to_all(summed, ("dp", "expert"), split_axis=0, concat_axis=0, tiled=True)
    mixing = (target[:, None] == column_ids[None, :]).astype(jnp.float32) * route_weights.reshape(
        -1
    )[:, None]
    mixing = mixing.reshape(tok_rows, 2, group_count * slot_share).sum(axis=1)
    mixed_out = jnp.dot(
        mixing,
        returned.reshape(group_count * slot_share, col_share).astype(jnp.float32),
        precision=lax.Precision.HIGHEST,
    )
    return mixed_out.astype(jnp.bfloat16)


def solution(mesh):
    return jax.shard_map(
        on_device,
        mesh=mesh,
        in_specs=(
            P(("dp", "expert"), None),
            P(("dp", "expert"), None),
            P(("dp", "expert"), None),
            P("expert", None, "pipe"),
            P("expert", None, "pipe"),
            P("expert", "pipe", None),
        ),
        out_specs=P(("dp", "expert"), "pipe"),
        check_vma=False,
    )
```

profile of v0, /device:TPU:0, one launch (start us, length us, event | category | flops | bytes accessed | tf_op | source)
XLA Modules:
  0.0 132.2 jit_solution(12432199007527661033)
XLA Ops:
  6.5 0.8 copy.50
  7.4 0.1 eq.44
  7.6 1.2 reduce-window.6
  8.8 0.1 slice.12
  8.9 0.1 copy.51
  9.0 0.1 copy.52
  9.1 0.1 add_bitcast_fusion
  9.3 0.2 broadcast_in_dim.2
  9.4 0.1 reshape.93
  9.6 0.2 convolution_convert_fusion
  9.8 0.1 reshape.94
  9.9 19.8 %all_to_all.10 = bf16[8,25,768]{2,1,0:T(8,128)(2,1)} all-to-all(bf16[8,25,768]{2,1,0:T(8,128)(2,1)S(1)} %reshape.94), channel_id=1, replica_groups=mesh['dp'=2,'pipe'=4,'expert'=4] {'dp','expert'}, dimensions={0} | all-to-all | bytes 614400 | tf_op jit(solution)/shard_map/all_to_all | solution.py:44
  29.7 0.0 all-gather.2.cloned.1.call-update
  29.7 0.0 reduce-scatter.2.cloned.1.call-start
  29.8 23.5 %reshape_squeeze.3 = bf16[2048,4,768]{2,1,0:T(4,128)(2,1)} reshape(bf16[1,2048,3072]{2,1,0:T(8,128)(2,1)} %param.11) | data formatting | bytes 25165824 | tf_op jit(solution)/shard_map/reshape;squeeze | solution.py:51
  53.3 9.8 %fusion.4 = f32[8,25,2048]{2,1,0:T(8,128)} fusion(bf16[8,25,3072]{2,1,0:T(8,128)(2,1)} %all-gather.2.cloned.1.call-done, bf16[1,3072,2048]{2,1,0:T(8,128)(2,1)} %param.9), kind=kOutput, calls=%fused_computation.4 | convolution fusion | flops 2516582400 | bytes 15450112 | tf_op jit(solution)/shard_map/gsd,df->gsf/dot_general | solution.py:46
  63.1 16.1 %fusion.28 = bf16[4,8,25,768]{3,2,0,1:T(8,128)(2,1)S(1)} fusion(bf16[2048,4,768]{2,1,0:T(4,128)(2,1)} %reshape_squeeze.3, bf16[8,25,3072]{2,1,0:T(8,128)(2,1)} %all-gather.2.cloned.1.call-done, bf16[1,3072,2048]{2,1,0:T(8,128)(2,1)} %param.10, f32[8,25,2048]{2,1,0:T(8,128)} %fusion.4), kind=kOutput, calls=%fused_computation.16 | convolution fusion | flops 5036236800 | bytes 29261824 | tf_op jit(solution)/shard_map/gsf,fke->kgse/dot_general | solution.py:52
  79.2 1.7 %copy.61 = bf16[4,8,25,768]{3,1,2,0:T(8,128)(2,1)} copy(bf16[4,8,25,768]{3,2,0,1:T(8,128)(2,1)S(1)} %fusion.28) | data formatting | bytes 2457600 | tf_op jit(solution)/shard_map/optimization_barrier | solution.py:55
  81.0 0.0 reduce-scatter.2.cloned.1.call-update
  81.0 23.7 %reduce-scatter.2.cloned.1.call-done = bf16[1,8,25,768]{3,1,2,0:T(8,128)(2,1)} async-done(((bf16[4,8,25,768]{3,1,2,0:T(8,128)(2,1)}), bf16[1,8,25,768]{3,1,2,0:T(8,128)(2,1)}) %reduce-scatter.2.cloned.1.call-update) | async-done | bytes 307216 | tf_op jit(solution)/shard_map/reduce_scatter | solution.py:56
  104.6 1.8 %copy.62 = bf16[8,25,768]{2,1,0:T(8,128)(2,1)} copy(bf16[8,25,768]{2,0,1:T(8,128)(2,1)} %bitcast.51) | data formatting | bytes 614400 | tf_op jit(solution)/shard_map/reshape | solution.py:59
  106.4 5.5 %all-to-all-start.1 = ((bf16[8,25,768]{2,1,0:T(8,128)(2,1)}), bf16[8,25,768]{2,1,0:T(8,128)(2,1)S(1)}, u32[]{:S(2)}, u32[]{:S(2)}) async-start(bf16[8,25,768]{2,1,0:T(8,128)(2,1)} %copy.62), calls=%async_computation.2 | async-start | bytes 786432 | tf_op jit(solution)/shard_map/all_to_all | solution.py:60
  111.9 0.1 rem.29
  112.0 0.1 copy.53
  112.1 0.2 div.22
  112.3 0.1 copy.55
  112.3 0.2 ne.57
  112.5 0.1 copy.54
  112.6 0.1 select_reduce_fusion
  112.8 11.6 %all-to-all-done.1 = bf16[8,25,768]{2,1,0:T(8,128)(2,1)S(1)} async-done(((bf16[8,25,768]{2,1,0:T(8,128)(2,1)}), bf16[8,25,768]{2,1,0:T(8,128)(2,1)S(1)}, u32[]{:S(2)}, u32[]{:S(2)}) %all-to-all-start.1) | async-done | bytes 307232 | tf_op jit(solution)/shard_map/all_to_all | solution.py:60
  124.3 0.1 reshape.96
  124.5 0.9 convolution_convert_fusion.1
  (18 shorter events, 0.2 us)
Async XLA Ops:
  6.5 2.7 %copy-start = (bf16[96,3072]{1,0:T(8,128)(2,1)S(1)}, bf16[96,3072]{1,0:T(8,128)(2,1)}, u32[]{:S(2)}) copy-start(bf16[96,3072]{1,0:T(8,128)(2,1)} %param.6) | copy-start | bytes 1769476
  6.5 46.7 %all-gather.2.cloned.1.call-start = ((), (), s32[]{:S(2)}) async-start(), calls=%async_computation.3 | async-start | bytes 1966080 | tf_op jit(solution)/shard_map/all_gather | solution.py:45
  29.7 74.9 %reduce-scatter.2.cloned.1.call-start = ((), (), s32[]{:S(2)}) async-start(), calls=%async_computation.4 | async-start | bytes 1536000 | tf_op jit(solution)/shard_map/reduce_scatter | solution.py:56
  80.9 31.7 %copy-start.1 = (s32[96,2]{0,1:T(2,128)S(1)}, s32[96,2]{0,1:T(2,128)}, u32[]{:S(2)}) copy-start(s32[96,2]{0,1:T(2,128)} %param.7) | copy-start | bytes 2308
  81.0 31.7 %copy-start.2 = (f32[96,2]{0,1:T(2,128)S(1)}, f32[96,2]{0,1:T(2,128)}, u32[]{:S(2)}) copy-start(f32[96,2]{0,1:T(2,128)} %param.8) | copy-start | bytes 2308
  106.4 17.9 %all-to-all-start.1 = ((bf16[8,25,768]{2,1,0:T(8,128)(2,1)}), bf16[8,25,768]{2,1,0:T(8,128)(2,1)S(1)}, u32[]{:S(2)}, u32[]{:S(2)}) async-start(bf16[8,25,768]{2,1,0:T(8,128)(2,1)} %copy.62), calls=%async_computation.2 | async-start | bytes 786432 | tf_op jit(solution)/shard_map/all_to_all | solution.py:60
Sparse Core Ops, SparseCore 0:
  29.8 17.2 all-gather.1
  81.1 23.4 reduce-scatter.1
where the time goes:
time: 133 us; the launch traced here: 132 us
  waiting for transfers between devices  35.3 us (27%)
  local copies, waits for them, and re-layouts  29.5 us (22%)
  matrix products  27.1 us (20%)
  blocking collectives  19.8 us (15%)
  between operations  13.5 us (10%)
  starting transfers between devices  5.56 us (4%)
  other arithmetic  1.53 us (1%)
    reduce_scatter x1, waiting for transfers between devices, on_device(): lax.psum_scatter(block_term.astype(jnp.float32).astype(jnp.bfloat16), 'pi...  23.7 us
    another operation x1, local copies, waits for them, and re-layouts, on_device(): down_blocks = w_down[0].reshape(hidden_width, pipe_count, col_share)  23.5 us
    all_to_all x1, blocking collectives, on_device(): lax.all_to_all(outgoing, ('dp', 'expert'), split_axis=0, concat_axis=0, t...  19.8 us
    dot_general x1, matrix products, on_device(): jnp.einsum('gsf,fke->kgse', hidden, down_blocks, preferred_element_type=j...  16.1 us
    all_to_all x1, waiting for transfers between devices, on_device(): lax.all_to_all(summed, ('dp', 'expert'), split_axis=0, concat_axis=0, til...  11.6 us
    dot_general x1, matrix products, on_device(): jnp.einsum('gsd,df->gsf', column_piece, gate_full, preferred_element_type...  9.83 us
    all_to_all x1, starting transfers between devices, on_device(): lax.all_to_all(summed, ('dp', 'expert'), split_axis=0, concat_axis=0, til...  5.52 us
  transfers between devices with their start and end apart: 3, of which 2 were waited for; matrix products, arithmetic and copies ran while one was open for 18% of the time, Pallas kernels for 0%

commit v1 on v0

v1 whole, which is shorter than its diff:
```python
import functools

import jax
import jax.numpy as jnp
from jax import lax
from jax.experimental import pallas as pl
from jax.experimental.pallas import tpu as pltpu
from jax.sharding import PartitionSpec as P

F32 = jnp.float32
BF16 = jnp.bfloat16
HBM = pl.BlockSpec(memory_space=pltpu.HBM)
VMEM = pl.BlockSpec(memory_space=pltpu.VMEM)
MIB = 1 << 20


def capacity_of(tok_rows, expert_total, replica_count):
    per_expert = (2 * tok_rows + expert_total - 1) // expert_total
    return min(tok_rows, replica_count * (per_expert // replica_count + 1))


def slot_table(route_rows, expert_total):
    choices = route_rows.reshape(-1)
    expert_ids = jnp.arange(expert_total, dtype=jnp.int32)
    matches = (choices[None, :] == expert_ids[:, None]).astype(jnp.int32)
    rank_of = jnp.cumsum(matches, axis=1) - 1
    return (choices, jnp.sum(rank_of * matches, axis=0))


def on_any_mesh(tokens, routes, route_weights, w_gate, w_up, w_down):
    expert_total = w_gate.shape[0] * lax.axis_size("expert")
    pipe_count = lax.axis_size("pipe")
    hidden_width = w_gate.shape[2]
    tok_rows, model_width = tokens.shape
    capacity = capacity_of(tok_rows, expert_total, lax.axis_size("dp"))
    col_share = model_width // pipe_count
    choices, slot_of = slot_table(routes, expert_total)
    target = choices * capacity + slot_of
    column_ids = jnp.arange(expert_total * capacity, dtype=jnp.int32)
    picker = (column_ids[:, None] == target[None, :]).astype(BF16)
    own_columns = lax.dynamic_slice_in_dim(tokens, lax.axis_index("pipe") * col_share, col_share, 1)
    outgoing = jnp.dot(picker, jnp.repeat(own_columns, 2, axis=0), preferred_element_type=F32)
    outgoing = outgoing.astype(BF16).reshape(expert_total, capacity, col_share)
    arrived = lax.all_to_all(outgoing, "expert", split_axis=0, concat_axis=0, tiled=True)
    rows = lax.all_gather(arrived, "pipe", axis=2, tiled=True)
    gate_part = jnp.einsum("gsd,df->gsf", rows, w_gate[0], preferred_element_type=F32)
    up_part = jnp.einsum("gsd,df->gsf", rows, w_up[0], preferred_element_type=F32)
    hidden = (jax.nn.silu(gate_part) * up_part).astype(BF16)
    down_blocks = w_down[0].reshape(hidden_width, pipe_count, col_share)
    block_term = jnp.einsum("gsf,fke->kgse", hidden, down_blocks, preferred_element_type=F32)
    block_term = lax.optimization_barrier(block_term.astype(BF16))
    section = lax.psum_scatter(block_term, "pipe", scatter_dimension=0, tiled=True)
    summed = section.reshape(expert_total, capacity, col_share)
    returned = lax.all_to_all(summed, "expert", split_axis=0, concat_axis=0, tiled=True)
    mixing = (target[:, None] == column_ids[None, :]).astype(F32) * route_weights.reshape(-1)[:, None]
    mixing = mixing.reshape(tok_rows, 2, expert_total * capacity).sum(axis=1)
    mixed = jnp.dot(
        mixing,
        returned.reshape(expert_total * capacity, col_share).astype(F32),
        precision=lax.Precision.HIGHEST,
    )
    return mixed.astype(BF16)


def load_all(pairs, sems):
    copies = [pltpu.make_async_copy(a, b, sems.at[i]) for i, (a, b) in enumerate(pairs)]
    for copy in copies:
        copy.start()
    return copies


def wait_all(copies):
    for copy in copies:
        copy.wait()


def rows_of(w_ref, share, height):
    return w_ref.at[0, pl.ds(pl.multiple_of(share * height, height), height), :]


def cols_of(w_ref, share, width):
    return w_ref.at[0, :, pl.ds(pl.multiple_of(share * width, width), width)]


def ranks(routes_t, experts):
    tok_rows = routes_t.shape[1]
    named = (routes_t[0:1, :] == experts) | (routes_t[1:2, :] == experts)
    named = named.astype(F32)
    earlier = lax.broadcasted_iota(jnp.int32, (tok_rows, tok_rows), 0)
    later = lax.broadcasted_iota(jnp.int32, (tok_rows, tok_rows), 1)
    before = (earlier < later).astype(BF16)
    count = jnp.dot(named.astype(BF16), before, preferred_element_type=F32)
    return named, count


def expert_rows(count, expert_total):
    mine = lax.axis_index("expert")
    return jnp.bitwise_xor(lax.broadcasted_iota(jnp.int32, (count, 1), 0), mine)


def pack_kernel(pipe_count, capacity, expert_total, routes_ref, own_ref, gate_ref, *refs):
    outs, vg_ref, pick_ref, sems = refs[:expert_total], refs[-3], refs[-2], refs[-1]
    share = lax.axis_index("pipe")
    loads = load_all([(rows_of(gate_ref, share, vg_ref.shape[0]), vg_ref)], sems)
    named, count = ranks(routes_ref[...], expert_rows(max(8, expert_total), expert_total))
    padded = pick_ref.shape[0] // expert_total
    slot_ids = lax.broadcasted_iota(jnp.int32, (padded, 1), 0).astype(F32)
    for k in range(expert_total):
        chosen = (count[k : k + 1, :] == slot_ids) & (named[k : k + 1, :] > 0.5)
        pick_ref[k * padded : (k + 1) * padded, :] = chosen.astype(BF16)
    picked = jnp.dot(pick_ref[...], own_ref[...], preferred_element_type=F32).astype(BF16)
    for k in range(expert_total):
        outs[k][...] = picked[k * padded : k * padded + capacity, :]
    wait_all(loads)


def local_kernel(
    pipe_count, capacity, expert_total, routes_ref, weights_ref, tokens_ref, up_ref, gate_ref, *refs
):
    own_ref, select_ref, scale_ref, vu_ref, vg_ref, sems = refs
    tok_rows = tokens_ref.shape[0]
    height = vg_ref.shape[0]
    share = lax.axis_index("pipe")
    loads = load_all(
        [
            (rows_of(up_ref, share, height), vu_ref),
            (rows_of(gate_ref, jnp.bitwise_xor(share, 1), height), vg_ref),
        ],
        sems,
    )
    routes_t = routes_ref[...]
    experts = expert_rows(max(8, expert_total), expert_total)
    named, count = ranks(routes_t, experts)
    slot_ids = lax.broadcasted_iota(jnp.int32, (capacity, 1), 0).astype(F32)
    chosen = ((count[0:1, :] == slot_ids) & (named[0:1, :] > 0.5)).astype(BF16)
    own_ref[...] = jnp.dot(chosen, tokens_ref[...], preferred_element_type=F32).astype(BF16)
    line = lax.broadcasted_iota(jnp.int32, (tok_rows, tok_rows), 0)
    lane = lax.broadcasted_iota(jnp.int32, (tok_rows, tok_rows), 1)
    eye = line == lane
    lane_slots = lax.broadcasted_iota(jnp.int32, (1, capacity), 1).astype(F32)

    def column(row):
        return jnp.sum(jnp.where(eye, row, 0.0), axis=1, keepdims=True)

    for c in range(2):
        route = routes_t[c : c + 1, :]
        slot = jnp.sum(jnp.where(route == experts, count, 0.0), axis=0, keepdims=True)
        slot_col = column(slot)
        route_col = column(jnp.bitwise_xor(route, lax.axis_index("expert")).astype(F32))
        scale_ref[c * tok_rows : (c + 1) * tok_rows, :] = jnp.broadcast_to(
            column(weights_ref[c : c + 1, :]), (tok_rows, scale_ref.shape[1])
        )
        for k in range(expert_total):
            hit = (slot_col == lane_slots) & (route_col == float(k))
            select_ref[k, c * tok_rows : (c + 1) * tok_rows, :] = hit.astype(BF16)
    wait_all(loads)


def fetch_kernel(pipe_count, plan, gate_ref, up_ref, *refs):
    outs, sems = refs[:-1], refs[-1]
    share = lax.axis_index("pipe")
    pairs = []
    for (which, j), out in zip(plan, outs):
        source = gate_ref if which == "g" else up_ref
        pairs.append((rows_of(source, jnp.bitwise_xor(share, j), out.shape[0]), out))
    wait_all(load_all(pairs, sems))


def join_kernel(j, capacity, own_ref, *refs):
    parts, out_ref = refs[:-1], refs[-1]
    width = out_ref.shape[1]
    share = jnp.bitwise_xor(lax.axis_index("pipe"), j)
    out_ref[0:capacity, :] = own_ref[:, pl.ds(pl.multiple_of(share * width, width), width)]
    for i, part in enumerate(parts):
        out_ref[(i + 1) * capacity : (i + 2) * capacity, :] = part[...]


def gate_up_kernel(j, step, first, last, x_ref, vg_ref, vu_ref, down_ref, *refs):
    sums_in = () if first else refs[:2]
    outs = refs[len(sums_in) :]
    vd_ref, sems = outs[-2], outs[-1]
    share = jnp.bitwise_xor(lax.axis_index("pipe"), j)
    loads = load_all([(cols_of(down_ref, share, vd_ref.shape[1]), vd_ref)], sems)
    width = vg_ref.shape[1]
    for f in range(0, width, step):
        sums = []
        for i, w_ref in enumerate((vg_ref, vu_ref)):
            term = jnp.dot(x_ref[...], w_ref[:, f : f + step], preferred_element_type=F32)
            if not first:
                term += sums_in[i][:, f : f + step]
            sums.append(term)
        if last:
            gate, up = sums
            outs[0][:, f : f + step] = (gate / (1.0 + jnp.exp(-gate)) * up).astype(BF16)
        else:
            for i in range(2):
                outs[i][:, f : f + step] = sums[i]
    wait_all(loads)


def down_kernel(count, hidden_ref, *refs):
    for vd_ref, out_ref in zip(refs[:count], refs[count:]):
        term = jnp.dot(hidden_ref[...], vd_ref[...], preferred_element_type=F32)
        out_ref[...] = term.astype(out_ref.dtype)


def pair_kernel(capacity, mine_ref, other_ref, *outs):
    for k, out_ref in enumerate(outs):
        rows = slice(k * capacity, (k + 1) * capacity)
        total = mine_ref[rows, :] + other_ref[rows, :].astype(F32)
        out_ref[...] = total.astype(BF16)


def down_pair_kernel(hidden_ref, vd_ref, other_ref, out_ref):
    term = jnp.dot(hidden_ref[...], vd_ref[...], preferred_element_type=F32)
    out_ref[...] = term + other_ref[...].astype(F32)


def final_kernel(k, capacity, mine_ref, other_ref, out_ref):
    total = mine_ref[k * capacity : (k + 1) * capacity, :] + other_ref[...].astype(F32)
    out_ref[...] = total.astype(BF16)


def mix_kernel(select_ref, scale_ref, *refs):
    parts, out_ref = refs[:-1], refs[-1]
    total = None
    for k, part in enumerate(parts):
        term = jnp.dot(select_ref[k], part[...], preferred_element_type=F32)
        total = term if total is None else total + term
    tok_rows = out_ref.shape[0]
    first = total[:tok_rows, :] * scale_ref[:tok_rows, 0:1]
    second = total[tok_rows:, :] * scale_ref[tok_rows:, 0:1]
    out_ref[...] = (first + second).astype(BF16)


def call(kernel, outs, args, specs, *, scratch=(), mib, flops=0, nbytes=0, aliases=None, name):
    return pl.pallas_call(
        kernel,
        out_shape=outs,
        in_specs=specs,
        out_specs=[VMEM] * len(outs),
        scratch_shapes=scratch,
        input_output_aliases=aliases or {},
        compiler_params=pltpu.CompilerParams(vmem_limit_bytes=int(mib * MIB)),
        cost_estimate=pl.CostEstimate(flops=int(flops), bytes_accessed=int(nbytes), transcendentals=0),
        name=name,
    )(*args)


def on_device(tokens, routes, route_weights, w_gate, w_up, w_down):
    expert_total = lax.axis_size("expert")
    pipe_count = lax.axis_size("pipe")
    hidden_width = w_gate.shape[2]
    tok_rows, model_width = tokens.shape
    capacity = capacity_of(tok_rows, expert_total, lax.axis_size("dp"))
    col = model_width // pipe_count
    rows = expert_total * capacity
    piece = col * hidden_width * 2
    dma = pltpu.SemaphoreType.DMA
    others = range(1, expert_total)

    def to_core(v):
        return lax.ppermute(v, "pipe", [(i, i ^ 1) for i in range(pipe_count)])

    def to_chip(v):
        return lax.ppermute(v, "pipe", [(i, i ^ 2) for i in range(pipe_count)])

    def to_expert(v, k):
        return lax.ppermute(v, "expert", [(i, i ^ k) for i in range(expert_total)])

    def array(shape, dtype=BF16):
        return jax.ShapeDtypeStruct(shape, dtype)

    wide = pltpu.VMEM((col, hidden_width), BF16)
    tall = pltpu.VMEM((hidden_width, col), BF16)

    routes_t = routes.T
    weights_t = route_weights.T
    own = lax.dynamic_slice_in_dim(tokens, lax.axis_index("pipe") * col, col, 1)
    padded = (capacity + 15) // 16 * 16
    *packed, vg0 = call(
        functools.partial(pack_kernel, pipe_count, capacity, expert_total),
        [array((capacity, col))] * expert_total + [wide],
        (routes_t, own, w_gate),
        [VMEM, VMEM, HBM],
        scratch=[pltpu.VMEM((expert_total * padded, tok_rows), BF16), dma((1,))],
        mib=4,
        flops=2 * rows * tok_rows * col,
        nbytes=piece,
        name="pack",
    )
    order = sorted(others, reverse=True)
    arrived = {k: to_expert(packed[k], k) for k in order}

    own_rows, select, scale, vu0, vg1 = call(
        functools.partial(local_kernel, pipe_count, capacity, expert_total),
        [
            array((capacity, model_width)),
            array((expert_total, 2 * tok_rows, capacity)),
            array((2 * tok_rows, 128), F32),
            wide,
            wide,
        ],
        (routes_t, weights_t, tokens, w_up, w_gate),
        [VMEM, VMEM, VMEM, HBM, HBM],
        scratch=[dma((2,))],
        mib=4,
        flops=2 * rows * tok_rows * model_width,
        nbytes=2 * piece,
        name="local",
    )

    def fetch(plan, name):
        return call(
            functools.partial(fetch_kernel, pipe_count, plan),
            [wide] * len(plan),
            (w_gate, w_up),
            [HBM, HBM],
            scratch=[dma((len(plan),))],
            mib=1,
            nbytes=len(plan) * piece,
            name=name,
        )

    vu1, vg2 = fetch((("u", 1), ("g", 2)), "fetch_a")
    vu2, vg3 = fetch((("u", 2), ("g", 3)), "fetch_b")
    (vu3,) = fetch((("u", 3),), "fetch_c")
    vg, vu = (vg0, vg1, vg2, vg3), (vu0, vu1, vu2, vu3)

    def join(j, parts, name):
        (out,) = call(
            functools.partial(join_kernel, j, capacity),
            [array((rows, col))],
            (own_rows, *[parts[k] for k in others]),
            [VMEM] * expert_total,
            mib=2,
            nbytes=2 * rows * col,
            name=name,
        )
        return out

    crossed = {k: to_chip(arrived[k]) for k in reversed(order)}
    x0 = join(0, arrived, "join_a")
    x1 = to_core(x0)
    x2 = join(2, crossed, "join_b")
    x3 = to_core(x2)

    sums = ()
    vd = {}
    total = pltpu.VMEM((rows, hidden_width), F32)
    for j, x in enumerate((x0, x1, x2, x3)):
        first, last = j == 0, j == pipe_count - 1
        take = pipe_count - 1 - j
        outs = [pltpu.VMEM((rows, hidden_width), BF16)] if last else [total, total]
        *sums, vd[take] = call(
            functools.partial(gate_up_kernel, take, min(512, hidden_width), first, last),
            outs + [tall],
            (x, vg[j], vu[j], w_down, *sums),
            [VMEM, VMEM, VMEM, HBM] + [VMEM] * len(sums),
            scratch=[dma((1,))],
            mib=6,
            flops=4 * rows * col * hidden_width,
            nbytes=piece,
            aliases={} if first or last else {4: 0, 5: 1},
            name=f"gate_up_{j}",
        )
    (hidden,) = sums

    def down(picks, dtypes, name):
        return call(
            functools.partial(down_kernel, len(picks)),
            [array((rows, col), d) for d in dtypes],
            (hidden, *[vd[j] for j in picks]),
            [VMEM] * (1 + len(picks)),
            mib=4,
            flops=2 * rows * col * hidden_width * len(picks),
            nbytes=piece,
            name=name,
        )

    (far_other,) = down((3,), (BF16,), "down_a")
    far_in = to_core(far_other)
    far_mine, near_other = down((2, 1), (F32, BF16), "down_b")
    near_in = to_core(near_other)
    halves = call(
        functools.partial(pair_kernel, capacity),
        [array((capacity, col))] * expert_total,
        (far_mine, far_in),
        [VMEM, VMEM],
        mib=4,
        nbytes=8 * rows * col,
        name="pair",
    )
    back_order = order + [0]
    half_in = {k: to_chip(halves[k]) for k in back_order}
    (mine,) = call(
        down_pair_kernel,
        [array((rows, col), F32)],
        (hidden, vd[0], near_in),
        [VMEM] * 3,
        mib=4,
        flops=2 * rows * col * hidden_width,
        nbytes=piece,
        name="down_c",
    )
    home = {}
    for k in back_order:
        (done,) = call(
            functools.partial(final_kernel, k, capacity),
            [array((capacity, col))],
            (mine, half_in[k]),
            [VMEM, VMEM],
            mib=2,
            nbytes=8 * capacity * col,
            name=f"final_{k}",
        )
        home[k] = to_expert(done, k) if k else done
    (mixed,) = call(
        mix_kernel,
        [array((tok_rows, col))],
        (select, scale, *[home[k] for k in range(expert_total)]),
        [VMEM] * (2 + expert_total),
        mib=4,
        flops=4 * rows * tok_rows * col,
        nbytes=2 * rows * col,
        name="mix",
    )
    return mixed


def solution(mesh):
    experts = mesh.shape["expert"]

    def body(tokens, routes, route_weights, w_gate, w_up, w_down):
        col = tokens.shape[1] // mesh.shape["pipe"]
        fits = (
            mesh.shape["pipe"] == 4
            and experts & (experts - 1) == 0
            and w_gate.shape[0] == 1
            and col % 128 == 0
            and w_gate.shape[2] % 128 == 0
        )
        step = on_device if fits else on_any_mesh
        return step(tokens, routes, route_weights, w_gate, w_up, w_down)

    return jax.shard_map(
        body,
        mesh=mesh,
        in_specs=(
            P(("dp", "expert"), None),
            P(("dp", "expert"), None),
            P(("dp", "expert"), None),
            P("expert", None, "pipe"),
            P("expert", None, "pipe"),
            P("expert", "pipe", None),
        ),
        out_specs=P(("dp", "expert"), "pipe"),
        check_vma=False,
    )
```

time: 133 us -> 62 us (0.47)
  waiting for transfers between devices: 35.3 us -> 5.19 us
  matrix products: 27.1 us -> 0 us
  blocking collectives: 19.8 us -> 0 us
  Pallas kernels: 0 us -> 16.4 us
  starting transfers between devices: 5.56 us -> 20.1 us
  between operations: 13.5 us -> 0.31 us
  local copies, waits for them, and re-layouts: 29.5 us -> 19.7 us
  other arithmetic: 1.53 us -> 0.01 us
    dot_general x4 -> x0, matrix products: 27.1 us -> none  [the longest x1 16.1 us: on_device(): jnp.einsum('gsf,fke->kgse', hidden, down_blocks, preferred_element_type=j...]
    reduce_scatter x1 -> x0, waiting for transfers between devices: 23.7 us -> none  [on_device(): lax.psum_scatter(block_term.astype(jnp.float32).astype(jnp.bfloat16), 'pi...]
    another operation x4 -> x0, local copies, waits for them, and re-layouts: 23.6 us -> none  [the longest x1 23.5 us: on_device(): down_blocks = w_down[0].reshape(hidden_width, pipe_count, col_share)]
    ppermute x0 -> x17, starting transfers between devices: none -> 20.1 us  [the longest x6 11.6 us: to_expert(): return lax.ppermute(v, 'expert', [(i, i ^ k) for i in range(expert_total)])]
    all_to_all x1 -> x0, blocking collectives: 19.8 us -> none  [on_device(): lax.all_to_all(outgoing, ('dp', 'expert'), split_axis=0, concat_axis=0, t...]
    unnamed x8 -> x30, local copies, waits for them, and re-layouts: 0.85 us -> 18.8 us
    pallas_call x0 -> x20, Pallas kernels: none -> 16.4 us  [call(): pl.pallas_call(kernel, out_shape=outs, in_specs=specs, out_specs=[VMEM] *...]
    all_to_all x1 -> x0, waiting for transfers between devices: 11.6 us -> none  [on_device(): lax.all_to_all(summed, ('dp', 'expert'), split_axis=0, concat_axis=0, til...]
  transfers between devices with their start and end apart: 3 -> 17, of which waited for: 2 -> 5; matrix products, arithmetic and copies ran while one was open for 18% -> 0% of each run, Pallas kernels for 0% -> 18%
where the time goes in v1:
time: 62 us; the launch traced here: 61.7 us
  starting transfers between devices  20.1 us (32%)
  local copies, waits for them, and re-layouts  19.7 us (32%)
  Pallas kernels  16.4 us (26%)
  waiting for transfers between devices  5.19 us (8%)
    unnamed x30, local copies, waits for them, and re-layouts  18.8 us
    pallas_call x20, Pallas kernels, call(): pl.pallas_call(kernel, out_shape=outs, in_specs=specs, out_specs=[VMEM] *...  16.4 us
    ppermute x6, starting transfers between devices, to_expert(): return lax.ppermute(v, 'expert', [(i, i ^ k) for i in range(expert_total)])  11.6 us
    ppermute x7, starting transfers between devices, to_chip(): return lax.ppermute(v, 'pipe', [(i, i ^ 2) for i in range(pipe_count)])  7.73 us
    ppermute x6, waiting for transfers between devices, to_expert(): return lax.ppermute(v, 'expert', [(i, i ^ k) for i in range(expert_total)])  4.67 us
  transfers between devices with their start and end apart: 17, of which 5 were waited for; matrix products, arithmetic and copies ran while one was open for 0% of the time, Pallas kernels for 18%

profile of v1, /device:TPU:0, one launch (start us, length us, event | category | flops | bytes accessed | tf_op | source)
XLA Modules:
  0.0 61.7 jit_solution(8559197445241685342)
XLA Ops:
  0.0 0.9 %constant_dynamic-slice_fusion.own_ref = bf16[96,768]{1,0:T(8,128)(2,1)S(1)} fusion(bf16[96,3072]{1,0:T(8,128)(2,1)} %tokens_ref.1, s32[]{:T(128)S(6)} %select_n.3), kind=kLoop, calls=%fused_computation | loop fusion | bytes 294916 | tf_op jit(solution)/shard_map/dynamic_slice | solution.py:279
  0.9 4.6 %copy-done = bf16[1,3072,2048]{2,1,0:T(8,128)(2,1)S(1)} copy-done((bf16[1,3072,2048]{2,1,0:T(8,128)(2,1)S(1)}, bf16[1,3072,2048]{2,1,0:T(8,128)(2,1)}, u32[]{:S(2)}) %copy-start) | copy-done | bytes 12582936
  5.5 0.7 %copy-done.10 = s32[96,2]{0,1:T(2,128)S(1)} copy-done((s32[96,2]{0,1:T(2,128)S(1)}, s32[96,2]{0,1:T(2,128)}, u32[]{:S(2)}) %copy-start.10) | copy-done | bytes 792
  6.2 1.2 %pack.1 = (bf16[50,768]{1,0:T(8,128)(2,1)}, bf16[50,768]{1,0:T(8,128)(2,1)S(1)}, bf16[50,768]{1,0:T(8,128)(2,1)S(1)}, bf16[50,768]{1,0:T(8,128)(2,1)S(1)}, bf16[768,2048]{1,0:T(8,128)(2,1)S(1)}) custom-call(s32[2,96]{1,0:T(2,128)S(1)} %bitcast.4, bf16[96,768]{1,0:T(8,128)(2,1)S(1)} %constant_dynamic-slice_fusion.own_ref, bf16[1,3072,2048]{2,1,0:T(8,128)(2,1)S(1)} %copy-done), custom_call_target="tpu_custom_call" | custom-call | flops 29491200 | bytes 3145728 | tf_op jit(solution)/shard_map/pack/pallas_call | solution.py:237
  7.4 3.1 %collective-permute-start = (bf16[50,768]{1,0:T(8,128)(2,1)S(1)}, bf16[50,768]{1,0:T(8,128)(2,1)S(1)}, u32[]{:S(2)}, u32[]{:S(2)}) collective-permute-start(bf16[50,768]{1,0:T(8,128)(2,1)S(1)} %get-tuple-element.38), channel_id=1, source_target_pairs={{0,1},{1,0},{2,3},{3,2},{4,5},{5,4},{6,7},{7,6},{8,9},{9,8},{10,11... | collective-permute-start | bytes 230408 | tf_op jit(solution)/shard_map/ppermute | solution.py:269
  10.6 2.6 %collective-permute-start.2 = (bf16[50,768]{1,0:T(8,128)(2,1)S(1)}, bf16[50,768]{1,0:T(8,128)(2,1)S(1)}, u32[]{:S(2)}, u32[]{:S(2)}) collective-permute-start(bf16[50,768]{1,0:T(8,128)(2,1)S(1)} %get-tuple-element.39), channel_id=1, source_target_pairs={{0,2},{1,3},{2,0},{3,1},{4,6},{5,7},{6,4},{7,5},{8,10},{9,11},{10,... | collective-permute-start | bytes 230408 | tf_op jit(solution)/shard_map/ppermute | solution.py:269
  13.2 4.6 %copy-done.2 = bf16[1,3072,2048]{2,1,0:T(8,128)(2,1)S(1)} copy-done((bf16[1,3072,2048]{2,1,0:T(8,128)(2,1)S(1)}, bf16[1,3072,2048]{2,1,0:T(8,128)(2,1)}, u32[]{:S(2)}) %copy-start.2) | copy-done | bytes 12582936
  17.7 1.1 %copy-done.9 = bf16[96,3072]{1,0:T(8,128)(2,1)S(1)} copy-done((bf16[96,3072]{1,0:T(8,128)(2,1)S(1)}, bf16[96,3072]{1,0:T(8,128)(2,1)}, u32[]{:S(2)}) %copy-start.9) | copy-done | bytes 589848
  18.8 0.8 %local.1 = (bf16[50,3072]{1,0:T(8,128)(2,1)S(1)}, bf16[4,192,50]{2,1,0:T(8,128)(2,1)S(1)}, f32[192,128]{1,0:T(8,128)S(1)}, bf16[768,2048]{1,0:T(8,128)(2,1)S(1)}, bf16[768,2048]{1,0:T(8,128)(2,1)S(1)}) custom-call(s32[2,96]{1,0:T(2,128)S(1)} %bitcast.5, f32[2,96]{1,0:T(2,128)S(1)} %bitcast.6, bf16[96,3072]{1,0:T(8,128)(2,1)S(1)} %copy-done.9, ...), custom_call_target="tpu_custom_call" | custom-call | flops 117964800 | bytes 6291456 | tf_op jit(solution)/shard_map/local/pallas_call | solution.py:237
  20.2 1.6 %collective-permute-start.1 = (bf16[50,768]{1,0:T(8,128)(2,1)S(1)}, bf16[50,768]{1,0:T(8,128)(2,1)S(1)}, u32[]{:S(2)}, u32[]{:S(2)}) collective-permute-start(bf16[50,768]{1,0:T(8,128)(2,1)S(1)} %collective-permute-done.refs_0_), channel_id=1, source_target_pairs={{0,8},{4,12},{8,0},{12,4},{1,9},{5,13},{9,1},{13,5},{2,10},{6,14},... | collective-permute-start | bytes 230408 | tf_op jit(solution)/shard_map/ppermute | solution.py:266
  22.3 1.5 %collective-permute-start.5 = (bf16[50,768]{1,0:T(8,128)(2,1)S(1)}, bf16[50,768]{1,0:T(8,128)(2,1)S(1)}, u32[]{:S(2)}, u32[]{:S(2)}) collective-permute-start(bf16[50,768]{1,0:T(8,128)(2,1)S(1)} %collective-permute-done.4.refs_2_), channel_id=1, source_target_pairs={{0,8},{4,12},{8,0},{12,4},{1,9},{5,13},{9,1},{13,5},{2,10},{6,14},... | collective-permute-start | bytes 230408 | tf_op jit(solution)/shard_map/ppermute | solution.py:266
  24.2 1.7 %copy-done.7 = bf16[768,2048]{1,0:T(8,128)(2,1)} copy-done((bf16[768,2048]{1,0:T(8,128)(2,1)}, bf16[768,2048]{1,0:T(8,128)(2,1)S(1)}, u32[]{:S(2)}) %copy-start.7) | copy-done | bytes 3145752
  26.4 1.6 %copy-done.3 = bf16[768,2048]{1,0:T(8,128)(2,1)} copy-done((bf16[768,2048]{1,0:T(8,128)(2,1)}, bf16[768,2048]{1,0:T(8,128)(2,1)S(1)}, u32[]{:S(2)}) %copy-start.3) | copy-done | bytes 3145752
  28.0 1.7 %copy-done.5 = bf16[768,2048]{1,0:T(8,128)(2,1)} copy-done((bf16[768,2048]{1,0:T(8,128)(2,1)}, bf16[768,2048]{1,0:T(8,128)(2,1)S(1)}, u32[]{:S(2)}) %copy-start.5) | copy-done | bytes 3145752
  30.1 1.6 %slice-done.1 = s8[4194304]{0:T(1024)(128)(4,1)S(1)} async-done(((s8[12582912]{0:T(1024)(128)(4,1)}), s8[4194304]{0:T(1024)(128)(4,1)S(1)}, s32[]{:S(2)}) %slice-start.1) | async-done | bytes 4194328
  31.7 1.3 %slice-done.2 = s8[4194304]{0:T(1024)(128)(4,1)S(1)} async-done(((s8[12582912]{0:T(1024)(128)(4,1)}), s8[4194304]{0:T(1024)(128)(4,1)S(1)}, s32[]{:S(2)}) %slice-start.2) | async-done | bytes 4194328
  33.0 1.9 %gate_up_0.1 = (f32[200,2048]{1,0:T(8,128)S(1)}, f32[200,2048]{1,0:T(8,128)S(1)}, bf16[2048,768]{1,0:T(8,128)(2,1)S(1)}) custom-call(bf16[200,768]{1,0:T(8,128)(2,1)S(1)} %join_a.1.x_ref, bf16[768,2048]{1,0:T(8,128)(2,1)S(1)} %get-tuple-element.46.vg_ref, bf16[768,2048]{1,0:T(8,128)(2,1)S(1)} %get-tuple-element.47.vu_ref, bf16[1,2048,3072]{2,1,0:T(8,128)(2,1)S(1)} %bitcast.3), custom_call_target="tpu_custom_call" | custom-call | flops 1258291200 | bytes 3145728 | tf_op jit(solution)/shard_map/gate_up_0/pallas_call | solution.py:237
  34.9 2.3 %gate_up_1.1 = (f32[200,2048]{1,0:T(8,128)S(1)}, f32[200,2048]{1,0:T(8,128)S(1)}, bf16[2048,768]{1,0:T(8,128)(2,1)S(1)}) custom-call(bf16[200,768]{1,0:T(8,128)(2,1)S(1)} %collective-permute-done.7.x_ref, bf16[768,2048]{1,0:T(8,128)(2,1)S(1)} %get-tuple-element.44.vg_ref, ...), custom_call_target="tpu_custom_call", output_to_operand_aliasing={{0}: (4, {}), {1}: (5, {})} | custom-call | flops 1258291200 | bytes 3145728 | tf_op jit(solution)/shard_map/gate_up_1/pallas_call | solution.py:237
  37.2 2.2 %gate_up_2.1 = (f32[200,2048]{1,0:T(8,128)S(1)}, f32[200,2048]{1,0:T(8,128)S(1)}, bf16[2048,768]{1,0:T(8,128)(2,1)S(1)}) custom-call(bf16[200,768]{1,0:T(8,128)(2,1)S(1)} %join_b.1.x_ref, bf16[768,2048]{1,0:T(8,128)(2,1)S(1)} %get-tuple-element.42.vg_ref, bf16[768,2048]{1,0:T(8,128)(2,1)S(1)} %copy-done.6, ...), custom_call_target="tpu_custom_call", output_to_operand_aliasing={{0}: (4, {}), {1}: (5, {})} | custom-call | flops 1258291200 | bytes 3145728 | tf_op jit(solution)/shard_map/gate_up_2/pallas_call | solution.py:237
  39.5 2.2 %gate_up_3.1 = (bf16[200,2048]{1,0:T(8,128)(2,1)S(1)}, bf16[2048,768]{1,0:T(8,128)(2,1)S(1)}) custom-call(bf16[200,768]{1,0:T(8,128)(2,1)S(1)} %collective-permute-done.6.x_ref, bf16[768,2048]{1,0:T(8,128)(2,1)S(1)} %copy-done.4, bf16[768,2048]{1,0:T(8,128)(2,1)S(1)} %fetch_c.1.vu_ref, bf16[1,2048,3072]{2,1,0:T(8,128)(2,1)S(1)} %bitcast.3, ...), custom_call_target="tpu_custom_call" | custom-call | flops 1258291200 | bytes 3145728 | tf_op jit(solution)/shard_map/gate_up_3/pallas_call | solution.py:237
  41.6 0.8 %down_a.1 = bf16[200,768]{1,0:T(8,128)(2,1)S(1)} custom-call(bf16[200,2048]{1,0:T(8,128)(2,1)S(1)} %get-tuple-element.54.hidden_ref, bf16[2048,768]{1,0:T(8,128)(2,1)S(1)} %get-tuple-element.60.refs_0_), custom_call_target="tpu_custom_call" | custom-call | flops 629145600 | bytes 3145728 | tf_op jit(solution)/shard_map/down_a/pallas_call | solution.py:237
  42.6 1.5 %down_b.1 = (f32[200,768]{1,0:T(8,128)S(1)}, bf16[200,768]{1,0:T(8,128)(2,1)S(1)}) custom-call(bf16[200,2048]{1,0:T(8,128)(2,1)S(1)} %get-tuple-element.54.hidden_ref, bf16[2048,768]{1,0:T(8,128)(2,1)S(1)} %get-tuple-element.56.refs_0_, bf16[2048,768]{1,0:T(8,128)(2,1)S(1)} %get-tuple-element.57.refs_1_), custom_call_target="tpu_custom_call" | custom-call | flops 1258291200 | bytes 3145728 | tf_op jit(solution)/shard_map/down_b/pallas_call | solution.py:237
  44.1 0.6 collective-permute-start.8
  44.8 0.6 collective-permute-start.15
  45.3 1.5 %collective-permute-start.13 = (bf16[50,768]{1,0:T(8,128)(2,1)S(1)}, bf16[50,768]{1,0:T(8,128)(2,1)S(1)}, u32[]{:S(2)}, u32[]{:S(2)}) collective-permute-start(bf16[50,768]{1,0:T(8,128)(2,1)S(1)} %get-tuple-element.63), channel_id=1, source_target_pairs={{0,8},{4,12},{8,0},{12,4},{1,9},{5,13},{9,1},{13,5},{2,10},{6,14},... | collective-permute-start | bytes 230408 | tf_op jit(solution)/shard_map/ppermute | solution.py:266
  47.4 1.5 %collective-permute-start.10 = (bf16[50,768]{1,0:T(8,128)(2,1)S(1)}, bf16[50,768]{1,0:T(8,128)(2,1)S(1)}, u32[]{:S(2)}, u32[]{:S(2)}) collective-permute-start(bf16[50,768]{1,0:T(8,128)(2,1)S(1)} %get-tuple-element.61), channel_id=1, source_target_pairs={{0,8},{4,12},{8,0},{12,4},{1,9},{5,13},{9,1},{13,5},{2,10},{6,14},... | collective-permute-start | bytes 230408 | tf_op jit(solution)/shard_map/ppermute | solution.py:266
  48.9 0.8 %down_c.1.mine_ref = f32[200,768]{1,0:T(8,128)S(1)} custom-call(bf16[200,2048]{1,0:T(8,128)(2,1)S(1)} %get-tuple-element.54.hidden_ref, bf16[2048,768]{1,0:T(8,128)(2,1)S(1)} %get-tuple-element.55.vd_ref, bf16[200,768]{1,0:T(8,128)(2,1)S(1)} %collective-permute-done.8.other_ref), custom_call_target="tpu_custom_call" | custom-call | flops 629145600 | bytes 3145728 | tf_op jit(solution)/shard_map/down_c/pallas_call | solution.py:237
  50.3 3.5 %collective-permute-start.16 = (bf16[50,768]{1,0:T(8,128)(2,1)S(1)}, bf16[50,768]{1,0:T(8,128)(2,1)S(1)}, u32[]{:S(2)}, u32[]{:S(2)}) collective-permute-start(bf16[50,768]{1,0:T(8,128)(2,1)S(1)} %final_3.1), channel_id=1, source_target_pairs={{0,3},{1,2},{2,1},{3,0},{4,7},{5,6},{6,5},{7,4},{8,11},{9,10},{10,... | collective-permute-start | bytes 230408 | tf_op jit(solution)/shard_map/ppermute | solution.py:269
  53.8 0.9 %collective-permute-start.14 = (bf16[50,768]{1,0:T(8,128)(2,1)S(1)}, bf16[50,768]{1,0:T(8,128)(2,1)S(1)}, u32[]{:S(2)}, u32[]{:S(2)}) collective-permute-start(bf16[50,768]{1,0:T(8,128)(2,1)S(1)} %final_2.1), channel_id=1, source_target_pairs={{0,2},{1,3},{2,0},{3,1},{4,6},{5,7},{6,4},{7,5},{8,10},{9,11},{10,... | collective-permute-start | bytes 230408 | tf_op jit(solution)/shard_map/ppermute | solution.py:269
  54.7 1.6 %collective-permute-start.12 = (bf16[50,768]{1,0:T(8,128)(2,1)S(1)}, bf16[50,768]{1,0:T(8,128)(2,1)S(1)}, u32[]{:S(2)}, u32[]{:S(2)}) collective-permute-start(bf16[50,768]{1,0:T(8,128)(2,1)S(1)} %final_1.1), channel_id=1, source_target_pairs={{0,1},{1,0},{2,3},{3,2},{4,5},{5,4},{6,7},{7,6},{8,9},{9,8},{10,11... | collective-permute-start | bytes 230408 | tf_op jit(solution)/shard_map/ppermute | solution.py:269
  56.9 3.6 %collective-permute-done.14.refs_2_ = bf16[50,768]{1,0:T(8,128)(2,1)S(1)} collective-permute-done((bf16[50,768]{1,0:T(8,128)(2,1)S(1)}, bf16[50,768]{1,0:T(8,128)(2,1)S(1)}, u32[]{:S(2)}, u32[]{:S(2)}) %collective-permute-start.14) | collective-permute-done | bytes 76832 | tf_op jit(solution)/shard_map/ppermute | solution.py:269
  60.6 1.1 %mix.1 = bf16[96,768]{1,0:T(8,128)(2,1)} custom-call(bf16[4,192,50]{2,1,0:T(8,128)(2,1)S(1)} %get-tuple-element.35.select_ref, f32[192,128]{1,0:T(8,128)S(1)} %get-tuple-element.36.scale_ref, bf16[50,768]{1,0:T(8,128)(2,1)S(1)} %final_0.1.refs_0_, bf16[50,768]{1,0:T(8,128)(2,1)S(1)} %collective-permute-done.12.refs_1_, ...), custom_call_target="tpu_custom_call" | custom-call | flops 58982400 | bytes 307200 | tf_op jit(solution)/shard_map/mix/pallas_call | solution.py:237
  (54 shorter events, 4.3 us)
Async XLA Ops:
  0.9 4.6 %copy-start = (bf16[1,3072,2048]{2,1,0:T(8,128)(2,1)S(1)}, bf16[1,3072,2048]{2,1,0:T(8,128)(2,1)}, u32[]{:S(2)}) copy-start(bf16[1,3072,2048]{2,1,0:T(8,128)(2,1)} %gate_ref.9) | copy-start | bytes 37748740
  5.5 0.7 %copy-start.10 = (s32[96,2]{0,1:T(2,128)S(1)}, s32[96,2]{0,1:T(2,128)}, u32[]{:S(2)}) copy-start(s32[96,2]{0,1:T(2,128)} %param.7) | copy-start | bytes 2308
  6.2 7.0 %copy-start.1 = (bf16[1,3072,2048]{2,1,0:T(8,128)(2,1)S(1)}, bf16[1,3072,2048]{2,1,0:T(8,128)(2,1)}, u32[]{:S(2)}) copy-start(bf16[1,3072,2048]{2,1,0:T(8,128)(2,1)} %gate_ref.9) | copy-start | bytes 37748740
  6.2 7.0 %copy-start.11 = (f32[96,2]{0,1:T(2,128)S(1)}, f32[96,2]{0,1:T(2,128)}, u32[]{:S(2)}) copy-start(f32[96,2]{0,1:T(2,128)} %param.8) | copy-start | bytes 2308
  7.4 12.2 %collective-permute-start = (bf16[50,768]{1,0:T(8,128)(2,1)S(1)}, bf16[50,768]{1,0:T(8,128)(2,1)S(1)}, u32[]{:S(2)}, u32[]{:S(2)}) collective-permute-start(bf16[50,768]{1,0:T(8,128)(2,1)S(1)} %get-tuple-element.38), channel_id=1, source_target_pairs={{0,1},{1,0},{2,3},{3,2},{4,5},{5,4},{6,7},{7,6},{8,9},{9,8},{10,11... | collective-permute-start | bytes 230408 | tf_op jit(solution)/shard_map/ppermute | solution.py:269
  10.6 9.5 %collective-permute-start.2 = (bf16[50,768]{1,0:T(8,128)(2,1)S(1)}, bf16[50,768]{1,0:T(8,128)(2,1)S(1)}, u32[]{:S(2)}, u32[]{:S(2)}) collective-permute-start(bf16[50,768]{1,0:T(8,128)(2,1)S(1)} %get-tuple-element.39), channel_id=1, source_target_pairs={{0,2},{1,3},{2,0},{3,1},{4,6},{5,7},{6,4},{7,5},{8,10},{9,11},{10,... | collective-permute-start | bytes 230408 | tf_op jit(solution)/shard_map/ppermute | solution.py:269
  13.1 6.9 %collective-permute-start.4 = (bf16[50,768]{1,0:T(8,128)(2,1)S(1)}, bf16[50,768]{1,0:T(8,128)(2,1)S(1)}, u32[]{:S(2)}, u32[]{:S(2)}) collective-permute-start(bf16[50,768]{1,0:T(8,128)(2,1)S(1)} %get-tuple-element.40), channel_id=1, source_target_pairs={{0,3},{1,2},{2,1},{3,0},{4,7},{5,6},{6,5},{7,4},{8,11},{9,10},{10,... | collective-permute-start | bytes 230408 | tf_op jit(solution)/shard_map/ppermute | solution.py:269
  13.2 4.6 %copy-start.2 = (bf16[1,3072,2048]{2,1,0:T(8,128)(2,1)S(1)}, bf16[1,3072,2048]{2,1,0:T(8,128)(2,1)}, u32[]{:S(2)}) copy-start(bf16[1,3072,2048]{2,1,0:T(8,128)(2,1)} %up_ref.7) | copy-start | bytes 37748740
  17.7 1.1 %copy-start.9 = (bf16[96,3072]{1,0:T(8,128)(2,1)S(1)}, bf16[96,3072]{1,0:T(8,128)(2,1)}, u32[]{:S(2)}) copy-start(bf16[96,3072]{1,0:T(8,128)(2,1)} %tokens_ref.1) | copy-start | bytes 1769476
  20.1 14.8 %collective-permute-start.7 = (bf16[200,768]{1,0:T(8,128)(2,1)S(1)}, bf16[200,768]{1,0:T(8,128)(2,1)S(1)}, u32[]{:S(2)}, u32[]{:S(2)}) collective-permute-start(bf16[200,768]{1,0:T(8,128)(2,1)S(1)} %join_a.1.x_ref), channel_id=1, source_target_pairs={{0,4},{4,0},{8,12},{12,8},{1,5},{5,1},{9,13},{13,9},{2,6},{6,2},{1... | collective-permute-start | bytes 921608 | tf_op jit(solution)/shard_map/ppermute | solution.py:263
  20.2 9.8 %collective-permute-start.1 = (bf16[50,768]{1,0:T(8,128)(2,1)S(1)}, bf16[50,768]{1,0:T(8,128)(2,1)S(1)}, u32[]{:S(2)}, u32[]{:S(2)}) collective-permute-start(bf16[50,768]{1,0:T(8,128)(2,1)S(1)} %collective-permute-done.refs_0_), channel_id=1, source_target_pairs={{0,8},{4,12},{8,0},{12,4},{1,9},{5,13},{9,1},{13,5},{2,10},{6,14},... | collective-permute-start | bytes 230408 | tf_op jit(solution)/shard_map/ppermute | solution.py:266
  21.8 8.2 %collective-permute-start.3 = (bf16[50,768]{1,0:T(8,128)(2,1)S(1)}, bf16[50,768]{1,0:T(8,128)(2,1)S(1)}, u32[]{:S(2)}, u32[]{:S(2)}) collective-permute-start(bf16[50,768]{1,0:T(8,128)(2,1)S(1)} %collective-permute-done.2.refs_1_), channel_id=1, source_target_pairs={{0,8},{4,12},{8,0},{12,4},{1,9},{5,13},{9,1},{13,5},{2,10},{6,14},... | collective-permute-start | bytes 230408 | tf_op jit(solution)/shard_map/ppermute | solution.py:266
  22.3 7.7 %collective-permute-start.5 = (bf16[50,768]{1,0:T(8,128)(2,1)S(1)}, bf16[50,768]{1,0:T(8,128)(2,1)S(1)}, u32[]{:S(2)}, u32[]{:S(2)}) collective-permute-start(bf16[50,768]{1,0:T(8,128)(2,1)S(1)} %collective-permute-done.4.refs_2_), channel_id=1, source_target_pairs={{0,8},{4,12},{8,0},{12,4},{1,9},{5,13},{9,1},{13,5},{2,10},{6,14},... | collective-permute-start | bytes 230408 | tf_op jit(solution)/shard_map/ppermute | solution.py:266
  24.2 1.7 %copy-start.7 = (bf16[768,2048]{1,0:T(8,128)(2,1)}, bf16[768,2048]{1,0:T(8,128)(2,1)S(1)}, u32[]{:S(2)}) copy-start(bf16[768,2048]{1,0:T(8,128)(2,1)S(1)} %get-tuple-element.45.vu_ref) | copy-start | bytes 9437188
  25.9 4.2 %slice-start = ((s8[12582912]{0:T(1024)(128)(4,1)}), s8[4194304]{0:T(1024)(128)(4,1)S(1)}, s32[]{:S(2)}) async-start(s8[12582912]{0:T(1024)(128)(4,1)} %bitcast.2), calls=%async_computation | async-start | bytes 8388608
  25.9 5.7 %slice-start.1 = ((s8[12582912]{0:T(1024)(128)(4,1)}), s8[4194304]{0:T(1024)(128)(4,1)S(1)}, s32[]{:S(2)}) async-start(s8[12582912]{0:T(1024)(128)(4,1)} %bitcast.2), calls=%async_computation.1 | async-start | bytes 8388608
  26.4 1.6 %copy-start.3 = (bf16[768,2048]{1,0:T(8,128)(2,1)}, bf16[768,2048]{1,0:T(8,128)(2,1)S(1)}, u32[]{:S(2)}) copy-start(bf16[768,2048]{1,0:T(8,128)(2,1)S(1)} %get-tuple-element.41.vg_ref) | copy-start | bytes 9437188
  28.0 1.7 %copy-start.5 = (bf16[768,2048]{1,0:T(8,128)(2,1)}, bf16[768,2048]{1,0:T(8,128)(2,1)S(1)}, u32[]{:S(2)}) copy-start(bf16[768,2048]{1,0:T(8,128)(2,1)S(1)} %get-tuple-element.43.vu_ref) | copy-start | bytes 9437188
  29.7 3.3 %slice-start.2 = ((s8[12582912]{0:T(1024)(128)(4,1)}), s8[4194304]{0:T(1024)(128)(4,1)S(1)}, s32[]{:S(2)}) async-start(s8[12582912]{0:T(1024)(128)(4,1)} %bitcast.2), calls=%async_computation.2 | async-start | bytes 8388608
  30.0 9.4 %collective-permute-start.6 = (bf16[200,768]{1,0:T(8,128)(2,1)S(1)}, bf16[200,768]{1,0:T(8,128)(2,1)S(1)}, u32[]{:S(2)}, u32[]{:S(2)}) collective-permute-start(bf16[200,768]{1,0:T(8,128)(2,1)S(1)} %join_b.1.x_ref), channel_id=1, source_target_pairs={{0,4},{4,0},{8,12},{12,8},{1,5},{5,1},{9,13},{13,9},{2,6},{6,2},{1... | collective-permute-start | bytes 921608 | tf_op jit(solution)/shard_map/ppermute | solution.py:263
  33.0 1.9 %copy-start.8 = (bf16[768,2048]{1,0:T(8,128)(2,1)S(1)}, bf16[768,2048]{1,0:T(8,128)(2,1)}, u32[]{:S(2)}) copy-start(bf16[768,2048]{1,0:T(8,128)(2,1)} %copy-done.7) | copy-start | bytes 9437188
  34.9 2.3 %copy-start.6 = (bf16[768,2048]{1,0:T(8,128)(2,1)S(1)}, bf16[768,2048]{1,0:T(8,128)(2,1)}, u32[]{:S(2)}) copy-start(bf16[768,2048]{1,0:T(8,128)(2,1)} %copy-done.5) | copy-start | bytes 9437188
  37.2 2.2 %copy-start.4 = (bf16[768,2048]{1,0:T(8,128)(2,1)S(1)}, bf16[768,2048]{1,0:T(8,128)(2,1)}, u32[]{:S(2)}) copy-start(bf16[768,2048]{1,0:T(8,128)(2,1)} %copy-done.3) | copy-start | bytes 9437188
  42.5 2.2 %collective-permute-start.9 = (bf16[200,768]{1,0:T(8,128)(2,1)S(1)}, bf16[200,768]{1,0:T(8,128)(2,1)S(1)}, u32[]{:S(2)}, u32[]{:S(2)}) collective-permute-start(bf16[200,768]{1,0:T(8,128)(2,1)S(1)} %down_a.1), channel_id=1, source_target_pairs={{0,4},{4,0},{8,12},{12,8},{1,5},{5,1},{9,13},{13,9},{2,6},{6,2},{1... | collective-permute-start | bytes 921608 | tf_op jit(solution)/shard_map/ppermute | solution.py:263
  44.1 4.8 %collective-permute-start.8 = (bf16[200,768]{1,0:T(8,128)(2,1)S(1)}, bf16[200,768]{1,0:T(8,128)(2,1)S(1)}, u32[]{:S(2)}, u32[]{:S(2)}) collective-permute-start(bf16[200,768]{1,0:T(8,128)(2,1)S(1)} %get-tuple-element.58), channel_id=1, source_target_pairs={{0,4},{4,0},{8,12},{12,8},{1,5},{5,1},{9,13},{13,9},{2,6},{6,2},{1... | collective-permute-start | bytes 921608 | tf_op jit(solution)/shard_map/ppermute | solution.py:263
  44.8 5.5 %collective-permute-start.15 = (bf16[50,768]{1,0:T(8,128)(2,1)S(1)}, bf16[50,768]{1,0:T(8,128)(2,1)S(1)}, u32[]{:S(2)}, u32[]{:S(2)}) collective-permute-start(bf16[50,768]{1,0:T(8,128)(2,1)S(1)} %get-tuple-element.64), channel_id=1, source_target_pairs={{0,8},{4,12},{8,0},{12,4},{1,9},{5,13},{9,1},{13,5},{2,10},{6,14},... | collective-permute-start | bytes 230408 | tf_op jit(solution)/shard_map/ppermute | solution.py:266
  45.3 8.4 %collective-permute-start.13 = (bf16[50,768]{1,0:T(8,128)(2,1)S(1)}, bf16[50,768]{1,0:T(8,128)(2,1)S(1)}, u32[]{:S(2)}, u32[]{:S(2)}) collective-permute-start(bf16[50,768]{1,0:T(8,128)(2,1)S(1)} %get-tuple-element.63), channel_id=1, source_target_pairs={{0,8},{4,12},{8,0},{12,4},{1,9},{5,13},{9,1},{13,5},{2,10},{6,14},... | collective-permute-start | bytes 230408 | tf_op jit(solution)/shard_map/ppermute | solution.py:266
  46.9 7.8 %collective-permute-start.11 = (bf16[50,768]{1,0:T(8,128)(2,1)S(1)}, bf16[50,768]{1,0:T(8,128)(2,1)S(1)}, u32[]{:S(2)}, u32[]{:S(2)}) collective-permute-start(bf16[50,768]{1,0:T(8,128)(2,1)S(1)} %get-tuple-element.62), channel_id=1, source_target_pairs={{0,8},{4,12},{8,0},{12,4},{1,9},{5,13},{9,1},{13,5},{2,10},{6,14},... | collective-permute-start | bytes 230408 | tf_op jit(solution)/shard_map/ppermute | solution.py:266
  47.4 8.9 %collective-permute-start.10 = (bf16[50,768]{1,0:T(8,128)(2,1)S(1)}, bf16[50,768]{1,0:T(8,128)(2,1)S(1)}, u32[]{:S(2)}, u32[]{:S(2)}) collective-permute-start(bf16[50,768]{1,0:T(8,128)(2,1)S(1)} %get-tuple-element.61), channel_id=1, source_target_pairs={{0,8},{4,12},{8,0},{12,4},{1,9},{5,13},{9,1},{13,5},{2,10},{6,14},... | collective-permute-start | bytes 230408 | tf_op jit(solution)/shard_map/ppermute | solution.py:266
  50.3 6.6 %collective-permute-start.16 = (bf16[50,768]{1,0:T(8,128)(2,1)S(1)}, bf16[50,768]{1,0:T(8,128)(2,1)S(1)}, u32[]{:S(2)}, u32[]{:S(2)}) collective-permute-start(bf16[50,768]{1,0:T(8,128)(2,1)S(1)} %final_3.1), channel_id=1, source_target_pairs={{0,3},{1,2},{2,1},{3,0},{4,7},{5,6},{6,5},{7,4},{8,11},{9,10},{10,... | collective-permute-start | bytes 230408 | tf_op jit(solution)/shard_map/ppermute | solution.py:269
  53.8 6.6 %collective-permute-start.14 = (bf16[50,768]{1,0:T(8,128)(2,1)S(1)}, bf16[50,768]{1,0:T(8,128)(2,1)S(1)}, u32[]{:S(2)}, u32[]{:S(2)}) collective-permute-start(bf16[50,768]{1,0:T(8,128)(2,1)S(1)} %final_2.1), channel_id=1, source_target_pairs={{0,2},{1,3},{2,0},{3,1},{4,6},{5,7},{6,4},{7,5},{8,10},{9,11},{10,... | collective-permute-start | bytes 230408 | tf_op jit(solution)/shard_map/ppermute | solution.py:269
  54.7 5.8 %collective-permute-start.12 = (bf16[50,768]{1,0:T(8,128)(2,1)S(1)}, bf16[50,768]{1,0:T(8,128)(2,1)S(1)}, u32[]{:S(2)}, u32[]{:S(2)}) collective-permute-start(bf16[50,768]{1,0:T(8,128)(2,1)S(1)} %final_1.1), channel_id=1, source_target_pairs={{0,1},{1,0},{2,3},{3,2},{4,5},{5,4},{6,7},{7,6},{8,9},{9,8},{10,11... | collective-permute-start | bytes 230408 | tf_op jit(solution)/shard_map/ppermute | solution.py:269

commit v2 on v1

v2 whole, which is shorter than its diff:
```python
import functools

import jax
import jax.numpy as jnp
from jax import lax
from jax.experimental import pallas as pl
from jax.experimental.pallas import tpu as pltpu
from jax.sharding import PartitionSpec as P


F32 = jnp.float32
BF16 = jnp.bfloat16
HBM = pl.BlockSpec(memory_space=pltpu.HBM)
VMEM = pl.BlockSpec(memory_space=pltpu.VMEM)
MIB = 1 << 20
PACK_COST = 0
LOCAL_COST = 12 << 20


def capacity_of(tok_rows, expert_total, replica_count):
    per_expert = (2 * tok_rows + expert_total - 1) // expert_total
    return min(tok_rows, replica_count * (per_expert // replica_count + 1))


def slot_table(route_rows, expert_total):
    choices = route_rows.reshape(-1)
    expert_ids = jnp.arange(expert_total, dtype=jnp.int32)
    matches = (choices[None, :] == expert_ids[:, None]).astype(jnp.int32)
    rank_of = jnp.cumsum(matches, axis=1) - 1
    return (choices, jnp.sum(rank_of * matches, axis=0))


def on_any_mesh(tokens, routes, route_weights, w_gate, w_up, w_down):
    expert_total = w_gate.shape[0] * lax.axis_size("expert")
    pipe_count = lax.axis_size("pipe")
    hidden_width = w_gate.shape[2]
    tok_rows, model_width = tokens.shape
    capacity = capacity_of(tok_rows, expert_total, lax.axis_size("dp"))
    col_share = model_width // pipe_count
    choices, slot_of = slot_table(routes, expert_total)
    target = choices * capacity + slot_of
    column_ids = jnp.arange(expert_total * capacity, dtype=jnp.int32)
    picker = (column_ids[:, None] == target[None, :]).astype(BF16)
    own_columns = lax.dynamic_slice_in_dim(tokens, lax.axis_index("pipe") * col_share, col_share, 1)
    outgoing = jnp.dot(picker, jnp.repeat(own_columns, 2, axis=0), preferred_element_type=F32)
    outgoing = outgoing.astype(BF16).reshape(expert_total, capacity, col_share)
    arrived = lax.all_to_all(outgoing, "expert", split_axis=0, concat_axis=0, tiled=True)
    rows = lax.all_gather(arrived, "pipe", axis=2, tiled=True)
    gate_part = jnp.einsum("gsd,df->gsf", rows, w_gate[0], preferred_element_type=F32)
    up_part = jnp.einsum("gsd,df->gsf", rows, w_up[0], preferred_element_type=F32)
    hidden = (jax.nn.silu(gate_part) * up_part).astype(BF16)
    down_blocks = w_down[0].reshape(hidden_width, pipe_count, col_share)
    block_term = jnp.einsum("gsf,fke->kgse", hidden, down_blocks, preferred_element_type=F32)
    block_term = lax.optimization_barrier(block_term.astype(BF16))
    section = lax.psum_scatter(block_term, "pipe", scatter_dimension=0, tiled=True)
    summed = section.reshape(expert_total, capacity, col_share)
    returned = lax.all_to_all(summed, "expert", split_axis=0, concat_axis=0, tiled=True)
    mixing = (target[:, None] == column_ids[None, :]).astype(F32) * route_weights.reshape(-1)[:, None]
    mixing = mixing.reshape(tok_rows, 2, expert_total * capacity).sum(axis=1)
    mixed = jnp.dot(
        mixing,
        returned.reshape(expert_total * capacity, col_share).astype(F32),
        precision=lax.Precision.HIGHEST,
    )
    return mixed.astype(BF16)


def load_all(pairs, sems):
    copies = [pltpu.make_async_copy(a, b, sems.at[i]) for i, (a, b) in enumerate(pairs)]
    for copy in copies:
        copy.start()
    return copies


def wait_all(copies):
    for copy in copies:
        copy.wait()


def put_packed(out_ref, values):
    height = values.shape[0]
    for b in range(values.shape[1] // 128):
        out_ref[b * height : (b + 1) * height, :] = values[:, b * 128 : (b + 1) * 128]


def take_packed(ref, height):
    blocks = ref.shape[0] // height
    return jnp.concatenate([ref[b * height : (b + 1) * height, :] for b in range(blocks)], axis=1)


def cols_of(w_ref, share, width):
    lead = (0,) if len(w_ref.shape) == 3 else ()
    return w_ref.at[(*lead, slice(None), pl.ds(pl.multiple_of(share * width, width), width))]


def ranks(routes_t, experts):
    tok_rows = routes_t.shape[1]
    named = (routes_t[0:1, :] == experts) | (routes_t[1:2, :] == experts)
    named = named.astype(F32)
    earlier = lax.broadcasted_iota(jnp.int32, (tok_rows, tok_rows), 0)
    later = lax.broadcasted_iota(jnp.int32, (tok_rows, tok_rows), 1)
    before = (earlier < later).astype(BF16)
    count = jnp.dot(named.astype(BF16), before, preferred_element_type=F32)
    return named, count


def expert_rows(count):
    mine = lax.axis_index("expert")
    return jnp.bitwise_xor(lax.broadcasted_iota(jnp.int32, (count, 1), 0), mine)


def pack_kernel(capacity, expert_total, routes_hbm, tokens_hbm, *refs):
    outs = refs[:expert_total]
    routes_ref, own_ref, pick_ref, sems = refs[expert_total:]
    share = lax.axis_index("pipe")
    wait_all(
        load_all(
            [
                (routes_hbm, routes_ref),
                (cols_of(tokens_hbm, share, own_ref.shape[1]), own_ref),
            ],
            sems,
        )
    )
    named, count = ranks(routes_ref[...], expert_rows(max(8, expert_total)))
    padded = pick_ref.shape[0] // expert_total
    slot_ids = lax.broadcasted_iota(jnp.int32, (padded, 1), 0).astype(F32)
    for k in range(expert_total):
        chosen = (count[k : k + 1, :] == slot_ids) & (named[k : k + 1, :] > 0.5)
        pick_ref[k * padded : (k + 1) * padded, :] = chosen.astype(BF16)
    picked = jnp.dot(pick_ref[...], own_ref[...], preferred_element_type=F32).astype(BF16)
    for k in range(expert_total):
        put_packed(outs[k], picked[k * padded : k * padded + capacity, :])


def local_kernel(capacity, expert_total, routes_hbm, weights_hbm, tokens_hbm, up_ref, *refs):
    own_ref, select_ref, scale_ref, vu_ref, routes_ref, weights_ref, tokens_ref, sems = refs
    wait_all(
        load_all(
            [(routes_hbm, routes_ref), (weights_hbm, weights_ref), (tokens_hbm, tokens_ref)], sems
        )
    )
    pieces = sems.shape[0] - 3
    height = vu_ref.shape[1] // pieces
    part = [pl.ds(i * height, height) for i in range(pieces)]
    loads = load_all([(up_ref.at[0, p, :], vu_ref.at[0, p, :]) for p in part], sems.at[pl.ds(3, pieces)])

    @pl.when(lax.axis_index("pipe") >= 0)
    def _():
        local_work(
            capacity, expert_total, routes_ref, weights_ref, tokens_ref, own_ref, select_ref, scale_ref
        )

    wait_all(loads)


def local_work(
    capacity, expert_total, routes_ref, weights_ref, tokens_ref, own_ref, select_ref, scale_ref
):
    tok_rows = tokens_ref.shape[0]
    routes_t = routes_ref[...]
    experts = expert_rows(max(8, expert_total))
    named, count = ranks(routes_t, experts)
    slot_ids = lax.broadcasted_iota(jnp.int32, (capacity, 1), 0).astype(F32)
    chosen = ((count[0:1, :] == slot_ids) & (named[0:1, :] > 0.5)).astype(BF16)
    own_ref[...] = jnp.dot(chosen, tokens_ref[...], preferred_element_type=F32).astype(BF16)
    line = lax.broadcasted_iota(jnp.int32, (tok_rows, tok_rows), 0)
    lane = lax.broadcasted_iota(jnp.int32, (tok_rows, tok_rows), 1)
    eye = line == lane
    lane_slots = lax.broadcasted_iota(jnp.int32, (1, capacity), 1).astype(F32)

    def column(row):
        return jnp.sum(jnp.where(eye, row, 0.0), axis=1, keepdims=True)

    for c in range(2):
        route = routes_t[c : c + 1, :]
        slot = jnp.sum(jnp.where(route == experts, count, 0.0), axis=0, keepdims=True)
        slot_col = column(slot)
        route_col = column(jnp.bitwise_xor(route, lax.axis_index("expert")).astype(F32))
        scale_ref[c * tok_rows : (c + 1) * tok_rows, :] = jnp.broadcast_to(
            column(weights_ref[c : c + 1, :]), (tok_rows, scale_ref.shape[1])
        )
        for k in range(expert_total):
            hit = (slot_col == lane_slots) & (route_col == float(k))
            select_ref[k, c * tok_rows : (c + 1) * tok_rows, :] = hit.astype(BF16)


def join_kernel(j, capacity, own_ref, *refs):
    parts, out_ref = refs[:-1], refs[-1]
    width = out_ref.shape[1]
    share = jnp.bitwise_xor(lax.axis_index("pipe"), j)
    out_ref[0:capacity, :] = own_ref[:, pl.ds(pl.multiple_of(share * width, width), width)]
    for i, part in enumerate(parts):
        out_ref[(i + 1) * capacity : (i + 2) * capacity, :] = take_packed(part, capacity)


def gate_up_kernel(j, take, step, first, last, x_ref, vg_ref, vu_ref, down_ref, *refs):
    sums_in = () if first else refs[:2]
    outs = refs[len(sums_in) :]
    vd_ref, sems = outs[-2], outs[-1]
    index = lax.axis_index("pipe")
    loads = load_all(
        [(cols_of(down_ref, jnp.bitwise_xor(index, take), vd_ref.shape[1]), vd_ref)], sems
    )
    width, height = vg_ref.shape[-1], x_ref.shape[1]
    rows = pl.ds(pl.multiple_of(jnp.bitwise_xor(index, j) * height, height), height)

    @pl.when(index >= 0)
    def _():
        for f in range(0, width, step):
            gate = jnp.dot(x_ref[...], vg_ref[0, rows, f : f + step], preferred_element_type=F32)
            up = jnp.dot(x_ref[...], vu_ref[0, rows, f : f + step], preferred_element_type=F32)
            if not first:
                gate += sums_in[0][:, f : f + step]
                up += sums_in[1][:, f : f + step]
            if last:
                outs[0][:, f : f + step] = (gate / (1.0 + jnp.exp(-gate)) * up).astype(BF16)
            else:
                outs[0][:, f : f + step] = gate
                outs[1][:, f : f + step] = up

    wait_all(loads)


def down_kernel(count, hidden_ref, *refs):
    for vd_ref, out_ref in zip(refs[:count], refs[count:]):
        term = jnp.dot(hidden_ref[...], vd_ref[...], preferred_element_type=F32)
        out_ref[...] = term.astype(out_ref.dtype)


def pair_kernel(capacity, mine_ref, other_ref, *outs):
    for k, out_ref in enumerate(outs):
        rows = slice(k * capacity, (k + 1) * capacity)
        total = mine_ref[rows, :] + other_ref[rows, :].astype(F32)
        put_packed(out_ref, total.astype(BF16))


def down_pair_kernel(capacity, hidden_ref, vd_ref, other_ref, *outs):
    term = jnp.dot(hidden_ref[...], vd_ref[...], preferred_element_type=F32)
    total = term + other_ref[...].astype(F32)
    for k, out_ref in enumerate(outs):
        put_packed(out_ref, total[k * capacity : (k + 1) * capacity, :])


def final_kernel(mine_ref, other_ref, out_ref):
    out_ref[...] = (mine_ref[...] + other_ref[...].astype(F32)).astype(BF16)


def mix_kernel(capacity, select_ref, scale_ref, *refs):
    parts, out_ref = refs[:-1], refs[-1]
    total = None
    for k, part in enumerate(parts):
        term = jnp.dot(select_ref[k], take_packed(part, capacity), preferred_element_type=F32)
        total = term if total is None else total + term
    tok_rows = out_ref.shape[0]
    first = total[:tok_rows, :] * scale_ref[:tok_rows, 0:1]
    second = total[tok_rows:, :] * scale_ref[tok_rows:, 0:1]
    out_ref[...] = (first + second).astype(BF16)


def call(kernel, outs, args, specs, *, scratch=(), mib, flops=0, nbytes=0, aliases=None):
    return pl.pallas_call(
        kernel,
        out_shape=outs,
        in_specs=specs,
        out_specs=[VMEM] * len(outs),
        scratch_shapes=scratch,
        input_output_aliases=aliases or {},
        compiler_params=pltpu.CompilerParams(vmem_limit_bytes=int(mib * MIB)),
        cost_estimate=pl.CostEstimate(flops=int(flops), bytes_accessed=int(nbytes), transcendentals=0),
    )(*args)


def on_device(tokens, routes, route_weights, w_gate, w_up, w_down):
    expert_total = lax.axis_size("expert")
    pipe_count = lax.axis_size("pipe")
    hidden_width = w_gate.shape[2]
    tok_rows, model_width = tokens.shape
    capacity = capacity_of(tok_rows, expert_total, lax.axis_size("dp"))
    col = model_width // pipe_count
    rows = expert_total * capacity
    piece = col * hidden_width * 2
    dma = pltpu.SemaphoreType.DMA
    others = range(1, expert_total)

    def send(v, axis, shift):
        return lax.ppermute(v, axis, [(i, i ^ shift) for i in range(lax.axis_size(axis))])

    def array(shape, dtype=BF16):
        return jax.ShapeDtypeStruct(shape, dtype)

    def in_hbm(v):
        return pltpu.with_memory_space_constraint(v, pltpu.HBM)

    packed_shape = (capacity * col // 128, 128)
    tall = pltpu.VMEM((hidden_width, col), BF16)

    routes_t = routes.T
    padded = (capacity + 15) // 16 * 16
    packed = call(
        functools.partial(pack_kernel, capacity, expert_total),
        [array(packed_shape)] * expert_total,
        (in_hbm(routes_t), in_hbm(tokens)),
        [HBM, HBM],
        scratch=[
            pltpu.VMEM((2, tok_rows), jnp.int32),
            pltpu.VMEM((tok_rows, col), BF16),
            pltpu.VMEM((expert_total * padded, tok_rows), BF16),
            dma((2,)),
        ],
        mib=4,
        flops=2 * rows * tok_rows * col,
        nbytes=PACK_COST,
    )
    order = sorted(others, reverse=True)
    arrived = {k: send(packed[k], "expert", k) for k in order}

    own_rows, select, scale, vu = call(
        functools.partial(local_kernel, capacity, expert_total),
        [
            array((capacity, model_width)),
            array((expert_total, 2 * tok_rows, capacity)),
            array((2 * tok_rows, 128), F32),
            pltpu.VMEM(w_up.shape, BF16),
        ],
        (in_hbm(routes_t), in_hbm(route_weights.T), in_hbm(tokens), in_hbm(w_up)),
        [HBM, HBM, HBM, HBM],
        scratch=[
            pltpu.VMEM((2, tok_rows), jnp.int32),
            pltpu.VMEM((2, tok_rows), F32),
            pltpu.VMEM((tok_rows, model_width), BF16),
            dma((3 + pipe_count,)),
        ],
        mib=4,
        flops=2 * rows * tok_rows * model_width,
        nbytes=LOCAL_COST,
    )
    vg = pltpu.with_memory_space_constraint(w_gate, pltpu.VMEM)

    def join(j, parts):
        (out,) = call(
            functools.partial(join_kernel, j, capacity),
            [array((rows, col))],
            (own_rows, *[parts[k] for k in others]),
            [VMEM] * expert_total,
            mib=2,
            nbytes=2 * rows * col,
        )
        return out

    crossed = {k: send(arrived[k], "pipe", 2) for k in order}
    x0 = join(0, arrived)
    x1 = send(x0, "pipe", 1)
    x2 = join(2, crossed)
    x3 = send(x2, "pipe", 1)

    sums = ()
    vd = {}
    total = pltpu.VMEM((rows, hidden_width), F32)
    for j, x in enumerate((x0, x1, x2, x3)):
        first, last = j == 0, j == pipe_count - 1
        take = pipe_count - 1 - j
        outs = [pltpu.VMEM((rows, hidden_width), BF16)] if last else [total, total]
        *sums, vd[take] = call(
            functools.partial(gate_up_kernel, j, take, min(256, hidden_width), first, last),
            outs + [tall],
            (x, vg, vu, in_hbm(w_down), *sums),
            [VMEM, VMEM, VMEM, HBM] + [VMEM] * len(sums),
            scratch=[dma((1,))],
            mib=6,
            flops=4 * rows * col * hidden_width,
            nbytes=piece,
            aliases={} if first or last else {4: 0, 5: 1},
        )
    (hidden,) = sums

    def down(picks, dtypes):
        return call(
            functools.partial(down_kernel, len(picks)),
            [array((rows, col), d) for d in dtypes],
            (hidden, *[vd[j] for j in picks]),
            [VMEM] * (1 + len(picks)),
            mib=4,
            flops=2 * rows * col * hidden_width * len(picks),
            nbytes=piece,
        )

    (far_other,) = down((3,), (BF16,))
    far_in = send(far_other, "pipe", 1)
    far_mine, near_other = down((2, 1), (F32, BF16))
    near_in = send(near_other, "pipe", 1)
    halves = call(
        functools.partial(pair_kernel, capacity),
        [array(packed_shape)] * expert_total,
        (far_mine, far_in),
        [VMEM, VMEM],
        mib=4,
        nbytes=8 * rows * col,
    )
    back_order = order + [0]
    half_in = {k: send(halves[k], "pipe", 2) for k in back_order}
    mine = call(
        functools.partial(down_pair_kernel, capacity),
        [array(packed_shape, F32)] * expert_total,
        (hidden, vd[0], near_in),
        [VMEM] * 3,
        mib=4,
        flops=2 * rows * col * hidden_width,
        nbytes=piece,
    )
    home = {}
    for k in back_order:
        (done,) = call(
            final_kernel,
            [array(packed_shape)],
            (mine[k], half_in[k]),
            [VMEM, VMEM],
            mib=2,
            nbytes=8 * capacity * col,
        )
        home[k] = send(done, "expert", k) if k else done
    (mixed,) = call(
        functools.partial(mix_kernel, capacity),
        [array((tok_rows, col))],
        (select, scale, *[home[k] for k in range(expert_total)]),
        [VMEM] * (2 + expert_total),
        mib=4,
        flops=4 * rows * tok_rows * col,
        nbytes=2 * rows * col,
    )
    return mixed


def solution(mesh):
    experts = mesh.shape["expert"]

    def body(tokens, routes, route_weights, w_gate, w_up, w_down):
        col = tokens.shape[1] // mesh.shape["pipe"]
        fits = (
            mesh.shape["pipe"] == 4
            and experts & (experts - 1) == 0
            and w_gate.shape[0] == 1
            and col % 128 == 0
            and w_gate.shape[2] % 128 == 0
        )
        step = on_device if fits else on_any_mesh
        return step(tokens, routes, route_weights, w_gate, w_up, w_down)

    return jax.shard_map(
        body,
        mesh=mesh,
        in_specs=(
            P(("dp", "expert"), None),
            P(("dp", "expert"), None),
            P(("dp", "expert"), None),
            P("expert", None, "pipe"),
            P("expert", None, "pipe"),
            P("expert", "pipe", None),
        ),
        out_specs=P(("dp", "expert"), "pipe"),
        check_vma=False,
    )
```

time: 62 us -> 50.7 us (0.82)
  local copies, waits for them, and re-layouts: 19.7 us -> 0.01 us
  Pallas kernels: 16.4 us -> 20.4 us
  waiting for transfers between devices: 5.19 us -> 8.51 us
  starting transfers between devices: 20.1 us -> 21.3 us
    unnamed x30 -> x2, local copies, waits for them, and re-layouts: 18.8 us -> 0.01 us
    pallas_call x20 -> x17, Pallas kernels: 16.4 us -> 20.4 us  [call(): pl.pallas_call(kernel, out_shape=outs, in_specs=specs, out_specs=[VMEM] *...]
    ppermute x17, waiting for transfers between devices: 5.19 us -> 8.51 us  [send(): lax.ppermute(v, axis, [(i, i ^ shift) for i in range(lax.axis_size(axis))])]
    ppermute x17, starting transfers between devices: 20.1 us -> 21.3 us  [send(): lax.ppermute(v, axis, [(i, i ^ shift) for i in range(lax.axis_size(axis))])]
    dynamic_slice x1 -> x0, local copies, waits for them, and re-layouts: 0.92 us -> none  [on_device(): own = lax.dynamic_slice_in_dim(tokens, lax.axis_index('pipe') * col, col, 1)]
  transfers between devices with their start and end apart: 17 -> 17, of which waited for: 5 -> 8; matrix products, arithmetic and copies ran while one was open for 0% -> 0% of each run, Pallas kernels for 18% -> 29%
where the time goes in v2:
time: 50.7 us; the launch traced here: 50.4 us
  starting transfers between devices  21.3 us (42%)
  Pallas kernels  20.4 us (40%)
  waiting for transfers between devices  8.51 us (17%)
    ppermute x17, starting transfers between devices, send(): lax.ppermute(v, axis, [(i, i ^ shift) for i in range(lax.axis_size(axis))])  21.3 us
    pallas_call x17, Pallas kernels, call(): pl.pallas_call(kernel, out_shape=outs, in_specs=specs, out_specs=[VMEM] *...  20.4 us
    ppermute x17, waiting for transfers between devices, send(): lax.ppermute(v, axis, [(i, i ^ shift) for i in range(lax.axis_size(axis))])  8.51 us
  transfers between devices with their start and end apart: 17, of which 8 were waited for; matrix products, arithmetic and copies ran while one was open for 0% of the time, Pallas kernels for 29%

profile of v2, /device:TPU:0, one launch (start us, length us, event | category | flops | bytes accessed | tf_op | source)
XLA Modules:
  0.0 50.4 jit_solution(17069948730653656597)
XLA Ops:
  0.0 1.9 %shard_map.65 = (bf16[300,128]{1,0:T(8,128)(2,1)}, bf16[300,128]{1,0:T(8,128)(2,1)S(1)}, bf16[300,128]{1,0:T(8,128)(2,1)S(1)}, bf16[300,128]{1,0:T(8,128)(2,1)S(1)}) custom-call(s32[2,96]{1,0:T(2,128)} %bitcast.2, bf16[96,3072]{1,0:T(8,128)(2,1)} %tokens_hbm.3), custom_call_target="tpu_custom_call" | custom-call | flops 29491200 | tf_op jit(solution)/shard_map/pallas_call | solution.py:262
  1.9 3.1 %collective-permute-start = (bf16[300,128]{1,0:T(8,128)(2,1)S(1)}, bf16[300,128]{1,0:T(8,128)(2,1)S(1)}, u32[]{:S(2)}, u32[]{:S(2)}) collective-permute-start(bf16[300,128]{1,0:T(8,128)(2,1)S(1)} %get-tuple-element.36), channel_id=1, source_target_pairs={{0,1},{1,0},{2,3},{3,2},{4,5},{5,4},{6,7},{7,6},{8,9},{9,8},{10,11... | collective-permute-start | bytes 230408 | tf_op jit(solution)/shard_map/ppermute | solution.py:287
  5.0 2.6 %collective-permute-start.2 = (bf16[300,128]{1,0:T(8,128)(2,1)S(1)}, bf16[300,128]{1,0:T(8,128)(2,1)S(1)}, u32[]{:S(2)}, u32[]{:S(2)}) collective-permute-start(bf16[300,128]{1,0:T(8,128)(2,1)S(1)} %get-tuple-element.37), channel_id=1, source_target_pairs={{0,2},{1,3},{2,0},{3,1},{4,6},{5,7},{6,4},{7,5},{8,10},{9,11},{10,... | collective-permute-start | bytes 230408 | tf_op jit(solution)/shard_map/ppermute | solution.py:287
  7.6 6.2 %shard_map.64 = (bf16[50,3072]{1,0:T(8,128)(2,1)S(1)}, bf16[4,192,50]{2,1,0:T(8,128)(2,1)S(1)}, f32[192,128]{1,0:T(8,128)S(1)}, bf16[1,3072,2048]{2,1,0:T(8,128)(2,1)S(1)}) custom-call(s32[2,96]{1,0:T(2,128)} %bitcast.3, f32[2,96]{1,0:T(2,128)} %bitcast.4, bf16[96,3072]{1,0:T(8,128)(2,1)} %tokens_hbm.3, bf16[1,3072,2048]{2,1,0:T(8,128)(2,1)} %up_ref.1), custom_call_target="tpu_custom_call" | custom-call | flops 117964800 | bytes 12582912 | tf_op jit(solution)/shard_map/pallas_call | solution.py:262
  13.8 0.1 collective-permute-done.4.refs_2_
  14.1 1.7 %collective-permute-start.1 = (bf16[300,128]{1,0:T(8,128)(2,1)S(1)}, bf16[300,128]{1,0:T(8,128)(2,1)S(1)}, u32[]{:S(2)}, u32[]{:S(2)}) collective-permute-start(bf16[300,128]{1,0:T(8,128)(2,1)S(1)} %collective-permute-done.refs_0_), channel_id=1, source_target_pairs={{0,8},{4,12},{8,0},{12,4},{1,9},{5,13},{9,1},{13,5},{2,10},{6,14},... | collective-permute-start | bytes 230408 | tf_op jit(solution)/shard_map/ppermute | solution.py:287
  15.8 0.4 collective-permute-start.3
  16.2 1.6 %collective-permute-start.5 = (bf16[300,128]{1,0:T(8,128)(2,1)S(1)}, bf16[300,128]{1,0:T(8,128)(2,1)S(1)}, u32[]{:S(2)}, u32[]{:S(2)}) collective-permute-start(bf16[300,128]{1,0:T(8,128)(2,1)S(1)} %collective-permute-done.4.refs_2_), channel_id=1, source_target_pairs={{0,8},{4,12},{8,0},{12,4},{1,9},{5,13},{9,1},{13,5},{2,10},{6,14},... | collective-permute-start | bytes 230408 | tf_op jit(solution)/shard_map/ppermute | solution.py:287
  17.8 1.3 %collective-permute-done.1.refs_0_ = bf16[300,128]{1,0:T(8,128)(2,1)S(1)} collective-permute-done((bf16[300,128]{1,0:T(8,128)(2,1)S(1)}, bf16[300,128]{1,0:T(8,128)(2,1)S(1)}, u32[]{:S(2)}, u32[]{:S(2)}) %collective-permute-start.1) | collective-permute-done | bytes 76832 | tf_op jit(solution)/shard_map/ppermute | solution.py:287
  19.1 1.9 %collective-permute-done.3.refs_1_ = bf16[300,128]{1,0:T(8,128)(2,1)S(1)} collective-permute-done((bf16[300,128]{1,0:T(8,128)(2,1)S(1)}, bf16[300,128]{1,0:T(8,128)(2,1)S(1)}, u32[]{:S(2)}, u32[]{:S(2)}) %collective-permute-start.3) | collective-permute-done | bytes 76832 | tf_op jit(solution)/shard_map/ppermute | solution.py:287
  21.0 1.2 %collective-permute-done.5.refs_2_ = bf16[300,128]{1,0:T(8,128)(2,1)S(1)} collective-permute-done((bf16[300,128]{1,0:T(8,128)(2,1)S(1)}, bf16[300,128]{1,0:T(8,128)(2,1)S(1)}, u32[]{:S(2)}, u32[]{:S(2)}) %collective-permute-start.5) | collective-permute-done | bytes 76832 | tf_op jit(solution)/shard_map/ppermute | solution.py:287
  22.3 1.9 %shard_map.68 = (f32[200,2048]{1,0:T(8,128)S(1)}, f32[200,2048]{1,0:T(8,128)S(1)}, bf16[2048,768]{1,0:T(8,128)(2,1)S(1)}) custom-call(bf16[200,768]{1,0:T(8,128)(2,1)S(1)} %shard_map.67.x_ref, bf16[1,3072,2048]{2,1,0:T(8,128)(2,1)S(1)} %copy-done, bf16[1,3072,2048]{2,1,0:T(8,128)(2,1)S(1)} %get-tuple-element.39.vu_ref, bf16[1,2048,3072]{2,1,0:T(8,128)(2,1)} %down_ref.7), custom_call_target="tpu_custom_call" | custom-call | flops 1258291200 | bytes 3145728 | tf_op jit(solution)/shard_map/pallas_call | solution.py:262
  24.2 1.9 %shard_map.69 = (f32[200,2048]{1,0:T(8,128)S(1)}, f32[200,2048]{1,0:T(8,128)S(1)}, bf16[2048,768]{1,0:T(8,128)(2,1)S(1)}) custom-call(bf16[200,768]{1,0:T(8,128)(2,1)S(1)} %collective-permute-done.7.x_ref, bf16[1,3072,2048]{2,1,0:T(8,128)(2,1)S(1)} %copy-done, ...), custom_call_target="tpu_custom_call", output_to_operand_aliasing={{0}: (4, {}), {1}: (5, {})} | custom-call | flops 1258291200 | bytes 3145728 | tf_op jit(solution)/shard_map/pallas_call | solution.py:262
  26.2 1.9 %shard_map.70 = (f32[200,2048]{1,0:T(8,128)S(1)}, f32[200,2048]{1,0:T(8,128)S(1)}, bf16[2048,768]{1,0:T(8,128)(2,1)S(1)}) custom-call(bf16[200,768]{1,0:T(8,128)(2,1)S(1)} %shard_map.66.x_ref, bf16[1,3072,2048]{2,1,0:T(8,128)(2,1)S(1)} %copy-done, bf16[1,3072,2048]{2,1,0:T(8,128)(2,1)S(1)} %get-tuple-element.39.vu_ref, ...), custom_call_target="tpu_custom_call", output_to_operand_aliasing={{0}: (4, {}), {1}: (5, {})} | custom-call | flops 1258291200 | bytes 3145728 | tf_op jit(solution)/shard_map/pallas_call | solution.py:262
  28.1 1.9 %shard_map.71 = (bf16[200,2048]{1,0:T(8,128)(2,1)S(1)}, bf16[2048,768]{1,0:T(8,128)(2,1)S(1)}) custom-call(bf16[200,768]{1,0:T(8,128)(2,1)S(1)} %collective-permute-done.6.x_ref, bf16[1,3072,2048]{2,1,0:T(8,128)(2,1)S(1)} %copy-done, bf16[1,3072,2048]{2,1,0:T(8,128)(2,1)S(1)} %get-tuple-element.39.vu_ref, bf16[1,2048,3072]{2,1,0:T(8,128)(2,1)} %down_ref.7, ...), custom_call_target="tpu_custom_call" | custom-call | flops 1258291200 | bytes 3145728 | tf_op jit(solution)/shard_map/pallas_call | solution.py:262
  30.0 0.8 %shard_map.74 = bf16[200,768]{1,0:T(8,128)(2,1)S(1)} custom-call(bf16[200,2048]{1,0:T(8,128)(2,1)S(1)} %get-tuple-element.46.hidden_ref, bf16[2048,768]{1,0:T(8,128)(2,1)S(1)} %get-tuple-element.53.refs_0_), custom_call_target="tpu_custom_call" | custom-call | flops 629145600 | bytes 3145728 | tf_op jit(solution)/shard_map/pallas_call | solution.py:262
  30.9 0.5 %collective-permute-start.9 = (bf16[200,768]{1,0:T(8,128)(2,1)S(1)}, bf16[200,768]{1,0:T(8,128)(2,1)S(1)}, u32[]{:S(2)}, u32[]{:S(2)}) collective-permute-start(bf16[200,768]{1,0:T(8,128)(2,1)S(1)} %shard_map.74), channel_id=1, source_target_pairs={{0,4},{4,0},{8,12},{12,8},{1,5},{5,1},{9,13},{13,9},{2,6},{6,2},{1... | collective-permute-start | bytes 921608 | tf_op jit(solution)/shard_map/ppermute | solution.py:287
  31.4 1.6 %shard_map.72 = (f32[200,768]{1,0:T(8,128)S(1)}, bf16[200,768]{1,0:T(8,128)(2,1)S(1)}) custom-call(bf16[200,2048]{1,0:T(8,128)(2,1)S(1)} %get-tuple-element.46.hidden_ref, bf16[2048,768]{1,0:T(8,128)(2,1)S(1)} %get-tuple-element.48.refs_0_, bf16[2048,768]{1,0:T(8,128)(2,1)S(1)} %get-tuple-element.49.refs_1_), custom_call_target="tpu_custom_call" | custom-call | flops 1258291200 | bytes 3145728 | tf_op jit(solution)/shard_map/pallas_call | solution.py:262
  33.1 0.1 shard_map.75
  33.2 1.7 %collective-permute-start.11 = (bf16[300,128]{1,0:T(8,128)(2,1)S(1)}, bf16[300,128]{1,0:T(8,128)(2,1)S(1)}, u32[]{:S(2)}, u32[]{:S(2)}) collective-permute-start(bf16[300,128]{1,0:T(8,128)(2,1)S(1)} %get-tuple-element.56), channel_id=1, source_target_pairs={{0,8},{4,12},{8,0},{12,4},{1,9},{5,13},{9,1},{13,5},{2,10},{6,14},... | collective-permute-start | bytes 230408 | tf_op jit(solution)/shard_map/ppermute | solution.py:287
  34.9 0.4 collective-permute-start.13
  35.3 1.6 %collective-permute-start.15 = (bf16[300,128]{1,0:T(8,128)(2,1)S(1)}, bf16[300,128]{1,0:T(8,128)(2,1)S(1)}, u32[]{:S(2)}, u32[]{:S(2)}) collective-permute-start(bf16[300,128]{1,0:T(8,128)(2,1)S(1)} %get-tuple-element.60), channel_id=1, source_target_pairs={{0,8},{4,12},{8,0},{12,4},{1,9},{5,13},{9,1},{13,5},{2,10},{6,14},... | collective-permute-start | bytes 230408 | tf_op jit(solution)/shard_map/ppermute | solution.py:287
  36.9 0.4 collective-permute-start.10
  37.3 0.8 %shard_map.73 = (f32[300,128]{1,0:T(8,128)S(1)}, f32[300,128]{1,0:T(8,128)S(1)}, f32[300,128]{1,0:T(8,128)S(1)}, f32[300,128]{1,0:T(8,128)S(1)}) custom-call(bf16[200,2048]{1,0:T(8,128)(2,1)S(1)} %get-tuple-element.46.hidden_ref, bf16[2048,768]{1,0:T(8,128)(2,1)S(1)} %get-tuple-element.47.vd_ref, bf16[200,768]{1,0:T(8,128)(2,1)S(1)} %collective-permute-done.8.other_ref), custom_call_target="tpu_custom_call" | custom-call | flops 629145600 | bytes 3145728 | tf_op jit(solution)/shard_map/pallas_call | solution.py:262
  38.2 0.1 collective-permute-done.11.other_ref
  38.3 1.6 %collective-permute-start.12 = (bf16[300,128]{1,0:T(8,128)(2,1)S(1)}, bf16[300,128]{1,0:T(8,128)(2,1)S(1)}, u32[]{:S(2)}, u32[]{:S(2)}) collective-permute-start(bf16[300,128]{1,0:T(8,128)(2,1)S(1)} %shard_map.77), channel_id=1, source_target_pairs={{0,1},{1,0},{2,3},{3,2},{4,5},{5,4},{6,7},{7,6},{8,9},{9,8},{10,11... | collective-permute-start | bytes 230408 | tf_op jit(solution)/shard_map/ppermute | solution.py:287
  39.9 0.2 collective-permute-done.13.other_ref
  40.2 2.7 %collective-permute-start.14 = (bf16[300,128]{1,0:T(8,128)(2,1)S(1)}, bf16[300,128]{1,0:T(8,128)(2,1)S(1)}, u32[]{:S(2)}, u32[]{:S(2)}) collective-permute-start(bf16[300,128]{1,0:T(8,128)(2,1)S(1)} %shard_map.78), channel_id=1, source_target_pairs={{0,2},{1,3},{2,0},{3,1},{4,6},{5,7},{6,4},{7,5},{8,10},{9,11},{10,... | collective-permute-start | bytes 230408 | tf_op jit(solution)/shard_map/ppermute | solution.py:287
  42.9 2.7 %collective-permute-start.16 = (bf16[300,128]{1,0:T(8,128)(2,1)S(1)}, bf16[300,128]{1,0:T(8,128)(2,1)S(1)}, u32[]{:S(2)}, u32[]{:S(2)}) collective-permute-start(bf16[300,128]{1,0:T(8,128)(2,1)S(1)} %shard_map.79), channel_id=1, source_target_pairs={{0,3},{1,2},{2,1},{3,0},{4,7},{5,6},{6,5},{7,4},{8,11},{9,10},{10,... | collective-permute-start | bytes 230408 | tf_op jit(solution)/shard_map/ppermute | solution.py:287
  45.6 2.4 %collective-permute-done.14.refs_2_ = bf16[300,128]{1,0:T(8,128)(2,1)S(1)} collective-permute-done((bf16[300,128]{1,0:T(8,128)(2,1)S(1)}, bf16[300,128]{1,0:T(8,128)(2,1)S(1)}, u32[]{:S(2)}, u32[]{:S(2)}) %collective-permute-start.14) | collective-permute-done | bytes 76832 | tf_op jit(solution)/shard_map/ppermute | solution.py:287
  48.0 1.2 %collective-permute-done.16.refs_3_ = bf16[300,128]{1,0:T(8,128)(2,1)S(1)} collective-permute-done((bf16[300,128]{1,0:T(8,128)(2,1)S(1)}, bf16[300,128]{1,0:T(8,128)(2,1)S(1)}, u32[]{:S(2)}, u32[]{:S(2)}) %collective-permute-start.16) | collective-permute-done | bytes 76832 | tf_op jit(solution)/shard_map/ppermute | solution.py:287
  49.3 1.1 %shard_map.80 = bf16[96,768]{1,0:T(8,128)(2,1)} custom-call(bf16[4,192,50]{2,1,0:T(8,128)(2,1)S(1)} %get-tuple-element.33.select_ref, f32[192,128]{1,0:T(8,128)S(1)} %get-tuple-element.34.scale_ref, bf16[300,128]{1,0:T(8,128)(2,1)S(1)} %shard_map.76.refs_0_, bf16[300,128]{1,0:T(8,128)(2,1)S(1)} %collective-permute-done.12.refs_1_, ...), custom_call_target="tpu_custom_call" | custom-call | flops 58982400 | bytes 307200 | tf_op jit(solution)/shard_map/pallas_call | solution.py:262
  (21 shorter events, 0.5 us)
Async XLA Ops:
  1.9 11.9 %collective-permute-start = (bf16[300,128]{1,0:T(8,128)(2,1)S(1)}, bf16[300,128]{1,0:T(8,128)(2,1)S(1)}, u32[]{:S(2)}, u32[]{:S(2)}) collective-permute-start(bf16[300,128]{1,0:T(8,128)(2,1)S(1)} %get-tuple-element.36), channel_id=1, source_target_pairs={{0,1},{1,0},{2,3},{3,2},{4,5},{5,4},{6,7},{7,6},{8,9},{9,8},{10,11... | collective-permute-start | bytes 230408 | tf_op jit(solution)/shard_map/ppermute | solution.py:287
  5.0 8.8 %collective-permute-start.2 = (bf16[300,128]{1,0:T(8,128)(2,1)S(1)}, bf16[300,128]{1,0:T(8,128)(2,1)S(1)}, u32[]{:S(2)}, u32[]{:S(2)}) collective-permute-start(bf16[300,128]{1,0:T(8,128)(2,1)S(1)} %get-tuple-element.37), channel_id=1, source_target_pairs={{0,2},{1,3},{2,0},{3,1},{4,6},{5,7},{6,4},{7,5},{8,10},{9,11},{10,... | collective-permute-start | bytes 230408 | tf_op jit(solution)/shard_map/ppermute | solution.py:287
  7.6 6.3 %collective-permute-start.4 = (bf16[300,128]{1,0:T(8,128)(2,1)S(1)}, bf16[300,128]{1,0:T(8,128)(2,1)S(1)}, u32[]{:S(2)}, u32[]{:S(2)}) collective-permute-start(bf16[300,128]{1,0:T(8,128)(2,1)S(1)} %get-tuple-element.38), channel_id=1, source_target_pairs={{0,3},{1,2},{2,1},{3,0},{4,7},{5,6},{6,5},{7,4},{8,11},{9,10},{10,... | collective-permute-start | bytes 230408 | tf_op jit(solution)/shard_map/ppermute | solution.py:287
  7.6 14.7 %copy-start = (bf16[1,3072,2048]{2,1,0:T(8,128)(2,1)S(1)}, bf16[1,3072,2048]{2,1,0:T(8,128)(2,1)}, u32[]{:S(2)}) copy-start(bf16[1,3072,2048]{2,1,0:T(8,128)(2,1)} %vg_ref.7) | copy-start | bytes 37748740
  14.0 10.2 %collective-permute-start.7 = (bf16[200,768]{1,0:T(8,128)(2,1)S(1)}, bf16[200,768]{1,0:T(8,128)(2,1)S(1)}, u32[]{:S(2)}, u32[]{:S(2)}) collective-permute-start(bf16[200,768]{1,0:T(8,128)(2,1)S(1)} %shard_map.67.x_ref), channel_id=1, source_target_pairs={{0,4},{4,0},{8,12},{12,8},{1,5},{5,1},{9,13},{13,9},{2,6},{6,2},{1... | collective-permute-start | bytes 921608 | tf_op jit(solution)/shard_map/ppermute | solution.py:287
  14.1 5.1 %collective-permute-start.1 = (bf16[300,128]{1,0:T(8,128)(2,1)S(1)}, bf16[300,128]{1,0:T(8,128)(2,1)S(1)}, u32[]{:S(2)}, u32[]{:S(2)}) collective-permute-start(bf16[300,128]{1,0:T(8,128)(2,1)S(1)} %collective-permute-done.refs_0_), channel_id=1, source_target_pairs={{0,8},{4,12},{8,0},{12,4},{1,9},{5,13},{9,1},{13,5},{2,10},{6,14},... | collective-permute-start | bytes 230408 | tf_op jit(solution)/shard_map/ppermute | solution.py:287
  15.8 5.2 %collective-permute-start.3 = (bf16[300,128]{1,0:T(8,128)(2,1)S(1)}, bf16[300,128]{1,0:T(8,128)(2,1)S(1)}, u32[]{:S(2)}, u32[]{:S(2)}) collective-permute-start(bf16[300,128]{1,0:T(8,128)(2,1)S(1)} %collective-permute-done.2.refs_1_), channel_id=1, source_target_pairs={{0,8},{4,12},{8,0},{12,4},{1,9},{5,13},{9,1},{13,5},{2,10},{6,14},... | collective-permute-start | bytes 230408 | tf_op jit(solution)/shard_map/ppermute | solution.py:287
  16.2 6.0 %collective-permute-start.5 = (bf16[300,128]{1,0:T(8,128)(2,1)S(1)}, bf16[300,128]{1,0:T(8,128)(2,1)S(1)}, u32[]{:S(2)}, u32[]{:S(2)}) collective-permute-start(bf16[300,128]{1,0:T(8,128)(2,1)S(1)} %collective-permute-done.4.refs_2_), channel_id=1, source_target_pairs={{0,8},{4,12},{8,0},{12,4},{1,9},{5,13},{9,1},{13,5},{2,10},{6,14},... | collective-permute-start | bytes 230408 | tf_op jit(solution)/shard_map/ppermute | solution.py:287
  22.2 5.9 %collective-permute-start.6 = (bf16[200,768]{1,0:T(8,128)(2,1)S(1)}, bf16[200,768]{1,0:T(8,128)(2,1)S(1)}, u32[]{:S(2)}, u32[]{:S(2)}) collective-permute-start(bf16[200,768]{1,0:T(8,128)(2,1)S(1)} %shard_map.66.x_ref), channel_id=1, source_target_pairs={{0,4},{4,0},{8,12},{12,8},{1,5},{5,1},{9,13},{13,9},{2,6},{6,2},{1... | collective-permute-start | bytes 921608 | tf_op jit(solution)/shard_map/ppermute | solution.py:287
  30.9 2.2 %collective-permute-start.9 = (bf16[200,768]{1,0:T(8,128)(2,1)S(1)}, bf16[200,768]{1,0:T(8,128)(2,1)S(1)}, u32[]{:S(2)}, u32[]{:S(2)}) collective-permute-start(bf16[200,768]{1,0:T(8,128)(2,1)S(1)} %shard_map.74), channel_id=1, source_target_pairs={{0,4},{4,0},{8,12},{12,8},{1,5},{5,1},{9,13},{13,9},{2,6},{6,2},{1... | collective-permute-start | bytes 921608 | tf_op jit(solution)/shard_map/ppermute | solution.py:287
  32.9 4.4 %collective-permute-start.8 = (bf16[200,768]{1,0:T(8,128)(2,1)S(1)}, bf16[200,768]{1,0:T(8,128)(2,1)S(1)}, u32[]{:S(2)}, u32[]{:S(2)}) collective-permute-start(bf16[200,768]{1,0:T(8,128)(2,1)S(1)} %get-tuple-element.50), channel_id=1, source_target_pairs={{0,4},{4,0},{8,12},{12,8},{1,5},{5,1},{9,13},{13,9},{2,6},{6,2},{1... | collective-permute-start | bytes 921608 | tf_op jit(solution)/shard_map/ppermute | solution.py:287
  33.2 5.1 %collective-permute-start.11 = (bf16[300,128]{1,0:T(8,128)(2,1)S(1)}, bf16[300,128]{1,0:T(8,128)(2,1)S(1)}, u32[]{:S(2)}, u32[]{:S(2)}) collective-permute-start(bf16[300,128]{1,0:T(8,128)(2,1)S(1)} %get-tuple-element.56), channel_id=1, source_target_pairs={{0,8},{4,12},{8,0},{12,4},{1,9},{5,13},{9,1},{13,5},{2,10},{6,14},... | collective-permute-start | bytes 230408 | tf_op jit(solution)/shard_map/ppermute | solution.py:287
  34.9 5.2 %collective-permute-start.13 = (bf16[300,128]{1,0:T(8,128)(2,1)S(1)}, bf16[300,128]{1,0:T(8,128)(2,1)S(1)}, u32[]{:S(2)}, u32[]{:S(2)}) collective-permute-start(bf16[300,128]{1,0:T(8,128)(2,1)S(1)} %get-tuple-element.58), channel_id=1, source_target_pairs={{0,8},{4,12},{8,0},{12,4},{1,9},{5,13},{9,1},{13,5},{2,10},{6,14},... | collective-permute-start | bytes 230408 | tf_op jit(solution)/shard_map/ppermute | solution.py:287
  35.3 7.6 %collective-permute-start.15 = (bf16[300,128]{1,0:T(8,128)(2,1)S(1)}, bf16[300,128]{1,0:T(8,128)(2,1)S(1)}, u32[]{:S(2)}, u32[]{:S(2)}) collective-permute-start(bf16[300,128]{1,0:T(8,128)(2,1)S(1)} %get-tuple-element.60), channel_id=1, source_target_pairs={{0,8},{4,12},{8,0},{12,4},{1,9},{5,13},{9,1},{13,5},{2,10},{6,14},... | collective-permute-start | bytes 230408 | tf_op jit(solution)/shard_map/ppermute | solution.py:287
  36.9 8.7 %collective-permute-start.10 = (bf16[300,128]{1,0:T(8,128)(2,1)S(1)}, bf16[300,128]{1,0:T(8,128)(2,1)S(1)}, u32[]{:S(2)}, u32[]{:S(2)}) collective-permute-start(bf16[300,128]{1,0:T(8,128)(2,1)S(1)} %get-tuple-element.54), channel_id=1, source_target_pairs={{0,8},{4,12},{8,0},{12,4},{1,9},{5,13},{9,1},{13,5},{2,10},{6,14},... | collective-permute-start | bytes 230408 | tf_op jit(solution)/shard_map/ppermute | solution.py:287
  38.3 7.3 %collective-permute-start.12 = (bf16[300,128]{1,0:T(8,128)(2,1)S(1)}, bf16[300,128]{1,0:T(8,128)(2,1)S(1)}, u32[]{:S(2)}, u32[]{:S(2)}) collective-permute-start(bf16[300,128]{1,0:T(8,128)(2,1)S(1)} %shard_map.77), channel_id=1, source_target_pairs={{0,1},{1,0},{2,3},{3,2},{4,5},{5,4},{6,7},{7,6},{8,9},{9,8},{10,11... | collective-permute-start | bytes 230408 | tf_op jit(solution)/shard_map/ppermute | solution.py:287
  40.2 7.9 %collective-permute-start.14 = (bf16[300,128]{1,0:T(8,128)(2,1)S(1)}, bf16[300,128]{1,0:T(8,128)(2,1)S(1)}, u32[]{:S(2)}, u32[]{:S(2)}) collective-permute-start(bf16[300,128]{1,0:T(8,128)(2,1)S(1)} %shard_map.78), channel_id=1, source_target_pairs={{0,2},{1,3},{2,0},{3,1},{4,6},{5,7},{6,4},{7,5},{8,10},{9,11},{10,... | collective-permute-start | bytes 230408 | tf_op jit(solution)/shard_map/ppermute | solution.py:287
  42.9 6.4 %collective-permute-start.16 = (bf16[300,128]{1,0:T(8,128)(2,1)S(1)}, bf16[300,128]{1,0:T(8,128)(2,1)S(1)}, u32[]{:S(2)}, u32[]{:S(2)}) collective-permute-start(bf16[300,128]{1,0:T(8,128)(2,1)S(1)} %shard_map.79), channel_id=1, source_target_pairs={{0,3},{1,2},{2,1},{3,0},{4,7},{5,6},{6,5},{7,4},{8,11},{9,10},{10,... | collective-permute-start | bytes 230408 | tf_op jit(solution)/shard_map/ppermute | solution.py:287

commit v3 on v2

--- a/solution.py
+++ b/solution.py
@@ -109,43 +109,47 @@
     return jnp.bitwise_xor(lax.broadcasted_iota(jnp.int32, (count, 1), 0), mine)
 
 
+def lead_kernel(mark_ref, *refs):
+    refs[-1][...] = mark_ref[...]
+
+
 def pack_kernel(capacity, expert_total, routes_hbm, tokens_hbm, *refs):
-    outs = refs[:expert_total]
-    routes_ref, own_ref, pick_ref, sems = refs[expert_total:]
+    outs = refs[: expert_total - 1]
+    mark_ref, routes_ref, own_ref, pick_ref, sems = refs[expert_total - 1 :]
     share = lax.axis_index("pipe")
-    wait_all(
-        load_all(
-            [
-                (routes_hbm, routes_ref),
-                (cols_of(tokens_hbm, share, own_ref.shape[1]), own_ref),
-            ],
-            sems,
-        )
-    )
+    routes_load, own_load = load_all(
+        [(routes_hbm, routes_ref), (cols_of(tokens_hbm, share, own_ref.shape[1]), own_ref)], sems
+    )
+    routes_load.wait()
     named, count = ranks(routes_ref[...], expert_rows(max(8, expert_total)))
-    padded = pick_ref.shape[0] // expert_total
+    padded = pick_ref.shape[0] // (expert_total - 1)
     slot_ids = lax.broadcasted_iota(jnp.int32, (padded, 1), 0).astype(F32)
-    for k in range(expert_total):
+    for k in range(1, expert_total):
         chosen = (count[k : k + 1, :] == slot_ids) & (named[k : k + 1, :] > 0.5)
-        pick_ref[k * padded : (k + 1) * padded, :] = chosen.astype(BF16)
+        pick_ref[(k - 1) * padded : k * padded, :] = chosen.astype(BF16)
+    own_load.wait()
     picked = jnp.dot(pick_ref[...], own_ref[...], preferred_element_type=F32).astype(BF16)
-    for k in range(expert_total):
-        put_packed(outs[k], picked[k * padded : k * padded + capacity, :])
-
-
-def local_kernel(capacity, expert_total, routes_hbm, weights_hbm, tokens_hbm, up_ref, *refs):
-    own_ref, select_ref, scale_ref, vu_ref, routes_ref, weights_ref, tokens_ref, sems = refs
-    wait_all(
-        load_all(
-            [(routes_hbm, routes_ref), (weights_hbm, weights_ref), (tokens_hbm, tokens_ref)], sems
-        )
-    )
-    pieces = sems.shape[0] - 3
-    height = vu_ref.shape[1] // pieces
-    part = [pl.ds(i * height, height) for i in range(pieces)]
-    loads = load_all([(up_ref.at[0, p, :], vu_ref.at[0, p, :]) for p in part], sems.at[pl.ds(3, pieces)])
-
-    @pl.when(lax.axis_index("pipe") >= 0)
+    for k, out_ref in enumerate(outs):
+        put_packed(out_ref, picked[k * padded : k * padded + capacity, :])
+    mark_ref[...] = jnp.zeros_like(mark_ref)
+
+
+def local_kernel(capacity, expert_total, takes, routes_hbm, weights_hbm, tokens_hbm, down_ref, mark_ref, *refs):
+    own_ref, select_ref, scale_ref, *vd_refs, routes_ref, weights_ref, tokens_ref, sems = refs
+    small = load_all(
+        [(routes_hbm, routes_ref), (weights_hbm, weights_ref), (tokens_hbm, tokens_ref)], sems
+    )
+    share = lax.axis_index("pipe")
+    loads = load_all(
+        [
+            (cols_of(down_ref, jnp.bitwise_xor(share, take), vd_ref.shape[1]), vd_ref)
+            for take, vd_ref in zip(takes, vd_refs)
+        ],
+        sems.at[pl.ds(len(small), len(takes))],
+    )
+    wait_all(small)
+
+    @pl.when(share >= 0)
     def _():
         local_work(
             capacity, expert_total, routes_ref, weights_ref, tokens_ref, own_ref, select_ref, scale_ref
@@ -194,18 +198,20 @@
         out_ref[(i + 1) * capacity : (i + 2) * capacity, :] = take_packed(part, capacity)
 
 
-def gate_up_kernel(j, take, step, first, last, x_ref, vg_ref, vu_ref, down_ref, *refs):
+def gate_up_kernel(j, take, step, first, last, x_ref, vg_ref, vu_ref, *refs):
     sums_in = () if first else refs[:2]
-    outs = refs[len(sums_in) :]
-    vd_ref, sems = outs[-2], outs[-1]
-    index = lax.axis_index("pipe")
-    loads = load_all(
-        [(cols_of(down_ref, jnp.bitwise_xor(index, take), vd_ref.shape[1]), vd_ref)], sems
-    )
+    refs = refs[len(sums_in) :]
+    share = lax.axis_index("pipe")
+    loads = []
+    if take is not None:
+        down_ref, *refs, vd_ref, sems = refs
+        source = cols_of(down_ref, jnp.bitwise_xor(share, take), vd_ref.shape[1])
+        loads = load_all([(source, vd_ref)], sems)
+    outs = refs
     width, height = vg_ref.shape[-1], x_ref.shape[1]
-    rows = pl.ds(pl.multiple_of(jnp.bitwise_xor(index, j) * height, height), height)
-
-    @pl.when(index >= 0)
+    rows = pl.ds(pl.multiple_of(jnp.bitwise_xor(share, j) * height, height), height)
+
+    @pl.when(share >= 0)
     def _():
         for f in range(0, width, step):
             gate = jnp.dot(x_ref[...], vg_ref[0, rows, f : f + step], preferred_element_type=F32)
@@ -222,10 +228,13 @@
     wait_all(loads)
 
 
+def down_dot(hidden_ref, vd_ref):
+    return jnp.dot(hidden_ref[...], vd_ref[...], preferred_element_type=F32)
+
+
 def down_kernel(count, hidden_ref, *refs):
     for vd_ref, out_ref in zip(refs[:count], refs[count:]):
-        term = jnp.dot(hidden_ref[...], vd_ref[...], preferred_element_type=F32)
-        out_ref[...] = term.astype(out_ref.dtype)
+        out_ref[...] = down_dot(hidden_ref, vd_ref).astype(out_ref.dtype)
 
 
 def pair_kernel(capacity, mine_ref, other_ref, *outs):
@@ -236,8 +245,7 @@
 
 
 def down_pair_kernel(capacity, hidden_ref, vd_ref, other_ref, *outs):
-    term = jnp.dot(hidden_ref[...], vd_ref[...], preferred_element_type=F32)
-    total = term + other_ref[...].astype(F32)
+    total = down_dot(hidden_ref, vd_ref) + other_ref[...].astype(F32)
     for k, out_ref in enumerate(outs):
         put_packed(out_ref, total[k * capacity : (k + 1) * capacity, :])
 
@@ -293,49 +301,58 @@
         return pltpu.with_memory_space_constraint(v, pltpu.HBM)
 
     packed_shape = (capacity * col // 128, 128)
+
     tall = pltpu.VMEM((hidden_width, col), BF16)
-
     routes_t = routes.T
     padded = (capacity + 15) // 16 * 16
-    packed = call(
+    *packed, mark = call(
         functools.partial(pack_kernel, capacity, expert_total),
-        [array(packed_shape)] * expert_total,
+        [array(packed_shape)] * (expert_total - 1) + [array((8, 128), F32)],
         (in_hbm(routes_t), in_hbm(tokens)),
         [HBM, HBM],
         scratch=[
             pltpu.VMEM((2, tok_rows), jnp.int32),
             pltpu.VMEM((tok_rows, col), BF16),
-            pltpu.VMEM((expert_total * padded, tok_rows), BF16),
+            pltpu.VMEM(((expert_total - 1) * padded, tok_rows), BF16),
             dma((2,)),
         ],
         mib=4,
         flops=2 * rows * tok_rows * col,
         nbytes=PACK_COST,
     )
+    (mark,) = call(
+        lead_kernel,
+        [array((8, 128), F32)],
+        (mark, in_hbm(w_gate), in_hbm(w_up)),
+        [VMEM, HBM, HBM],
+        mib=1,
+    )
     order = sorted(others, reverse=True)
-    arrived = {k: send(packed[k], "expert", k) for k in order}
-
-    own_rows, select, scale, vu = call(
-        functools.partial(local_kernel, capacity, expert_total),
+    arrived = {k: send(packed[k - 1], "expert", k) for k in order}
+
+    takes = (3, 2)
+    own_rows, select, scale, *fetched = call(
+        functools.partial(local_kernel, capacity, expert_total, takes),
         [
             array((capacity, model_width)),
             array((expert_total, 2 * tok_rows, capacity)),
             array((2 * tok_rows, 128), F32),
-            pltpu.VMEM(w_up.shape, BF16),
+            *[tall for _ in takes],
         ],
-        (in_hbm(routes_t), in_hbm(route_weights.T), in_hbm(tokens), in_hbm(w_up)),
-        [HBM, HBM, HBM, HBM],
+        (in_hbm(routes_t), in_hbm(route_weights.T), in_hbm(tokens), in_hbm(w_down), mark),
+        [HBM, HBM, HBM, HBM, VMEM],
         scratch=[
             pltpu.VMEM((2, tok_rows), jnp.int32),
             pltpu.VMEM((2, tok_rows), F32),
             pltpu.VMEM((tok_rows, model_width), BF16),
-            dma((3 + pipe_count,)),
+            dma((3 + len(takes),)),
         ],
         mib=4,
         flops=2 * rows * tok_rows * model_width,
         nbytes=LOCAL_COST,
     )
     vg = pltpu.with_memory_space_constraint(w_gate, pltpu.VMEM)
+    vu = pltpu.with_memory_space_constraint(w_up, pltpu.VMEM)
 
     def join(j, parts):
         (out,) = call(
@@ -355,23 +372,26 @@
     x3 = send(x2, "pipe", 1)
 
     sums = ()
-    vd = {}
+    vd = dict(zip(takes, fetched))
     total = pltpu.VMEM((rows, hidden_width), F32)
     for j, x in enumerate((x0, x1, x2, x3)):
         first, last = j == 0, j == pipe_count - 1
-        take = pipe_count - 1 - j
-        outs = [pltpu.VMEM((rows, hidden_width), BF16)] if last else [total, total]
-        *sums, vd[take] = call(
+        take = {0: 1, 1: 0}.get(j)
+        fetch = take is not None
+        outs = call(
             functools.partial(gate_up_kernel, j, take, min(256, hidden_width), first, last),
-            outs + [tall],
-            (x, vg, vu, in_hbm(w_down), *sums),
-            [VMEM, VMEM, VMEM, HBM] + [VMEM] * len(sums),
-            scratch=[dma((1,))],
+            ([pltpu.VMEM((rows, hidden_width), BF16)] if last else [total, total]) + [tall] * fetch,
+            (x, vg, vu, *sums) + (in_hbm(w_down),) * fetch,
+            [VMEM] * (3 + len(sums)) + [HBM] * fetch,
+            scratch=[dma((1,))] * fetch,
             mib=6,
             flops=4 * rows * col * hidden_width,
-            nbytes=piece,
-            aliases={} if first or last else {4: 0, 5: 1},
-        )
+            nbytes=2 * piece,
+            aliases={} if first or last else {3: 0, 4: 1},
+        )
+        if fetch:
+            vd[take] = outs.pop() if isinstance(outs, list) else outs[-1]
+        sums = tuple(outs[: 1 if last else 2])
     (hidden,) = sums
 
     def down(picks, dtypes):
@@ -397,7 +417,7 @@
         mib=4,
         nbytes=8 * rows * col,
     )
-    back_order = order + [0]
+    back_order = back_order_of(expert_total)
     half_in = {k: send(halves[k], "pipe", 2) for k in back_order}
     mine = call(
         functools.partial(down_pair_kernel, capacity),
@@ -429,6 +449,10 @@
         nbytes=2 * rows * col,
     )
     return mixed
+
+
+def back_order_of(experts):
+    return [experts - 1, *range(1, experts - 1), 0]
 
 
 def solution(mesh):

time: 50.7 us -> 48.6 us (0.959)
  waiting for transfers between devices: 8.51 us -> 12.7 us
  Pallas kernels: 20.4 us -> 16.4 us
  starting transfers between devices: 21.3 us -> 19 us
    ppermute x17, waiting for transfers between devices: 8.51 us -> 12.7 us  [send(): lax.ppermute(v, axis, [(i, i ^ shift) for i in range(lax.axis_size(axis))])]
    pallas_call x17 -> x18, Pallas kernels: 20.4 us -> 16.4 us  [call(): pl.pallas_call(kernel, out_shape=outs, in_specs=specs, out_specs=[VMEM] *...]
    ppermute x17, starting transfers between devices: 21.3 us -> 19 us  [send(): lax.ppermute(v, axis, [(i, i ^ shift) for i in range(lax.axis_size(axis))])]
  transfers between devices with their start and end apart: 17 -> 17, of which waited for: 8 -> 9; matrix products, arithmetic and copies ran while one was open for 0% -> 0% of each run, Pallas kernels for 29% -> 24%
where the time goes in v3:
time: 48.6 us; the launch traced here: 48.4 us
  starting transfers between devices  19 us (39%)
  Pallas kernels  16.4 us (34%)
  waiting for transfers between devices  12.7 us (26%)
    ppermute x17, starting transfers between devices, send(): lax.ppermute(v, axis, [(i, i ^ shift) for i in range(lax.axis_size(axis))])  19 us
    pallas_call x18, Pallas kernels, call(): pl.pallas_call(kernel, out_shape=outs, in_specs=specs, out_specs=[VMEM] *...  16.4 us
    ppermute x17, waiting for transfers between devices, send(): lax.ppermute(v, axis, [(i, i ^ shift) for i in range(lax.axis_size(axis))])  12.7 us
  transfers between devices with their start and end apart: 17, of which 9 were waited for; matrix products, arithmetic and copies ran while one was open for 0% of the time, Pallas kernels for 24%

profile of v3, /device:TPU:0, one launch (start us, length us, event | category | flops | bytes accessed | tf_op | source)
XLA Modules:
  0.0 48.4 jit_solution(2089980345309006734)
XLA Ops:
  0.0 1.2 %shard_map.64 = (bf16[300,128]{1,0:T(8,128)(2,1)S(1)}, bf16[300,128]{1,0:T(8,128)(2,1)S(1)}, bf16[300,128]{1,0:T(8,128)(2,1)S(1)}, f32[8,128]{1,0:T(8,128)S(1)}) custom-call(s32[2,96]{1,0:T(2,128)} %bitcast.6, bf16[96,3072]{1,0:T(8,128)(2,1)} %tokens_hbm.3), custom_call_target="tpu_custom_call" | custom-call | flops 29491200 | tf_op jit(solution)/shard_map/pallas_call | solution.py:270
  1.2 3.1 %collective-permute-start = (bf16[300,128]{1,0:T(8,128)(2,1)S(1)}, bf16[300,128]{1,0:T(8,128)(2,1)S(1)}, u32[]{:S(2)}, u32[]{:S(2)}) collective-permute-start(bf16[300,128]{1,0:T(8,128)(2,1)S(1)} %get-tuple-element.36), channel_id=1, source_target_pairs={{0,1},{1,0},{2,3},{3,2},{4,5},{5,4},{6,7},{7,6},{8,9},{9,8},{10,11... | collective-permute-start | bytes 230408 | tf_op jit(solution)/shard_map/ppermute | solution.py:295
  4.3 2.6 %collective-permute-start.2 = (bf16[300,128]{1,0:T(8,128)(2,1)S(1)}, bf16[300,128]{1,0:T(8,128)(2,1)S(1)}, u32[]{:S(2)}, u32[]{:S(2)}) collective-permute-start(bf16[300,128]{1,0:T(8,128)(2,1)S(1)} %get-tuple-element.37), channel_id=1, source_target_pairs={{0,2},{1,3},{2,0},{3,1},{4,6},{5,7},{6,4},{7,5},{8,10},{9,11},{10,... | collective-permute-start | bytes 230408 | tf_op jit(solution)/shard_map/ppermute | solution.py:295
  6.9 3.3 %shard_map.66 = (bf16[50,3072]{1,0:T(8,128)(2,1)S(1)}, bf16[4,192,50]{2,1,0:T(8,128)(2,1)S(1)}, f32[192,128]{1,0:T(8,128)S(1)}, bf16[2048,768]{1,0:T(8,128)(2,1)S(1)}, bf16[2048,768]{1,0:T(8,128)(2,1)S(1)}) custom-call(s32[2,96]{1,0:T(2,128)} %bitcast.7, f32[2,96]{1,0:T(2,128)} %bitcast.8, bf16[96,3072]{1,0:T(8,128)(2,1)} %tokens_hbm.3, ...), custom_call_target="tpu_custom_call" | custom-call | flops 117964800 | bytes 12582912 | tf_op jit(solution)/shard_map/pallas_call | solution.py:270
  10.2 2.1 %collective-permute-done.2.refs_1_ = bf16[300,128]{1,0:T(8,128)(2,1)S(1)} collective-permute-done((bf16[300,128]{1,0:T(8,128)(2,1)S(1)}, bf16[300,128]{1,0:T(8,128)(2,1)S(1)}, u32[]{:S(2)}, u32[]{:S(2)}) %collective-permute-start.2) | collective-permute-done | bytes 76832 | tf_op jit(solution)/shard_map/ppermute | solution.py:295
  12.4 0.8 %collective-permute-done.4.refs_2_ = bf16[300,128]{1,0:T(8,128)(2,1)S(1)} collective-permute-done((bf16[300,128]{1,0:T(8,128)(2,1)S(1)}, bf16[300,128]{1,0:T(8,128)(2,1)S(1)}, u32[]{:S(2)}, u32[]{:S(2)}) %collective-permute-start.4) | collective-permute-done | bytes 76832 | tf_op jit(solution)/shard_map/ppermute | solution.py:295
  13.3 1.6 %collective-permute-start.1 = (bf16[300,128]{1,0:T(8,128)(2,1)S(1)}, bf16[300,128]{1,0:T(8,128)(2,1)S(1)}, u32[]{:S(2)}, u32[]{:S(2)}) collective-permute-start(bf16[300,128]{1,0:T(8,128)(2,1)S(1)} %collective-permute-done.refs_0_), channel_id=1, source_target_pairs={{0,8},{4,12},{8,0},{12,4},{1,9},{5,13},{9,1},{13,5},{2,10},{6,14},... | collective-permute-start | bytes 230408 | tf_op jit(solution)/shard_map/ppermute | solution.py:295
  14.9 0.5 %collective-permute-start.3 = (bf16[300,128]{1,0:T(8,128)(2,1)S(1)}, bf16[300,128]{1,0:T(8,128)(2,1)S(1)}, u32[]{:S(2)}, u32[]{:S(2)}) collective-permute-start(bf16[300,128]{1,0:T(8,128)(2,1)S(1)} %collective-permute-done.2.refs_1_), channel_id=1, source_target_pairs={{0,8},{4,12},{8,0},{12,4},{1,9},{5,13},{9,1},{13,5},{2,10},{6,14},... | collective-permute-start | bytes 230408 | tf_op jit(solution)/shard_map/ppermute | solution.py:295
  15.4 1.5 %collective-permute-start.5 = (bf16[300,128]{1,0:T(8,128)(2,1)S(1)}, bf16[300,128]{1,0:T(8,128)(2,1)S(1)}, u32[]{:S(2)}, u32[]{:S(2)}) collective-permute-start(bf16[300,128]{1,0:T(8,128)(2,1)S(1)} %collective-permute-done.4.refs_2_), channel_id=1, source_target_pairs={{0,8},{4,12},{8,0},{12,4},{1,9},{5,13},{9,1},{13,5},{2,10},{6,14},... | collective-permute-start | bytes 230408 | tf_op jit(solution)/shard_map/ppermute | solution.py:295
  16.9 1.6 %collective-permute-done.1.refs_0_ = bf16[300,128]{1,0:T(8,128)(2,1)S(1)} collective-permute-done((bf16[300,128]{1,0:T(8,128)(2,1)S(1)}, bf16[300,128]{1,0:T(8,128)(2,1)S(1)}, u32[]{:S(2)}, u32[]{:S(2)}) %collective-permute-start.1) | collective-permute-done | bytes 76832 | tf_op jit(solution)/shard_map/ppermute | solution.py:295
  18.5 1.7 %collective-permute-done.3.refs_1_ = bf16[300,128]{1,0:T(8,128)(2,1)S(1)} collective-permute-done((bf16[300,128]{1,0:T(8,128)(2,1)S(1)}, bf16[300,128]{1,0:T(8,128)(2,1)S(1)}, u32[]{:S(2)}, u32[]{:S(2)}) %collective-permute-start.3) | collective-permute-done | bytes 76832 | tf_op jit(solution)/shard_map/ppermute | solution.py:295
  20.2 1.2 %collective-permute-done.5.refs_2_ = bf16[300,128]{1,0:T(8,128)(2,1)S(1)} collective-permute-done((bf16[300,128]{1,0:T(8,128)(2,1)S(1)}, bf16[300,128]{1,0:T(8,128)(2,1)S(1)}, u32[]{:S(2)}, u32[]{:S(2)}) %collective-permute-start.5) | collective-permute-done | bytes 76832 | tf_op jit(solution)/shard_map/ppermute | solution.py:295
  21.6 1.9 %shard_map.69 = (f32[200,2048]{1,0:T(8,128)S(1)}, f32[200,2048]{1,0:T(8,128)S(1)}, bf16[2048,768]{1,0:T(8,128)(2,1)S(1)}) custom-call(bf16[200,768]{1,0:T(8,128)(2,1)S(1)} %shard_map.68.x_ref, bf16[1,3072,2048]{2,1,0:T(8,128)(2,1)S(1)} %bitcast.3, bf16[1,3072,2048]{2,1,0:T(8,128)(2,1)S(1)} %bitcast.5, bf16[1,2048,3072]{2,1,0:T(8,128)(2,1)} %refs_2_.1), custom_call_target="tpu_custom_call" | custom-call | flops 1258291200 | bytes 6291456 | tf_op jit(solution)/shard_map/pallas_call | solution.py:270
  23.6 1.9 %shard_map.70 = (f32[200,2048]{1,0:T(8,128)S(1)}, f32[200,2048]{1,0:T(8,128)S(1)}, bf16[2048,768]{1,0:T(8,128)(2,1)S(1)}) custom-call(bf16[200,768]{1,0:T(8,128)(2,1)S(1)} %collective-permute-done.7.x_ref, bf16[1,3072,2048]{2,1,0:T(8,128)(2,1)S(1)} %bitcast.3, bf16[1,3072,2048]{2,1,0:T(8,128)(2,1)S(1)} %bitcast.5, ...), custom_call_target="tpu_custom_call", output_to_operand_aliasing={{0}: (3, {}), {1}: (4, {})} | custom-call | flops 1258291200 | bytes 6291456 | tf_op jit(solution)/shard_map/pallas_call | solution.py:270
  25.5 1.7 %shard_map.71 = (f32[200,2048]{1,0:T(8,128)S(1)}, f32[200,2048]{1,0:T(8,128)S(1)}) custom-call(bf16[200,768]{1,0:T(8,128)(2,1)S(1)} %shard_map.67.x_ref, bf16[1,3072,2048]{2,1,0:T(8,128)(2,1)S(1)} %bitcast.3, bf16[1,3072,2048]{2,1,0:T(8,128)(2,1)S(1)} %bitcast.5, ...), custom_call_target="tpu_custom_call", output_to_operand_aliasing={{0}: (3, {}), {1}: (4, {})} | custom-call | flops 1258291200 | bytes 6291456 | tf_op jit(solution)/shard_map/pallas_call | solution.py:270
  27.2 1.7 %shard_map.72.hidden_ref = bf16[200,2048]{1,0:T(8,128)(2,1)S(1)} custom-call(bf16[200,768]{1,0:T(8,128)(2,1)S(1)} %collective-permute-done.6.x_ref, bf16[1,3072,2048]{2,1,0:T(8,128)(2,1)S(1)} %bitcast.3, bf16[1,3072,2048]{2,1,0:T(8,128)(2,1)S(1)} %bitcast.5, f32[200,2048]{1,0:T(8,128)S(1)} %get-tuple-element.43.refs_0_, ...), custom_call_target="tpu_custom_call" | custom-call | flops 1258291200 | bytes 6291456 | tf_op jit(solution)/shard_map/pallas_call | solution.py:270
  28.9 0.9 %shard_map.75 = bf16[200,768]{1,0:T(8,128)(2,1)S(1)} custom-call(bf16[200,2048]{1,0:T(8,128)(2,1)S(1)} %shard_map.72.hidden_ref, bf16[2048,768]{1,0:T(8,128)(2,1)S(1)} %get-tuple-element.51.refs_0_), custom_call_target="tpu_custom_call" | custom-call | flops 629145600 | bytes 3145728 | tf_op jit(solution)/shard_map/pallas_call | solution.py:270
  29.8 0.5 %collective-permute-start.9 = (bf16[200,768]{1,0:T(8,128)(2,1)S(1)}, bf16[200,768]{1,0:T(8,128)(2,1)S(1)}, u32[]{:S(2)}, u32[]{:S(2)}) collective-permute-start(bf16[200,768]{1,0:T(8,128)(2,1)S(1)} %shard_map.75), channel_id=1, source_target_pairs={{0,4},{4,0},{8,12},{12,8},{1,5},{5,1},{9,13},{13,9},{2,6},{6,2},{1... | collective-permute-start | bytes 921608 | tf_op jit(solution)/shard_map/ppermute | solution.py:295
  30.3 1.5 %shard_map.73 = (f32[200,768]{1,0:T(8,128)S(1)}, bf16[200,768]{1,0:T(8,128)(2,1)S(1)}) custom-call(bf16[200,2048]{1,0:T(8,128)(2,1)S(1)} %shard_map.72.hidden_ref, bf16[2048,768]{1,0:T(8,128)(2,1)S(1)} %get-tuple-element.46.refs_0_, bf16[2048,768]{1,0:T(8,128)(2,1)S(1)} %get-tuple-element.47.refs_1_), custom_call_target="tpu_custom_call" | custom-call | flops 1258291200 | bytes 3145728 | tf_op jit(solution)/shard_map/pallas_call | solution.py:270
  32.1 1.6 %collective-permute-start.15 = (bf16[300,128]{1,0:T(8,128)(2,1)S(1)}, bf16[300,128]{1,0:T(8,128)(2,1)S(1)}, u32[]{:S(2)}, u32[]{:S(2)}) collective-permute-start(bf16[300,128]{1,0:T(8,128)(2,1)S(1)} %get-tuple-element.58), channel_id=1, source_target_pairs={{0,8},{4,12},{8,0},{12,4},{1,9},{5,13},{9,1},{13,5},{2,10},{6,14},... | collective-permute-start | bytes 230408 | tf_op jit(solution)/shard_map/ppermute | solution.py:295
  33.7 0.5 %collective-permute-start.13 = (bf16[300,128]{1,0:T(8,128)(2,1)S(1)}, bf16[300,128]{1,0:T(8,128)(2,1)S(1)}, u32[]{:S(2)}, u32[]{:S(2)}) collective-permute-start(bf16[300,128]{1,0:T(8,128)(2,1)S(1)} %get-tuple-element.56), channel_id=1, source_target_pairs={{0,8},{4,12},{8,0},{12,4},{1,9},{5,13},{9,1},{13,5},{2,10},{6,14},... | collective-permute-start | bytes 230408 | tf_op jit(solution)/shard_map/ppermute | solution.py:295
  34.2 1.5 %collective-permute-start.11 = (bf16[300,128]{1,0:T(8,128)(2,1)S(1)}, bf16[300,128]{1,0:T(8,128)(2,1)S(1)}, u32[]{:S(2)}, u32[]{:S(2)}) collective-permute-start(bf16[300,128]{1,0:T(8,128)(2,1)S(1)} %get-tuple-element.54), channel_id=1, source_target_pairs={{0,8},{4,12},{8,0},{12,4},{1,9},{5,13},{9,1},{13,5},{2,10},{6,14},... | collective-permute-start | bytes 230408 | tf_op jit(solution)/shard_map/ppermute | solution.py:295
  35.7 0.5 %collective-permute-start.10 = (bf16[300,128]{1,0:T(8,128)(2,1)S(1)}, bf16[300,128]{1,0:T(8,128)(2,1)S(1)}, u32[]{:S(2)}, u32[]{:S(2)}) collective-permute-start(bf16[300,128]{1,0:T(8,128)(2,1)S(1)} %get-tuple-element.52), channel_id=1, source_target_pairs={{0,8},{4,12},{8,0},{12,4},{1,9},{5,13},{9,1},{13,5},{2,10},{6,14},... | collective-permute-start | bytes 230408 | tf_op jit(solution)/shard_map/ppermute | solution.py:295
  36.2 0.9 %shard_map.74 = (f32[300,128]{1,0:T(8,128)S(1)}, f32[300,128]{1,0:T(8,128)S(1)}, f32[300,128]{1,0:T(8,128)S(1)}, f32[300,128]{1,0:T(8,128)S(1)}) custom-call(bf16[200,2048]{1,0:T(8,128)(2,1)S(1)} %shard_map.72.hidden_ref, bf16[2048,768]{1,0:T(8,128)(2,1)S(1)} %get-tuple-element.45.vd_ref, bf16[200,768]{1,0:T(8,128)(2,1)S(1)} %collective-permute-done.8.other_ref), custom_call_target="tpu_custom_call" | custom-call | flops 629145600 | bytes 3145728 | tf_op jit(solution)/shard_map/pallas_call | solution.py:270
  37.1 0.2 collective-permute-done.15.other_ref
  37.4 2.5 %collective-permute-start.16 = (bf16[300,128]{1,0:T(8,128)(2,1)S(1)}, bf16[300,128]{1,0:T(8,128)(2,1)S(1)}, u32[]{:S(2)}, u32[]{:S(2)}) collective-permute-start(bf16[300,128]{1,0:T(8,128)(2,1)S(1)} %shard_map.80), channel_id=1, source_target_pairs={{0,3},{1,2},{2,1},{3,0},{4,7},{5,6},{6,5},{7,4},{8,11},{9,10},{10,... | collective-permute-start | bytes 230408 | tf_op jit(solution)/shard_map/ppermute | solution.py:295
  39.9 1.6 %collective-permute-start.14 = (bf16[300,128]{1,0:T(8,128)(2,1)S(1)}, bf16[300,128]{1,0:T(8,128)(2,1)S(1)}, u32[]{:S(2)}, u32[]{:S(2)}) collective-permute-start(bf16[300,128]{1,0:T(8,128)(2,1)S(1)} %shard_map.79), channel_id=1, source_target_pairs={{0,2},{1,3},{2,0},{3,1},{4,6},{5,7},{6,4},{7,5},{8,10},{9,11},{10,... | collective-permute-start | bytes 230408 | tf_op jit(solution)/shard_map/ppermute | solution.py:295
  41.5 0.7 %collective-permute-start.12 = (bf16[300,128]{1,0:T(8,128)(2,1)S(1)}, bf16[300,128]{1,0:T(8,128)(2,1)S(1)}, u32[]{:S(2)}, u32[]{:S(2)}) collective-permute-start(bf16[300,128]{1,0:T(8,128)(2,1)S(1)} %shard_map.78), channel_id=1, source_target_pairs={{0,1},{1,0},{2,3},{3,2},{4,5},{5,4},{6,7},{7,6},{8,9},{9,8},{10,11... | collective-permute-start | bytes 230408 | tf_op jit(solution)/shard_map/ppermute | solution.py:295
  42.2 2.3 %collective-permute-done.16.refs_3_ = bf16[300,128]{1,0:T(8,128)(2,1)S(1)} collective-permute-done((bf16[300,128]{1,0:T(8,128)(2,1)S(1)}, bf16[300,128]{1,0:T(8,128)(2,1)S(1)}, u32[]{:S(2)}, u32[]{:S(2)}) %collective-permute-start.16) | collective-permute-done | bytes 76832 | tf_op jit(solution)/shard_map/ppermute | solution.py:295
  44.5 2.3 %collective-permute-done.14.refs_2_ = bf16[300,128]{1,0:T(8,128)(2,1)S(1)} collective-permute-done((bf16[300,128]{1,0:T(8,128)(2,1)S(1)}, bf16[300,128]{1,0:T(8,128)(2,1)S(1)}, u32[]{:S(2)}, u32[]{:S(2)}) %collective-permute-start.14) | collective-permute-done | bytes 76832 | tf_op jit(solution)/shard_map/ppermute | solution.py:295
  46.8 0.4 collective-permute-done.12.refs_1_
  47.3 1.1 %shard_map.81 = bf16[96,768]{1,0:T(8,128)(2,1)} custom-call(bf16[4,192,50]{2,1,0:T(8,128)(2,1)S(1)} %get-tuple-element.33.select_ref, f32[192,128]{1,0:T(8,128)S(1)} %get-tuple-element.34.scale_ref, bf16[300,128]{1,0:T(8,128)(2,1)S(1)} %shard_map.77.refs_0_, bf16[300,128]{1,0:T(8,128)(2,1)S(1)} %collective-permute-done.12.refs_1_, ...), custom_call_target="tpu_custom_call" | custom-call | flops 58982400 | bytes 307200 | tf_op jit(solution)/shard_map/pallas_call | solution.py:270
  (34 shorter events, 0.6 us)
Async XLA Ops:
  1.2 9.0 %collective-permute-start = (bf16[300,128]{1,0:T(8,128)(2,1)S(1)}, bf16[300,128]{1,0:T(8,128)(2,1)S(1)}, u32[]{:S(2)}, u32[]{:S(2)}) collective-permute-start(bf16[300,128]{1,0:T(8,128)(2,1)S(1)} %get-tuple-element.36), channel_id=1, source_target_pairs={{0,1},{1,0},{2,3},{3,2},{4,5},{5,4},{6,7},{7,6},{8,9},{9,8},{10,11... | collective-permute-start | bytes 230408 | tf_op jit(solution)/shard_map/ppermute | solution.py:295
  4.3 8.1 %collective-permute-start.2 = (bf16[300,128]{1,0:T(8,128)(2,1)S(1)}, bf16[300,128]{1,0:T(8,128)(2,1)S(1)}, u32[]{:S(2)}, u32[]{:S(2)}) collective-permute-start(bf16[300,128]{1,0:T(8,128)(2,1)S(1)} %get-tuple-element.37), channel_id=1, source_target_pairs={{0,2},{1,3},{2,0},{3,1},{4,6},{5,7},{6,4},{7,5},{8,10},{9,11},{10,... | collective-permute-start | bytes 230408 | tf_op jit(solution)/shard_map/ppermute | solution.py:295
  6.9 6.3 %collective-permute-start.4 = (bf16[300,128]{1,0:T(8,128)(2,1)S(1)}, bf16[300,128]{1,0:T(8,128)(2,1)S(1)}, u32[]{:S(2)}, u32[]{:S(2)}) collective-permute-start(bf16[300,128]{1,0:T(8,128)(2,1)S(1)} %get-tuple-element.38), channel_id=1, source_target_pairs={{0,3},{1,2},{2,1},{3,0},{4,7},{5,6},{6,5},{7,4},{8,11},{9,10},{10,... | collective-permute-start | bytes 230408 | tf_op jit(solution)/shard_map/ppermute | solution.py:295
  6.9 14.7 %slice-start = ((s8[12582912]{0:T(1024)(128)(4,1)}), s8[4194304]{0:T(1024)(128)(4,1)S(1)}, s32[]{:S(2)}) async-start(s8[12582912]{0:T(1024)(128)(4,1)} %bitcast.2), calls=%async_computation | async-start | bytes 8388608
  6.9 14.7 %slice-start.1 = ((s8[12582912]{0:T(1024)(128)(4,1)}), s8[4194304]{0:T(1024)(128)(4,1)S(1)}, s32[]{:S(2)}) async-start(s8[12582912]{0:T(1024)(128)(4,1)} %bitcast.2), calls=%async_computation.1 | async-start | bytes 8388608
  6.9 14.7 %slice-start.3 = ((s8[12582912]{0:T(1024)(128)(4,1)}), s8[4194304]{0:T(1024)(128)(4,1)S(1)}, s32[]{:S(2)}) async-start(s8[12582912]{0:T(1024)(128)(4,1)} %bitcast.4), calls=%async_computation.3 | async-start | bytes 8388608
  6.9 14.7 %slice-start.4 = ((s8[12582912]{0:T(1024)(128)(4,1)}), s8[4194304]{0:T(1024)(128)(4,1)S(1)}, s32[]{:S(2)}) async-start(s8[12582912]{0:T(1024)(128)(4,1)} %bitcast.4), calls=%async_computation.4 | async-start | bytes 8388608
  6.9 14.7 %slice-start.2 = ((s8[12582912]{0:T(1024)(128)(4,1)}), s8[4194304]{0:T(1024)(128)(4,1)S(1)}, s32[]{:S(2)}) async-start(s8[12582912]{0:T(1024)(128)(4,1)} %bitcast.2), calls=%async_computation.2 | async-start | bytes 8388608
  6.9 14.7 %slice-start.5 = ((s8[12582912]{0:T(1024)(128)(4,1)}), s8[4194304]{0:T(1024)(128)(4,1)S(1)}, s32[]{:S(2)}) async-start(s8[12582912]{0:T(1024)(128)(4,1)} %bitcast.4), calls=%async_computation.5 | async-start | bytes 8388608
  13.2 10.3 %collective-permute-start.7 = (bf16[200,768]{1,0:T(8,128)(2,1)S(1)}, bf16[200,768]{1,0:T(8,128)(2,1)S(1)}, u32[]{:S(2)}, u32[]{:S(2)}) collective-permute-start(bf16[200,768]{1,0:T(8,128)(2,1)S(1)} %shard_map.68.x_ref), channel_id=1, source_target_pairs={{0,4},{4,0},{8,12},{12,8},{1,5},{5,1},{9,13},{13,9},{2,6},{6,2},{1... | collective-permute-start | bytes 921608 | tf_op jit(solution)/shard_map/ppermute | solution.py:295
  13.3 5.2 %collective-permute-start.1 = (bf16[300,128]{1,0:T(8,128)(2,1)S(1)}, bf16[300,128]{1,0:T(8,128)(2,1)S(1)}, u32[]{:S(2)}, u32[]{:S(2)}) collective-permute-start(bf16[300,128]{1,0:T(8,128)(2,1)S(1)} %collective-permute-done.refs_0_), channel_id=1, source_target_pairs={{0,8},{4,12},{8,0},{12,4},{1,9},{5,13},{9,1},{13,5},{2,10},{6,14},... | collective-permute-start | bytes 230408 | tf_op jit(solution)/shard_map/ppermute | solution.py:295
  14.9 5.3 %collective-permute-start.3 = (bf16[300,128]{1,0:T(8,128)(2,1)S(1)}, bf16[300,128]{1,0:T(8,128)(2,1)S(1)}, u32[]{:S(2)}, u32[]{:S(2)}) collective-permute-start(bf16[300,128]{1,0:T(8,128)(2,1)S(1)} %collective-permute-done.2.refs_1_), channel_id=1, source_target_pairs={{0,8},{4,12},{8,0},{12,4},{1,9},{5,13},{9,1},{13,5},{2,10},{6,14},... | collective-permute-start | bytes 230408 | tf_op jit(solution)/shard_map/ppermute | solution.py:295
  15.4 6.0 %collective-permute-start.5 = (bf16[300,128]{1,0:T(8,128)(2,1)S(1)}, bf16[300,128]{1,0:T(8,128)(2,1)S(1)}, u32[]{:S(2)}, u32[]{:S(2)}) collective-permute-start(bf16[300,128]{1,0:T(8,128)(2,1)S(1)} %collective-permute-done.4.refs_2_), channel_id=1, source_target_pairs={{0,8},{4,12},{8,0},{12,4},{1,9},{5,13},{9,1},{13,5},{2,10},{6,14},... | collective-permute-start | bytes 230408 | tf_op jit(solution)/shard_map/ppermute | solution.py:295
  21.5 5.7 %collective-permute-start.6 = (bf16[200,768]{1,0:T(8,128)(2,1)S(1)}, bf16[200,768]{1,0:T(8,128)(2,1)S(1)}, u32[]{:S(2)}, u32[]{:S(2)}) collective-permute-start(bf16[200,768]{1,0:T(8,128)(2,1)S(1)} %shard_map.67.x_ref), channel_id=1, source_target_pairs={{0,4},{4,0},{8,12},{12,8},{1,5},{5,1},{9,13},{13,9},{2,6},{6,2},{1... | collective-permute-start | bytes 921608 | tf_op jit(solution)/shard_map/ppermute | solution.py:295
  29.8 2.2 %collective-permute-start.9 = (bf16[200,768]{1,0:T(8,128)(2,1)S(1)}, bf16[200,768]{1,0:T(8,128)(2,1)S(1)}, u32[]{:S(2)}, u32[]{:S(2)}) collective-permute-start(bf16[200,768]{1,0:T(8,128)(2,1)S(1)} %shard_map.75), channel_id=1, source_target_pairs={{0,4},{4,0},{8,12},{12,8},{1,5},{5,1},{9,13},{13,9},{2,6},{6,2},{1... | collective-permute-start | bytes 921608 | tf_op jit(solution)/shard_map/ppermute | solution.py:295
  31.9 4.4 %collective-permute-start.8 = (bf16[200,768]{1,0:T(8,128)(2,1)S(1)}, bf16[200,768]{1,0:T(8,128)(2,1)S(1)}, u32[]{:S(2)}, u32[]{:S(2)}) collective-permute-start(bf16[200,768]{1,0:T(8,128)(2,1)S(1)} %get-tuple-element.48), channel_id=1, source_target_pairs={{0,4},{4,0},{8,12},{12,8},{1,5},{5,1},{9,13},{13,9},{2,6},{6,2},{1... | collective-permute-start | bytes 921608 | tf_op jit(solution)/shard_map/ppermute | solution.py:295
  32.1 5.2 %collective-permute-start.15 = (bf16[300,128]{1,0:T(8,128)(2,1)S(1)}, bf16[300,128]{1,0:T(8,128)(2,1)S(1)}, u32[]{:S(2)}, u32[]{:S(2)}) collective-permute-start(bf16[300,128]{1,0:T(8,128)(2,1)S(1)} %get-tuple-element.58), channel_id=1, source_target_pairs={{0,8},{4,12},{8,0},{12,4},{1,9},{5,13},{9,1},{13,5},{2,10},{6,14},... | collective-permute-start | bytes 230408 | tf_op jit(solution)/shard_map/ppermute | solution.py:295
  33.7 6.2 %collective-permute-start.13 = (bf16[300,128]{1,0:T(8,128)(2,1)S(1)}, bf16[300,128]{1,0:T(8,128)(2,1)S(1)}, u32[]{:S(2)}, u32[]{:S(2)}) collective-permute-start(bf16[300,128]{1,0:T(8,128)(2,1)S(1)} %get-tuple-element.56), channel_id=1, source_target_pairs={{0,8},{4,12},{8,0},{12,4},{1,9},{5,13},{9,1},{13,5},{2,10},{6,14},... | collective-permute-start | bytes 230408 | tf_op jit(solution)/shard_map/ppermute | solution.py:295
  34.2 7.3 %collective-permute-start.11 = (bf16[300,128]{1,0:T(8,128)(2,1)S(1)}, bf16[300,128]{1,0:T(8,128)(2,1)S(1)}, u32[]{:S(2)}, u32[]{:S(2)}) collective-permute-start(bf16[300,128]{1,0:T(8,128)(2,1)S(1)} %get-tuple-element.54), channel_id=1, source_target_pairs={{0,8},{4,12},{8,0},{12,4},{1,9},{5,13},{9,1},{13,5},{2,10},{6,14},... | collective-permute-start | bytes 230408 | tf_op jit(solution)/shard_map/ppermute | solution.py:295
  35.7 6.5 %collective-permute-start.10 = (bf16[300,128]{1,0:T(8,128)(2,1)S(1)}, bf16[300,128]{1,0:T(8,128)(2,1)S(1)}, u32[]{:S(2)}, u32[]{:S(2)}) collective-permute-start(bf16[300,128]{1,0:T(8,128)(2,1)S(1)} %get-tuple-element.52), channel_id=1, source_target_pairs={{0,8},{4,12},{8,0},{12,4},{1,9},{5,13},{9,1},{13,5},{2,10},{6,14},... | collective-permute-start | bytes 230408 | tf_op jit(solution)/shard_map/ppermute | solution.py:295
  37.4 7.2 %collective-permute-start.16 = (bf16[300,128]{1,0:T(8,128)(2,1)S(1)}, bf16[300,128]{1,0:T(8,128)(2,1)S(1)}, u32[]{:S(2)}, u32[]{:S(2)}) collective-permute-start(bf16[300,128]{1,0:T(8,128)(2,1)S(1)} %shard_map.80), channel_id=1, source_target_pairs={{0,3},{1,2},{2,1},{3,0},{4,7},{5,6},{6,5},{7,4},{8,11},{9,10},{10,... | collective-permute-start | bytes 230408 | tf_op jit(solution)/shard_map/ppermute | solution.py:295
  39.9 6.9 %collective-permute-start.14 = (bf16[300,128]{1,0:T(8,128)(2,1)S(1)}, bf16[300,128]{1,0:T(8,128)(2,1)S(1)}, u32[]{:S(2)}, u32[]{:S(2)}) collective-permute-start(bf16[300,128]{1,0:T(8,128)(2,1)S(1)} %shard_map.79), channel_id=1, source_target_pairs={{0,2},{1,3},{2,0},{3,1},{4,6},{5,7},{6,4},{7,5},{8,10},{9,11},{10,... | collective-permute-start | bytes 230408 | tf_op jit(solution)/shard_map/ppermute | solution.py:295
  41.5 5.7 %collective-permute-start.12 = (bf16[300,128]{1,0:T(8,128)(2,1)S(1)}, bf16[300,128]{1,0:T(8,128)(2,1)S(1)}, u32[]{:S(2)}, u32[]{:S(2)}) collective-permute-start(bf16[300,128]{1,0:T(8,128)(2,1)S(1)} %shard_map.78), channel_id=1, source_target_pairs={{0,1},{1,0},{2,3},{3,2},{4,5},{5,4},{6,7},{7,6},{8,9},{9,8},{10,11... | collective-permute-start | bytes 230408 | tf_op jit(solution)/shard_map/ppermute | solution.py:295

commit v4 on v3

--- a/solution.py
+++ b/solution.py
@@ -14,6 +14,8 @@
 VMEM = pl.BlockSpec(memory_space=pltpu.VMEM)
 MIB = 1 << 20
 PACK_COST = 0
+FETCH = {1: 1}
+DOWN_STEP = 256
 LOCAL_COST = 12 << 20
 
 
@@ -77,15 +79,17 @@
         copy.wait()
 
 
-def put_packed(out_ref, values):
+def put_packed(out_ref, values, first=0):
     height = values.shape[0]
     for b in range(values.shape[1] // 128):
-        out_ref[b * height : (b + 1) * height, :] = values[:, b * 128 : (b + 1) * 128]
-
-
-def take_packed(ref, height):
-    blocks = ref.shape[0] // height
-    return jnp.concatenate([ref[b * height : (b + 1) * height, :] for b in range(blocks)], axis=1)
+        at = (first // 128 + b) * height
+        out_ref[at : at + height, :] = values[:, b * 128 : (b + 1) * 128]
+
+
+def take_packed(ref, height, first, count):
+    return jnp.concatenate(
+        [ref[b * height : (b + 1) * height, :] for b in range(first, first + count)], axis=1
+    )
 
 
 def cols_of(w_ref, share, width):
@@ -115,10 +119,16 @@
 
 def pack_kernel(capacity, expert_total, routes_hbm, tokens_hbm, *refs):
     outs = refs[: expert_total - 1]
-    mark_ref, routes_ref, own_ref, pick_ref, sems = refs[expert_total - 1 :]
+    mark_ref, routes_ref, own_ref, other_ref, pick_ref, sems = refs[expert_total - 1 :]
     share = lax.axis_index("pipe")
-    routes_load, own_load = load_all(
-        [(routes_hbm, routes_ref), (cols_of(tokens_hbm, share, own_ref.shape[1]), own_ref)], sems
+    width = own_ref.shape[1]
+    routes_load, own_load, other_load = load_all(
+        [
+            (routes_hbm, routes_ref),
+            (cols_of(tokens_hbm, share, width), own_ref),
+            (cols_of(tokens_hbm, jnp.bitwise_xor(share, 2), width), other_ref),
+        ],
+        sems,
     )
     routes_load.wait()
     named, count = ranks(routes_ref[...], expert_rows(max(8, expert_total)))
@@ -131,6 +141,9 @@
     picked = jnp.dot(pick_ref[...], own_ref[...], preferred_element_type=F32).astype(BF16)
     for k, out_ref in enumerate(outs):
         put_packed(out_ref, picked[k * padded : k * padded + capacity, :])
+    other_load.wait()
+    picked = jnp.dot(pick_ref[:padded, :], other_ref[...], preferred_element_type=F32).astype(BF16)
+    put_packed(outs[0], picked[:capacity, :], picked.shape[1])
     mark_ref[...] = jnp.zeros_like(mark_ref)
 
 
@@ -194,8 +207,10 @@
     width = out_ref.shape[1]
     share = jnp.bitwise_xor(lax.axis_index("pipe"), j)
     out_ref[0:capacity, :] = own_ref[:, pl.ds(pl.multiple_of(share * width, width), width)]
+    blocks = width // 128
     for i, part in enumerate(parts):
-        out_ref[(i + 1) * capacity : (i + 2) * capacity, :] = take_packed(part, capacity)
+        first = blocks if j and part.shape[0] > blocks * capacity else 0
+        out_ref[(i + 1) * capacity : (i + 2) * capacity, :] = take_packed(part, capacity, first, blocks)
 
 
 def gate_up_kernel(j, take, step, first, last, x_ref, vg_ref, vu_ref, *refs):
@@ -228,13 +243,21 @@
     wait_all(loads)
 
 
-def down_dot(hidden_ref, vd_ref):
-    return jnp.dot(hidden_ref[...], vd_ref[...], preferred_element_type=F32)
-
-
-def down_kernel(count, hidden_ref, *refs):
-    for vd_ref, out_ref in zip(refs[:count], refs[count:]):
-        out_ref[...] = down_dot(hidden_ref, vd_ref).astype(out_ref.dtype)
+def down_dots(j, hidden_ref, vd_ref, width):
+    step = DOWN_STEP if width % DOWN_STEP == 0 else width
+    start = jnp.bitwise_xor(lax.axis_index("pipe"), j) * width
+    for f in range(0, width, step):
+        if len(vd_ref.shape) == 2:
+            weights = vd_ref[:, f : f + step]
+        else:
+            weights = vd_ref[0, :, pl.ds(pl.multiple_of(start + f, 128), step)]
+        yield slice(f, f + step), jnp.dot(hidden_ref[...], weights, preferred_element_type=F32)
+
+
+def down_kernel(picks, hidden_ref, *refs):
+    for j, vd_ref, out_ref in zip(picks, refs, refs[len(picks) :]):
+        for columns, term in down_dots(j, hidden_ref, vd_ref, out_ref.shape[1]):
+            out_ref[:, columns] = term.astype(out_ref.dtype)
 
 
 def pair_kernel(capacity, mine_ref, other_ref, *outs):
@@ -245,33 +268,54 @@
 
 
 def down_pair_kernel(capacity, hidden_ref, vd_ref, other_ref, *outs):
-    total = down_dot(hidden_ref, vd_ref) + other_ref[...].astype(F32)
-    for k, out_ref in enumerate(outs):
-        put_packed(out_ref, total[k * capacity : (k + 1) * capacity, :])
+    for columns, term in down_dots(0, hidden_ref, vd_ref, other_ref.shape[1]):
+        total = term + other_ref[:, columns].astype(F32)
+        for k, out_ref in enumerate(outs):
+            put_packed(out_ref, total[k * capacity : (k + 1) * capacity, :], columns.start)
 
 
 def final_kernel(mine_ref, other_ref, out_ref):
     out_ref[...] = (mine_ref[...] + other_ref[...].astype(F32)).astype(BF16)
 
 
-def mix_kernel(capacity, select_ref, scale_ref, *refs):
+def mix_terms(capacity, picks, select_ref, parts, b):
+    total = None
+    for k, part in zip(picks, parts):
+        rows = part[b * capacity : (b + 1) * capacity, :]
+        term = jnp.dot(select_ref[k], rows, preferred_element_type=F32)
+        total = term if total is None else total + term
+    return total
+
+
+def premix_kernel(capacity, picks, select_ref, *refs):
     parts, out_ref = refs[:-1], refs[-1]
-    total = None
-    for k, part in enumerate(parts):
-        term = jnp.dot(select_ref[k], take_packed(part, capacity), preferred_element_type=F32)
-        total = term if total is None else total + term
+    for b in range(out_ref.shape[1] // 128):
+        out_ref[:, b * 128 : (b + 1) * 128] = mix_terms(capacity, picks, select_ref, parts, b)
+
+
+def mix_kernel(capacity, picks, select_ref, scale_ref, sums_ref, *refs):
+    parts, (out_hbm, out_ref, sems) = refs[:-3], refs[-3:]
     tok_rows = out_ref.shape[0]
-    first = total[:tok_rows, :] * scale_ref[:tok_rows, 0:1]
-    second = total[tok_rows:, :] * scale_ref[tok_rows:, 0:1]
-    out_ref[...] = (first + second).astype(BF16)
-
-
-def call(kernel, outs, args, specs, *, scratch=(), mib, flops=0, nbytes=0, aliases=None):
+    copies = []
+    for b in range(out_ref.shape[1] // 128):
+        columns = slice(b * 128, (b + 1) * 128)
+        total = mix_terms(capacity, picks, select_ref, parts, b) + sums_ref[:, columns]
+        weighted = total * scale_ref[...]
+        out_ref[:, columns] = (weighted[:tok_rows, :] + weighted[tok_rows:, :]).astype(BF16)
+        if b % 2:
+            pair = slice((b - 1) * 128, (b + 1) * 128)
+            copy = pltpu.make_async_copy(out_ref.at[:, pair], out_hbm.at[:, pair], sems.at[len(copies)])
+            copy.start()
+            copies.append(copy)
+    wait_all(copies)
+
+
+def call(kernel, outs, args, specs, *, scratch=(), mib, flops=0, nbytes=0, aliases=None, results=VMEM):
     return pl.pallas_call(
         kernel,
         out_shape=outs,
         in_specs=specs,
-        out_specs=[VMEM] * len(outs),
+        out_specs=[results] * len(outs),
         scratch_shapes=scratch,
         input_output_aliases=aliases or {},
         compiler_params=pltpu.CompilerParams(vmem_limit_bytes=int(mib * MIB)),
@@ -307,26 +351,23 @@
     padded = (capacity + 15) // 16 * 16
     *packed, mark = call(
         functools.partial(pack_kernel, capacity, expert_total),
-        [array(packed_shape)] * (expert_total - 1) + [array((8, 128), F32)],
+        [array((2 * packed_shape[0], 128))]
+        + [array(packed_shape)] * (expert_total - 2)
+        + [array((8, 128), F32)],
         (in_hbm(routes_t), in_hbm(tokens)),
         [HBM, HBM],
         scratch=[
             pltpu.VMEM((2, tok_rows), jnp.int32),
             pltpu.VMEM((tok_rows, col), BF16),
+            pltpu.VMEM((tok_rows, col), BF16),
             pltpu.VMEM(((expert_total - 1) * padded, tok_rows), BF16),
-            dma((2,)),
+            dma((3,)),
         ],
         mib=4,
         flops=2 * rows * tok_rows * col,
         nbytes=PACK_COST,
     )
-    (mark,) = call(
-        lead_kernel,
-        [array((8, 128), F32)],
-        (mark, in_hbm(w_gate), in_hbm(w_up)),
-        [VMEM, HBM, HBM],
-        mib=1,
-    )
+    (mark,) = call(lead_kernel, [array((8, 128), F32)], (mark, in_hbm(w_gate), in_hbm(w_up)), [VMEM, HBM, HBM], mib=1)
     order = sorted(others, reverse=True)
     arrived = {k: send(packed[k - 1], "expert", k) for k in order}
 
@@ -365,18 +406,19 @@
         )
         return out
 
-    crossed = {k: send(arrived[k], "pipe", 2) for k in order}
+    crossed = {k: send(arrived[k], "pipe", 2) for k in order if k != 1}
+    crossed[1] = arrived[1]
     x0 = join(0, arrived)
     x1 = send(x0, "pipe", 1)
     x2 = join(2, crossed)
     x3 = send(x2, "pipe", 1)
 
     sums = ()
-    vd = dict(zip(takes, fetched))
+    vd = {0: pltpu.with_memory_space_constraint(w_down, pltpu.VMEM), **dict(zip(takes, fetched))}
     total = pltpu.VMEM((rows, hidden_width), F32)
     for j, x in enumerate((x0, x1, x2, x3)):
         first, last = j == 0, j == pipe_count - 1
-        take = {0: 1, 1: 0}.get(j)
+        take = FETCH.get(j)
         fetch = take is not None
         outs = call(
             functools.partial(gate_up_kernel, j, take, min(256, hidden_width), first, last),
@@ -390,13 +432,13 @@
             aliases={} if first or last else {3: 0, 4: 1},
         )
         if fetch:
-            vd[take] = outs.pop() if isinstance(outs, list) else outs[-1]
+            vd[take] = outs[-1]
         sums = tuple(outs[: 1 if last else 2])
     (hidden,) = sums
 
     def down(picks, dtypes):
         return call(
-            functools.partial(down_kernel, len(picks)),
+            functools.partial(down_kernel, picks),
             [array((rows, col), d) for d in dtypes],
             (hidden, *[vd[j] for j in picks]),
             [VMEM] * (1 + len(picks)),
@@ -431,22 +473,28 @@
     home = {}
     for k in back_order:
         (done,) = call(
-            final_kernel,
-            [array(packed_shape)],
-            (mine[k], half_in[k]),
-            [VMEM, VMEM],
-            mib=2,
-            nbytes=8 * capacity * col,
+            final_kernel, [array(packed_shape)], (mine[k], half_in[k]), [VMEM, VMEM], mib=2, nbytes=8 * capacity * col
         )
         home[k] = send(done, "expert", k) if k else done
-    (mixed,) = call(
-        functools.partial(mix_kernel, capacity),
-        [array((tok_rows, col))],
-        (select, scale, *[home[k] for k in range(expert_total)]),
-        [VMEM] * (2 + expert_total),
+    last = back_order[-2:-1]
+    early = [k for k in range(expert_total) if k not in last]
+    (premixed,) = call(
+        functools.partial(premix_kernel, capacity, early),
+        [array((2 * tok_rows, col), F32)],
+        (select, *[home[k] for k in early]),
+        [VMEM] * (1 + len(early)),
         mib=4,
         flops=4 * rows * tok_rows * col,
-        nbytes=2 * rows * col,
+    )
+    (mixed,) = call(
+        functools.partial(mix_kernel, capacity, last),
+        [array((tok_rows, col))],
+        (select, scale, premixed, *[home[k] for k in last]),
+        [VMEM] * (3 + len(last)),
+        scratch=[pltpu.VMEM((tok_rows, col), BF16), dma((col // 256,))],
+        mib=4,
+        flops=4 * capacity * tok_rows * col,
+        results=HBM,
     )
     return mixed
 
@@ -462,6 +510,7 @@
         col = tokens.shape[1] // mesh.shape["pipe"]
         fits = (
             mesh.shape["pipe"] == 4
+            and experts > 2
             and experts & (experts - 1) == 0
             and w_gate.shape[0] == 1
             and col % 128 == 0

time: 48.6 us -> 48.8 us (level)
  waiting for transfers between devices: 12.7 us -> 14.6 us
  starting transfers between devices: 19 us -> 17.3 us
    ppermute x17 -> x16, waiting for transfers between devices: 12.7 us -> 14.6 us  [send(): lax.ppermute(v, axis, [(i, i ^ shift) for i in range(lax.axis_size(axis))])]
    ppermute x17 -> x16, starting transfers between devices: 19 us -> 17.3 us  [send(): lax.ppermute(v, axis, [(i, i ^ shift) for i in range(lax.axis_size(axis))])]
    pallas_call x18 -> x19, Pallas kernels: 16.4 us -> 16.4 us  [call(): pl.pallas_call(kernel, out_shape=outs, in_specs=specs, out_specs=[results...]
  transfers between devices with their start and end apart: 17 -> 16, of which waited for: 9 -> 8; matrix products, arithmetic and copies ran while one was open for 0% -> 0% of each run, Pallas kernels for 24% -> 24%
where the time goes in v4:
time: 48.8 us; the launch traced here: 48.6 us
  starting transfers between devices  17.3 us (35%)
  Pallas kernels  16.4 us (34%)
  waiting for transfers between devices  14.6 us (30%)
    ppermute x16, starting transfers between devices, send(): lax.ppermute(v, axis, [(i, i ^ shift) for i in range(lax.axis_size(axis))])  17.3 us
    pallas_call x19, Pallas kernels, call(): pl.pallas_call(kernel, out_shape=outs, in_specs=specs, out_specs=[results...  16.4 us
    ppermute x16, waiting for transfers between devices, send(): lax.ppermute(v, axis, [(i, i ^ shift) for i in range(lax.axis_size(axis))])  14.6 us
  transfers between devices with their start and end apart: 16, of which 8 were waited for; matrix products, arithmetic and copies ran while one was open for 0% of the time, Pallas kernels for 24%

profile of v4, /device:TPU:0, one launch (start us, length us, event | category | flops | bytes accessed | tf_op | source)
XLA Modules:
  0.0 48.6 jit_solution(13603250763125448155)
XLA Ops:
  0.0 1.4 %shard_map.64 = (bf16[600,128]{1,0:T(8,128)(2,1)S(1)}, bf16[300,128]{1,0:T(8,128)(2,1)S(1)}, bf16[300,128]{1,0:T(8,128)(2,1)S(1)}, f32[8,128]{1,0:T(8,128)S(1)}) custom-call(s32[2,96]{1,0:T(2,128)} %bitcast.8, bf16[96,3072]{1,0:T(8,128)(2,1)} %tokens_hbm.3), custom_call_target="tpu_custom_call" | custom-call | flops 29491200 | tf_op jit(solution)/shard_map/pallas_call | solution.py:314
  1.4 3.1 %collective-permute-start = (bf16[600,128]{1,0:T(8,128)(2,1)S(1)}, bf16[600,128]{1,0:T(8,128)(2,1)S(1)}, u32[]{:S(2)}, u32[]{:S(2)}) collective-permute-start(bf16[600,128]{1,0:T(8,128)(2,1)S(1)} %get-tuple-element.35), channel_id=1, source_target_pairs={{0,1},{1,0},{2,3},{3,2},{4,5},{5,4},{6,7},{7,6},{8,9},{9,8},{10,11... | collective-permute-start | bytes 460808 | tf_op jit(solution)/shard_map/ppermute | solution.py:339
  4.5 2.6 %collective-permute-start.1 = (bf16[300,128]{1,0:T(8,128)(2,1)S(1)}, bf16[300,128]{1,0:T(8,128)(2,1)S(1)}, u32[]{:S(2)}, u32[]{:S(2)}) collective-permute-start(bf16[300,128]{1,0:T(8,128)(2,1)S(1)} %get-tuple-element.36), channel_id=1, source_target_pairs={{0,2},{1,3},{2,0},{3,1},{4,6},{5,7},{6,4},{7,5},{8,10},{9,11},{10,... | collective-permute-start | bytes 230408 | tf_op jit(solution)/shard_map/ppermute | solution.py:339
  7.2 3.3 %shard_map.66 = (bf16[50,3072]{1,0:T(8,128)(2,1)S(1)}, bf16[4,192,50]{2,1,0:T(8,128)(2,1)S(1)}, f32[192,128]{1,0:T(8,128)S(1)}, bf16[2048,768]{1,0:T(8,128)(2,1)S(1)}, bf16[2048,768]{1,0:T(8,128)(2,1)S(1)}) custom-call(s32[2,96]{1,0:T(2,128)} %bitcast.9, f32[2,96]{1,0:T(2,128)} %bitcast.10, bf16[96,3072]{1,0:T(8,128)(2,1)} %tokens_hbm.3, ...), custom_call_target="tpu_custom_call" | custom-call | flops 117964800 | bytes 12582912 | tf_op jit(solution)/shard_map/pallas_call | solution.py:314
  10.4 1.1 %collective-permute-done.1.refs_1_ = bf16[300,128]{1,0:T(8,128)(2,1)S(1)} collective-permute-done((bf16[300,128]{1,0:T(8,128)(2,1)S(1)}, bf16[300,128]{1,0:T(8,128)(2,1)S(1)}, u32[]{:S(2)}, u32[]{:S(2)}) %collective-permute-start.1) | collective-permute-done | bytes 76832 | tf_op jit(solution)/shard_map/ppermute | solution.py:339
  11.5 2.6 %collective-permute-done.3.refs_2_ = bf16[300,128]{1,0:T(8,128)(2,1)S(1)} collective-permute-done((bf16[300,128]{1,0:T(8,128)(2,1)S(1)}, bf16[300,128]{1,0:T(8,128)(2,1)S(1)}, u32[]{:S(2)}, u32[]{:S(2)}) %collective-permute-start.3) | collective-permute-done | bytes 76832 | tf_op jit(solution)/shard_map/ppermute | solution.py:339
  14.3 1.6 %collective-permute-start.2 = (bf16[300,128]{1,0:T(8,128)(2,1)S(1)}, bf16[300,128]{1,0:T(8,128)(2,1)S(1)}, u32[]{:S(2)}, u32[]{:S(2)}) collective-permute-start(bf16[300,128]{1,0:T(8,128)(2,1)S(1)} %collective-permute-done.1.refs_1_), channel_id=1, source_target_pairs={{0,8},{4,12},{8,0},{12,4},{1,9},{5,13},{9,1},{13,5},{2,10},{6,14},... | collective-permute-start | bytes 230408 | tf_op jit(solution)/shard_map/ppermute | solution.py:339
  15.8 0.5 %collective-permute-start.4 = (bf16[300,128]{1,0:T(8,128)(2,1)S(1)}, bf16[300,128]{1,0:T(8,128)(2,1)S(1)}, u32[]{:S(2)}, u32[]{:S(2)}) collective-permute-start(bf16[300,128]{1,0:T(8,128)(2,1)S(1)} %collective-permute-done.3.refs_2_), channel_id=1, source_target_pairs={{0,8},{4,12},{8,0},{12,4},{1,9},{5,13},{9,1},{13,5},{2,10},{6,14},... | collective-permute-start | bytes 230408 | tf_op jit(solution)/shard_map/ppermute | solution.py:339
  16.3 3.1 %collective-permute-done.2.refs_1_ = bf16[300,128]{1,0:T(8,128)(2,1)S(1)} collective-permute-done((bf16[300,128]{1,0:T(8,128)(2,1)S(1)}, bf16[300,128]{1,0:T(8,128)(2,1)S(1)}, u32[]{:S(2)}, u32[]{:S(2)}) %collective-permute-start.2) | collective-permute-done | bytes 76832 | tf_op jit(solution)/shard_map/ppermute | solution.py:339
  19.4 1.2 %collective-permute-done.4.refs_2_ = bf16[300,128]{1,0:T(8,128)(2,1)S(1)} collective-permute-done((bf16[300,128]{1,0:T(8,128)(2,1)S(1)}, bf16[300,128]{1,0:T(8,128)(2,1)S(1)}, u32[]{:S(2)}, u32[]{:S(2)}) %collective-permute-start.4) | collective-permute-done | bytes 76832 | tf_op jit(solution)/shard_map/ppermute | solution.py:339
  20.9 1.6 %shard_map.69 = (f32[200,2048]{1,0:T(8,128)S(1)}, f32[200,2048]{1,0:T(8,128)S(1)}) custom-call(bf16[200,768]{1,0:T(8,128)(2,1)S(1)} %shard_map.68.x_ref, bf16[1,3072,2048]{2,1,0:T(8,128)(2,1)S(1)} %bitcast.3, bf16[1,3072,2048]{2,1,0:T(8,128)(2,1)S(1)} %bitcast.5), custom_call_target="tpu_custom_call" | custom-call | flops 1258291200 | bytes 6291456 | tf_op jit(solution)/shard_map/pallas_call | solution.py:314
  22.5 1.9 %shard_map.70 = (f32[200,2048]{1,0:T(8,128)S(1)}, f32[200,2048]{1,0:T(8,128)S(1)}, bf16[2048,768]{1,0:T(8,128)(2,1)S(1)}) custom-call(bf16[200,768]{1,0:T(8,128)(2,1)S(1)} %collective-permute-done.6.x_ref, bf16[1,3072,2048]{2,1,0:T(8,128)(2,1)S(1)} %bitcast.3, bf16[1,3072,2048]{2,1,0:T(8,128)(2,1)S(1)} %bitcast.5, ...), custom_call_target="tpu_custom_call", output_to_operand_aliasing={{0}: (3, {}), {1}: (4, {})} | custom-call | flops 1258291200 | bytes 6291456 | tf_op jit(solution)/shard_map/pallas_call | solution.py:314
  24.4 1.7 %shard_map.71 = (f32[200,2048]{1,0:T(8,128)S(1)}, f32[200,2048]{1,0:T(8,128)S(1)}) custom-call(bf16[200,768]{1,0:T(8,128)(2,1)S(1)} %shard_map.67.x_ref, bf16[1,3072,2048]{2,1,0:T(8,128)(2,1)S(1)} %bitcast.3, bf16[1,3072,2048]{2,1,0:T(8,128)(2,1)S(1)} %bitcast.5, ...), custom_call_target="tpu_custom_call", output_to_operand_aliasing={{0}: (3, {}), {1}: (4, {})} | custom-call | flops 1258291200 | bytes 6291456 | tf_op jit(solution)/shard_map/pallas_call | solution.py:314
  26.1 1.7 %shard_map.72.hidden_ref = bf16[200,2048]{1,0:T(8,128)(2,1)S(1)} custom-call(bf16[200,768]{1,0:T(8,128)(2,1)S(1)} %collective-permute-done.5.x_ref, bf16[1,3072,2048]{2,1,0:T(8,128)(2,1)S(1)} %bitcast.3, bf16[1,3072,2048]{2,1,0:T(8,128)(2,1)S(1)} %bitcast.5, f32[200,2048]{1,0:T(8,128)S(1)} %get-tuple-element.42.refs_0_, ...), custom_call_target="tpu_custom_call" | custom-call | flops 1258291200 | bytes 6291456 | tf_op jit(solution)/shard_map/pallas_call | solution.py:314
  27.9 0.8 %shard_map.75 = bf16[200,768]{1,0:T(8,128)(2,1)S(1)} custom-call(bf16[200,2048]{1,0:T(8,128)(2,1)S(1)} %shard_map.72.hidden_ref, bf16[2048,768]{1,0:T(8,128)(2,1)S(1)} %get-tuple-element.49.refs_0_), custom_call_target="tpu_custom_call" | custom-call | flops 629145600 | bytes 3145728 | tf_op jit(solution)/shard_map/pallas_call | solution.py:314
  28.7 0.5 %collective-permute-start.8 = (bf16[200,768]{1,0:T(8,128)(2,1)S(1)}, bf16[200,768]{1,0:T(8,128)(2,1)S(1)}, u32[]{:S(2)}, u32[]{:S(2)}) collective-permute-start(bf16[200,768]{1,0:T(8,128)(2,1)S(1)} %shard_map.75), channel_id=1, source_target_pairs={{0,4},{4,0},{8,12},{12,8},{1,5},{5,1},{9,13},{13,9},{2,6},{6,2},{1... | collective-permute-start | bytes 921608 | tf_op jit(solution)/shard_map/ppermute | solution.py:339
  29.2 1.6 %shard_map.73 = (f32[200,768]{1,0:T(8,128)S(1)}, bf16[200,768]{1,0:T(8,128)(2,1)S(1)}) custom-call(bf16[200,2048]{1,0:T(8,128)(2,1)S(1)} %shard_map.72.hidden_ref, bf16[2048,768]{1,0:T(8,128)(2,1)S(1)} %get-tuple-element.44.refs_0_, bf16[2048,768]{1,0:T(8,128)(2,1)S(1)} %get-tuple-element.45.refs_1_), custom_call_target="tpu_custom_call" | custom-call | flops 1258291200 | bytes 3145728 | tf_op jit(solution)/shard_map/pallas_call | solution.py:314
  30.9 0.1 shard_map.76
  31.1 1.6 %collective-permute-start.10 = (bf16[300,128]{1,0:T(8,128)(2,1)S(1)}, bf16[300,128]{1,0:T(8,128)(2,1)S(1)}, u32[]{:S(2)}, u32[]{:S(2)}) collective-permute-start(bf16[300,128]{1,0:T(8,128)(2,1)S(1)} %get-tuple-element.52), channel_id=1, source_target_pairs={{0,8},{4,12},{8,0},{12,4},{1,9},{5,13},{9,1},{13,5},{2,10},{6,14},... | collective-permute-start | bytes 230408 | tf_op jit(solution)/shard_map/ppermute | solution.py:339
  32.6 0.5 %collective-permute-start.12 = (bf16[300,128]{1,0:T(8,128)(2,1)S(1)}, bf16[300,128]{1,0:T(8,128)(2,1)S(1)}, u32[]{:S(2)}, u32[]{:S(2)}) collective-permute-start(bf16[300,128]{1,0:T(8,128)(2,1)S(1)} %get-tuple-element.54), channel_id=1, source_target_pairs={{0,8},{4,12},{8,0},{12,4},{1,9},{5,13},{9,1},{13,5},{2,10},{6,14},... | collective-permute-start | bytes 230408 | tf_op jit(solution)/shard_map/ppermute | solution.py:339
  33.1 1.5 %collective-permute-start.14 = (bf16[300,128]{1,0:T(8,128)(2,1)S(1)}, bf16[300,128]{1,0:T(8,128)(2,1)S(1)}, u32[]{:S(2)}, u32[]{:S(2)}) collective-permute-start(bf16[300,128]{1,0:T(8,128)(2,1)S(1)} %get-tuple-element.56), channel_id=1, source_target_pairs={{0,8},{4,12},{8,0},{12,4},{1,9},{5,13},{9,1},{13,5},{2,10},{6,14},... | collective-permute-start | bytes 230408 | tf_op jit(solution)/shard_map/ppermute | solution.py:339
  34.7 0.5 %collective-permute-start.9 = (bf16[300,128]{1,0:T(8,128)(2,1)S(1)}, bf16[300,128]{1,0:T(8,128)(2,1)S(1)}, u32[]{:S(2)}, u32[]{:S(2)}) collective-permute-start(bf16[300,128]{1,0:T(8,128)(2,1)S(1)} %get-tuple-element.50), channel_id=1, source_target_pairs={{0,8},{4,12},{8,0},{12,4},{1,9},{5,13},{9,1},{13,5},{2,10},{6,14},... | collective-permute-start | bytes 230408 | tf_op jit(solution)/shard_map/ppermute | solution.py:339
  35.2 0.9 %shard_map.74 = (f32[300,128]{1,0:T(8,128)S(1)}, f32[300,128]{1,0:T(8,128)S(1)}, f32[300,128]{1,0:T(8,128)S(1)}, f32[300,128]{1,0:T(8,128)S(1)}) custom-call(bf16[200,2048]{1,0:T(8,128)(2,1)S(1)} %shard_map.72.hidden_ref, bf16[1,2048,3072]{2,1,0:T(8,128)(2,1)S(1)} %bitcast.7, bf16[200,768]{1,0:T(8,128)(2,1)S(1)} %collective-permute-done.7.other_ref), custom_call_target="tpu_custom_call" | custom-call | flops 629145600 | bytes 3145728 | tf_op jit(solution)/shard_map/pallas_call | solution.py:314
  36.1 0.2 collective-permute-done.10.other_ref
  36.3 1.2 %collective-permute-start.11 = (bf16[300,128]{1,0:T(8,128)(2,1)S(1)}, bf16[300,128]{1,0:T(8,128)(2,1)S(1)}, u32[]{:S(2)}, u32[]{:S(2)}) collective-permute-start(bf16[300,128]{1,0:T(8,128)(2,1)S(1)} %shard_map.78), channel_id=1, source_target_pairs={{0,1},{1,0},{2,3},{3,2},{4,5},{5,4},{6,7},{7,6},{8,9},{9,8},{10,11... | collective-permute-start | bytes 230408 | tf_op jit(solution)/shard_map/ppermute | solution.py:339
  37.5 0.4 collective-permute-done.12.other_ref
  38.0 1.8 %collective-permute-start.13 = (bf16[300,128]{1,0:T(8,128)(2,1)S(1)}, bf16[300,128]{1,0:T(8,128)(2,1)S(1)}, u32[]{:S(2)}, u32[]{:S(2)}) collective-permute-start(bf16[300,128]{1,0:T(8,128)(2,1)S(1)} %shard_map.79), channel_id=1, source_target_pairs={{0,3},{1,2},{2,1},{3,0},{4,7},{5,6},{6,5},{7,4},{8,11},{9,10},{10,... | collective-permute-start | bytes 230408 | tf_op jit(solution)/shard_map/ppermute | solution.py:339
  39.8 1.6 %collective-permute-start.15 = (bf16[300,128]{1,0:T(8,128)(2,1)S(1)}, bf16[300,128]{1,0:T(8,128)(2,1)S(1)}, u32[]{:S(2)}, u32[]{:S(2)}) collective-permute-start(bf16[300,128]{1,0:T(8,128)(2,1)S(1)} %shard_map.81), channel_id=1, source_target_pairs={{0,2},{1,3},{2,0},{3,1},{4,6},{5,7},{6,4},{7,5},{8,10},{9,11},{10,... | collective-permute-start | bytes 230408 | tf_op jit(solution)/shard_map/ppermute | solution.py:339
  41.4 3.3 %collective-permute-done.13.refs_2_ = bf16[300,128]{1,0:T(8,128)(2,1)S(1)} collective-permute-done((bf16[300,128]{1,0:T(8,128)(2,1)S(1)}, bf16[300,128]{1,0:T(8,128)(2,1)S(1)}, u32[]{:S(2)}, u32[]{:S(2)}) %collective-permute-start.13) | collective-permute-done | bytes 76832 | tf_op jit(solution)/shard_map/ppermute | solution.py:339
  44.7 0.4 shard_map.80.sums_ref
  45.1 2.6 %collective-permute-done.15.refs_0_ = bf16[300,128]{1,0:T(8,128)(2,1)S(1)} collective-permute-done((bf16[300,128]{1,0:T(8,128)(2,1)S(1)}, bf16[300,128]{1,0:T(8,128)(2,1)S(1)}, u32[]{:S(2)}, u32[]{:S(2)}) %collective-permute-start.15) | collective-permute-done | bytes 76832 | tf_op jit(solution)/shard_map/ppermute | solution.py:339
  47.7 0.9 %shard_map.82 = bf16[96,768]{1,0:T(8,128)(2,1)} custom-call(bf16[4,192,50]{2,1,0:T(8,128)(2,1)S(1)} %get-tuple-element.32.select_ref, f32[192,128]{1,0:T(8,128)S(1)} %get-tuple-element.33.scale_ref, f32[192,768]{1,0:T(8,128)S(1)} %shard_map.80.sums_ref, bf16[300,128]{1,0:T(8,128)(2,1)S(1)} %collective-permute-done.15.refs_0_), custom_call_target="tpu_custom_call" | custom-call | flops 14745600 | tf_op jit(solution)/shard_map/pallas_call | solution.py:314
  (40 shorter events, 0.5 us)
Async XLA Ops:
  1.4 12.7 %collective-permute-start = (bf16[600,128]{1,0:T(8,128)(2,1)S(1)}, bf16[600,128]{1,0:T(8,128)(2,1)S(1)}, u32[]{:S(2)}, u32[]{:S(2)}) collective-permute-start(bf16[600,128]{1,0:T(8,128)(2,1)S(1)} %get-tuple-element.35), channel_id=1, source_target_pairs={{0,1},{1,0},{2,3},{3,2},{4,5},{5,4},{6,7},{7,6},{8,9},{9,8},{10,11... | collective-permute-start | bytes 460808 | tf_op jit(solution)/shard_map/ppermute | solution.py:339
  4.5 7.0 %collective-permute-start.1 = (bf16[300,128]{1,0:T(8,128)(2,1)S(1)}, bf16[300,128]{1,0:T(8,128)(2,1)S(1)}, u32[]{:S(2)}, u32[]{:S(2)}) collective-permute-start(bf16[300,128]{1,0:T(8,128)(2,1)S(1)} %get-tuple-element.36), channel_id=1, source_target_pairs={{0,2},{1,3},{2,0},{3,1},{4,6},{5,7},{6,4},{7,5},{8,10},{9,11},{10,... | collective-permute-start | bytes 230408 | tf_op jit(solution)/shard_map/ppermute | solution.py:339
  7.1 7.0 %collective-permute-start.3 = (bf16[300,128]{1,0:T(8,128)(2,1)S(1)}, bf16[300,128]{1,0:T(8,128)(2,1)S(1)}, u32[]{:S(2)}, u32[]{:S(2)}) collective-permute-start(bf16[300,128]{1,0:T(8,128)(2,1)S(1)} %get-tuple-element.37), channel_id=1, source_target_pairs={{0,3},{1,2},{2,1},{3,0},{4,7},{5,6},{6,5},{7,4},{8,11},{9,10},{10,... | collective-permute-start | bytes 230408 | tf_op jit(solution)/shard_map/ppermute | solution.py:339
  7.1 13.7 %slice-start = ((s8[12582912]{0:T(1024)(128)(4,1)}), s8[4194304]{0:T(1024)(128)(4,1)S(1)}, s32[]{:S(2)}) async-start(s8[12582912]{0:T(1024)(128)(4,1)} %bitcast.2), calls=%async_computation | async-start | bytes 8388608
  7.1 13.7 %slice-start.1 = ((s8[12582912]{0:T(1024)(128)(4,1)}), s8[4194304]{0:T(1024)(128)(4,1)S(1)}, s32[]{:S(2)}) async-start(s8[12582912]{0:T(1024)(128)(4,1)} %bitcast.2), calls=%async_computation.1 | async-start | bytes 8388608
  7.1 13.7 %slice-start.3 = ((s8[12582912]{0:T(1024)(128)(4,1)}), s8[4194304]{0:T(1024)(128)(4,1)S(1)}, s32[]{:S(2)}) async-start(s8[12582912]{0:T(1024)(128)(4,1)} %bitcast.4), calls=%async_computation.3 | async-start | bytes 8388608
  7.1 13.7 %slice-start.4 = ((s8[12582912]{0:T(1024)(128)(4,1)}), s8[4194304]{0:T(1024)(128)(4,1)S(1)}, s32[]{:S(2)}) async-start(s8[12582912]{0:T(1024)(128)(4,1)} %bitcast.4), calls=%async_computation.4 | async-start | bytes 8388608
  7.1 13.7 %slice-start.2 = ((s8[12582912]{0:T(1024)(128)(4,1)}), s8[4194304]{0:T(1024)(128)(4,1)S(1)}, s32[]{:S(2)}) async-start(s8[12582912]{0:T(1024)(128)(4,1)} %bitcast.2), calls=%async_computation.2 | async-start | bytes 8388608
  7.1 13.7 %slice-start.5 = ((s8[12582912]{0:T(1024)(128)(4,1)}), s8[4194304]{0:T(1024)(128)(4,1)S(1)}, s32[]{:S(2)}) async-start(s8[12582912]{0:T(1024)(128)(4,1)} %bitcast.4), calls=%async_computation.5 | async-start | bytes 8388608
  14.2 8.3 %collective-permute-start.6 = (bf16[200,768]{1,0:T(8,128)(2,1)S(1)}, bf16[200,768]{1,0:T(8,128)(2,1)S(1)}, u32[]{:S(2)}, u32[]{:S(2)}) collective-permute-start(bf16[200,768]{1,0:T(8,128)(2,1)S(1)} %shard_map.68.x_ref), channel_id=1, source_target_pairs={{0,4},{4,0},{8,12},{12,8},{1,5},{5,1},{9,13},{13,9},{2,6},{6,2},{1... | collective-permute-start | bytes 921608 | tf_op jit(solution)/shard_map/ppermute | solution.py:339
  14.3 5.2 %collective-permute-start.2 = (bf16[300,128]{1,0:T(8,128)(2,1)S(1)}, bf16[300,128]{1,0:T(8,128)(2,1)S(1)}, u32[]{:S(2)}, u32[]{:S(2)}) collective-permute-start(bf16[300,128]{1,0:T(8,128)(2,1)S(1)} %collective-permute-done.1.refs_1_), channel_id=1, source_target_pairs={{0,8},{4,12},{8,0},{12,4},{1,9},{5,13},{9,1},{13,5},{2,10},{6,14},... | collective-permute-start | bytes 230408 | tf_op jit(solution)/shard_map/ppermute | solution.py:339
  15.8 4.8 %collective-permute-start.4 = (bf16[300,128]{1,0:T(8,128)(2,1)S(1)}, bf16[300,128]{1,0:T(8,128)(2,1)S(1)}, u32[]{:S(2)}, u32[]{:S(2)}) collective-permute-start(bf16[300,128]{1,0:T(8,128)(2,1)S(1)} %collective-permute-done.3.refs_2_), channel_id=1, source_target_pairs={{0,8},{4,12},{8,0},{12,4},{1,9},{5,13},{9,1},{13,5},{2,10},{6,14},... | collective-permute-start | bytes 230408 | tf_op jit(solution)/shard_map/ppermute | solution.py:339
  20.7 5.3 %collective-permute-start.5 = (bf16[200,768]{1,0:T(8,128)(2,1)S(1)}, bf16[200,768]{1,0:T(8,128)(2,1)S(1)}, u32[]{:S(2)}, u32[]{:S(2)}) collective-permute-start(bf16[200,768]{1,0:T(8,128)(2,1)S(1)} %shard_map.67.x_ref), channel_id=1, source_target_pairs={{0,4},{4,0},{8,12},{12,8},{1,5},{5,1},{9,13},{13,9},{2,6},{6,2},{1... | collective-permute-start | bytes 921608 | tf_op jit(solution)/shard_map/ppermute | solution.py:339
  26.1 9.1 %slice-start.6 = ((s8[12582912]{0:T(1024)(128)(4,1)}), s8[4194304]{0:T(1024)(128)(4,1)S(1)}, s32[]{:S(2)}) async-start(s8[12582912]{0:T(1024)(128)(4,1)} %bitcast.6), calls=%async_computation.6 | async-start | bytes 8388608
  26.1 9.1 %slice-start.7 = ((s8[12582912]{0:T(1024)(128)(4,1)}), s8[4194304]{0:T(1024)(128)(4,1)S(1)}, s32[]{:S(2)}) async-start(s8[12582912]{0:T(1024)(128)(4,1)} %bitcast.6), calls=%async_computation.7 | async-start | bytes 8388608
  26.1 9.1 %slice-start.8 = ((s8[12582912]{0:T(1024)(128)(4,1)}), s8[4194304]{0:T(1024)(128)(4,1)S(1)}, s32[]{:S(2)}) async-start(s8[12582912]{0:T(1024)(128)(4,1)} %bitcast.6), calls=%async_computation.8 | async-start | bytes 8388608
  28.7 2.2 %collective-permute-start.8 = (bf16[200,768]{1,0:T(8,128)(2,1)S(1)}, bf16[200,768]{1,0:T(8,128)(2,1)S(1)}, u32[]{:S(2)}, u32[]{:S(2)}) collective-permute-start(bf16[200,768]{1,0:T(8,128)(2,1)S(1)} %shard_map.75), channel_id=1, source_target_pairs={{0,4},{4,0},{8,12},{12,8},{1,5},{5,1},{9,13},{13,9},{2,6},{6,2},{1... | collective-permute-start | bytes 921608 | tf_op jit(solution)/shard_map/ppermute | solution.py:339
  30.8 4.4 %collective-permute-start.7 = (bf16[200,768]{1,0:T(8,128)(2,1)S(1)}, bf16[200,768]{1,0:T(8,128)(2,1)S(1)}, u32[]{:S(2)}, u32[]{:S(2)}) collective-permute-start(bf16[200,768]{1,0:T(8,128)(2,1)S(1)} %get-tuple-element.46), channel_id=1, source_target_pairs={{0,4},{4,0},{8,12},{12,8},{1,5},{5,1},{9,13},{13,9},{2,6},{6,2},{1... | collective-permute-start | bytes 921608 | tf_op jit(solution)/shard_map/ppermute | solution.py:339
  31.1 5.2 %collective-permute-start.10 = (bf16[300,128]{1,0:T(8,128)(2,1)S(1)}, bf16[300,128]{1,0:T(8,128)(2,1)S(1)}, u32[]{:S(2)}, u32[]{:S(2)}) collective-permute-start(bf16[300,128]{1,0:T(8,128)(2,1)S(1)} %get-tuple-element.52), channel_id=1, source_target_pairs={{0,8},{4,12},{8,0},{12,4},{1,9},{5,13},{9,1},{13,5},{2,10},{6,14},... | collective-permute-start | bytes 230408 | tf_op jit(solution)/shard_map/ppermute | solution.py:339
  32.6 5.3 %collective-permute-start.12 = (bf16[300,128]{1,0:T(8,128)(2,1)S(1)}, bf16[300,128]{1,0:T(8,128)(2,1)S(1)}, u32[]{:S(2)}, u32[]{:S(2)}) collective-permute-start(bf16[300,128]{1,0:T(8,128)(2,1)S(1)} %get-tuple-element.54), channel_id=1, source_target_pairs={{0,8},{4,12},{8,0},{12,4},{1,9},{5,13},{9,1},{13,5},{2,10},{6,14},... | collective-permute-start | bytes 230408 | tf_op jit(solution)/shard_map/ppermute | solution.py:339
  33.1 6.7 %collective-permute-start.14 = (bf16[300,128]{1,0:T(8,128)(2,1)S(1)}, bf16[300,128]{1,0:T(8,128)(2,1)S(1)}, u32[]{:S(2)}, u32[]{:S(2)}) collective-permute-start(bf16[300,128]{1,0:T(8,128)(2,1)S(1)} %get-tuple-element.56), channel_id=1, source_target_pairs={{0,8},{4,12},{8,0},{12,4},{1,9},{5,13},{9,1},{13,5},{2,10},{6,14},... | collective-permute-start | bytes 230408 | tf_op jit(solution)/shard_map/ppermute | solution.py:339
  34.7 6.7 %collective-permute-start.9 = (bf16[300,128]{1,0:T(8,128)(2,1)S(1)}, bf16[300,128]{1,0:T(8,128)(2,1)S(1)}, u32[]{:S(2)}, u32[]{:S(2)}) collective-permute-start(bf16[300,128]{1,0:T(8,128)(2,1)S(1)} %get-tuple-element.50), channel_id=1, source_target_pairs={{0,8},{4,12},{8,0},{12,4},{1,9},{5,13},{9,1},{13,5},{2,10},{6,14},... | collective-permute-start | bytes 230408 | tf_op jit(solution)/shard_map/ppermute | solution.py:339
  36.3 5.1 %collective-permute-start.11 = (bf16[300,128]{1,0:T(8,128)(2,1)S(1)}, bf16[300,128]{1,0:T(8,128)(2,1)S(1)}, u32[]{:S(2)}, u32[]{:S(2)}) collective-permute-start(bf16[300,128]{1,0:T(8,128)(2,1)S(1)} %shard_map.78), channel_id=1, source_target_pairs={{0,1},{1,0},{2,3},{3,2},{4,5},{5,4},{6,7},{7,6},{8,9},{9,8},{10,11... | collective-permute-start | bytes 230408 | tf_op jit(solution)/shard_map/ppermute | solution.py:339
  38.0 6.7 %collective-permute-start.13 = (bf16[300,128]{1,0:T(8,128)(2,1)S(1)}, bf16[300,128]{1,0:T(8,128)(2,1)S(1)}, u32[]{:S(2)}, u32[]{:S(2)}) collective-permute-start(bf16[300,128]{1,0:T(8,128)(2,1)S(1)} %shard_map.79), channel_id=1, source_target_pairs={{0,3},{1,2},{2,1},{3,0},{4,7},{5,6},{6,5},{7,4},{8,11},{9,10},{10,... | collective-permute-start | bytes 230408 | tf_op jit(solution)/shard_map/ppermute | solution.py:339
  39.8 7.9 %collective-permute-start.15 = (bf16[300,128]{1,0:T(8,128)(2,1)S(1)}, bf16[300,128]{1,0:T(8,128)(2,1)S(1)}, u32[]{:S(2)}, u32[]{:S(2)}) collective-permute-start(bf16[300,128]{1,0:T(8,128)(2,1)S(1)} %shard_map.81), channel_id=1, source_target_pairs={{0,2},{1,3},{2,0},{3,1},{4,6},{5,7},{6,4},{7,5},{8,10},{9,11},{10,... | collective-permute-start | bytes 230408 | tf_op jit(solution)/shard_map/ppermute | solution.py:339
